TPU v7x, 32 devices: a whole 2x2x4 slice. The times are simulated.
32 devices in a mesh: vox: 16 (over z, y, x), tm: 2 (over core).
Axes of the slice: x: 2, y: 2, z: 4, core: 2. Of those that a mesh axis runs over, the one named last changes fastest.
Arguments:
- movie: bfloat16 [32768, 1024], P('vox', 'tm'), may hold values from -192 to 192
- footprints: bfloat16 [128, 32768], P(None, 'vox'), may hold values from 0 to 1
- traces: bfloat16 [128, 1024], P(None, 'tm'), may hold values from -3 to 3
- support: int32 [128, 256], P(None, 'vox'), may hold values 0 or 1
- block_order: int32 [8], replicated, may hold values from 0 to 7, each once
Outputs:
- new_footprints: bfloat16 [128, 32768], P(None, 'vox')
- new_traces: float32 [128, 1024], P(None, 'tm')
Inputs may be any that keep to these rules, and one draw needn't show every extreme that they name: block_order holds each block number exactly once.
All inputs are finite; a program needn't handle non-finite values. No bound on the sum of `support` on one device may be relied on, other than what follows from the above.
Results may differ from a plain program's by a relative error of at most 0.011.
Values may be sent and summed in bfloat16 or wider, within the bound.
No kernel may reach another device: no remote copies, remote signals or barrier semaphores. Data moves between devices by JAX's collectives and lax.ppermute only.
A program may use at most 64 MiB of HBM per device.

v0:
```python
import jax
import jax.numpy as jnp
from jax import lax
from jax.sharding import PartitionSpec as P

BLOCKC = 16
PLANES = 1
YR = 16
XC = 128
INNER = 3


smooth_weight = 256.0
ridge_weight = 2048.0


def padded_2(cells, sides, width):
    for axis, dim in sides:
        count = lax.axis_size(axis)
        ends = count - 1
        head = lax.slice_in_dim(cells, 0, width, axis=dim)
        tail = lax.slice_in_dim(cells, cells.shape[dim] - width, cells.shape[dim], axis=dim)
        cells = jnp.concatenate(
            [
                lax.ppermute(tail, axis, [(i, (i + 1) % count) for i in range(ends)]),
                cells,
                lax.ppermute(head, axis, [((i + 1) % count, i) for i in range(ends)]),
            ],
            axis=dim,
        )
    return cells


def laplace_local(extended):
    center = extended[:, 1:-1]
    beside = extended[:, 2:] + extended[:, :-2]
    padded = jnp.pad(center, ((0, 0), (0, 0), (1, 1), (1, 1)))
    beside = beside + padded[:, :, 2:, 1:-1] + padded[:, :, :-2, 1:-1]
    beside = beside + padded[:, :, 1:-1, 2:] + padded[:, :, 1:-1, :-2]
    return smooth_weight * (6.0 * center - beside)


def footprint_sweep(weights, correlation, smoothing, kept_mask, trace_gram, block_order):
    diagonal_f = jnp.diagonal(trace_gram) + 6.0 * smooth_weight

    def footprint_advance(position, current):
        start = block_order[position] * BLOCKC
        gram_rows = lax.dynamic_slice_in_dim(trace_gram, start, BLOCKC, 0)
        block_now = lax.dynamic_slice_in_dim(current, start, BLOCKC, 0)
        corr_rows = lax.dynamic_slice_in_dim(correlation, start, BLOCKC, 0)
        smooth_rows = lax.dynamic_slice_in_dim(smoothing, start, BLOCKC, 0)
        mask_rows = lax.dynamic_slice_in_dim(kept_mask, start, BLOCKC, 0)
        scale_rows = lax.dynamic_slice_in_dim(diagonal_f, start, BLOCKC, 0)
        product = jnp.dot(gram_rows, current, precision=lax.Precision.HIGHEST)
        updated = mask_rows * jnp.maximum(
            block_now + (corr_rows - product - smooth_rows) / scale_rows[:, None], 0.0
        )
        return lax.dynamic_update_slice_in_dim(current, updated, start, 0)

    for sweep_pass in range(INNER):
        weights = lax.fori_loop(0, block_order.shape[0], footprint_advance, weights)
    return weights


def trace_sweep(values, projection, cross, block_order):
    diagonal_c = jnp.diagonal(cross) + ridge_weight

    def trace_advance(position, current):
        start = block_order[position] * BLOCKC
        cross_rows = lax.dynamic_slice_in_dim(cross, start, BLOCKC, 0)
        block_now = lax.dynamic_slice_in_dim(current, start, BLOCKC, 0)
        proj_rows = lax.dynamic_slice_in_dim(projection, start, BLOCKC, 0)
        scale_rows = lax.dynamic_slice_in_dim(diagonal_c, start, BLOCKC, 0)
        product = jnp.dot(cross_rows, current, precision=lax.Precision.HIGHEST)
        updated = jnp.maximum(
            block_now + (proj_rows - product - ridge_weight * block_now) / scale_rows[:, None], 0.0
        )
        return lax.dynamic_update_slice_in_dim(current, updated, start, 0)

    for sweep_pass in range(INNER):
        values = lax.fori_loop(0, block_order.shape[0], trace_advance, values)
    return values


def local(movie, footprints, traces, support, block_order):
    comps, vox_local = footprints.shape
    row_count = support.shape[1]
    shaped = footprints.reshape(comps, PLANES, YR, XC)
    extended = padded_2(shaped, (("vox", 1),), 1)
    smoothing = laplace_local(extended.astype(jnp.float32)).reshape(comps, vox_local)
    kept_mask = jnp.broadcast_to(
        support.astype(jnp.float32)[:, :, None], (comps, row_count, XC)
    ).reshape(comps, vox_local)
    correlation = lax.dot_general(
        traces, movie, (((1,), (1,)), ((), ())), preferred_element_type=jnp.float32
    )
    trace_gram = lax.dot_general(
        traces, traces, (((1,), (1,)), ((), ())), preferred_element_type=jnp.float32
    )
    start_fp = footprints.astype(jnp.float32) * kept_mask
    correlation, trace_gram = lax.psum((correlation, trace_gram), "tm")
    new_footprints = footprint_sweep(
        start_fp, correlation, smoothing, kept_mask, trace_gram, block_order
    ).astype(jnp.bfloat16)
    projection = jnp.dot(new_footprints, movie, preferred_element_type=jnp.float32)
    cross = lax.dot_general(
        new_footprints, new_footprints, (((1,), (1,)), ((), ())), preferred_element_type=jnp.float32
    )
    start_tr = traces.astype(jnp.float32)
    projection, cross = lax.psum((projection, cross), "vox")
    new_traces = trace_sweep(start_tr, projection, cross, block_order)
    return (new_footprints, new_traces)


def solution(mesh):
    placed = (P("vox", "tm"), P(None, "vox"), P(None, "tm"), P(None, "vox"), P())
    return jax.shard_map(
        local,
        mesh=mesh,
        in_specs=placed,
        out_specs=(P(None, "vox"), P(None, "tm")),
        check_vma=False,
    )
```

profile of v0, /device:TPU:0, one launch (start us, length us, event | category | flops | bytes accessed | tf_op | source)
XLA Modules:
  0.0 295.9 jit_solution(4837519908755833080)
XLA Ops:
  7.2 2.1 copy.10
  9.3 5.7 %collective-permute-start = (bf16[128,1,16,128]{3,2,0,1:T(8,128)(2,1)}, bf16[128,1,16,128]{3,2,0,1:T(8,128)(2,1)}, u32[]{:S(2)}, u32[]{:S(2)}) collective-permute-start(bf16[128,1,16,128]{3,2,0,1:T(8,128)(2,1)} %bitcast.12), channel_id=1, source_target_pairs={{0,2},{2,4},{4,6},{6,8},{8,10},{10,12},{12,14},{14,16},{16,18},{18... | collective-permute-start | bytes 1572872 | tf_op jit(solution)/shard_map/ppermute | solution.py:25
  15.0 1.3 collective-permute-start.1
  16.3 1.8 fusion.46
  18.1 2.7 fusion.45
  21.3 1.5 convert_multiply_fusion
  22.8 14.1 %collective-permute-done = bf16[128,1,16,128]{3,2,0,1:T(8,128)(2,1)} collective-permute-done((bf16[128,1,16,128]{3,2,0,1:T(8,128)(2,1)}, bf16[128,1,16,128]{3,2,0,1:T(8,128)(2,1)}, u32[]{:S(2)}, u32[]{:S(2)}) %collective-permute-start) | collective-permute-done | bytes 524320 | tf_op jit(solution)/shard_map/ppermute | solution.py:25
  36.9 1.9 collective-permute-done.1
  38.8 1.7 maximum_convert_fusion
  41.2 2.2 copy_bitcast_fusion
  43.4 1.9 gather_fusion
  45.4 24.2 %while.78 = (s32[]{:T(128)}, f32[128,2048]{1,0:T(8,128)S(1)}, s32[8]{0:T(128)S(1)}, f32[128,2048]{1,0:T(8,128)}, f32[128,2048]{1,0:T(8,128)}, /*index=5*/f32[128...) while((s32[]{:T(128)}, f32[128,2048]{1,0:T(8,128)S(1)}, ...), condition=%wide.region_3.4_spmd, body=%wide.region_2.3_spmd.sunk | while | flops 50528260 | bytes 1976119 | solution.py:61
  46.7 1.7 fusion.83
  49.7 1.7 fusion.83
  52.7 1.7 fusion.83
  55.8 1.7 fusion.83
  58.8 1.7 fusion.83
  61.8 1.7 fusion.83
  64.9 1.7 fusion.83
  67.9 1.7 fusion.83
  69.6 24.2 %while.79 = (s32[]{:T(128)}, f32[128,2048]{1,0:T(8,128)S(1)}, s32[8]{0:T(128)S(1)}, f32[128,2048]{1,0:T(8,128)}, f32[128,2048]{1,0:T(8,128)}, /*index=5*/f32[128...) while((s32[]{:T(128)}, f32[128,2048]{1,0:T(8,128)S(1)}, ...), condition=%wide.region_5.6_spmd, body=%wide.region_4.5_spmd.sunk | while | flops 50528260 | bytes 1976119 | solution.py:61
  70.9 1.7 fusion.86
  74.0 1.7 fusion.86
  77.0 1.7 fusion.86
  80.0 1.7 fusion.86
  83.0 1.7 fusion.86
  86.1 1.7 fusion.86
  89.1 1.7 fusion.86
  92.1 1.7 fusion.86
  93.8 24.2 %while.80 = (s32[]{:T(128)}, f32[128,2048]{1,0:T(8,128)S(1)}, s32[8]{0:T(128)S(1)}, f32[128,2048]{1,0:T(8,128)}, f32[128,2048]{1,0:T(8,128)}, /*index=5*/f32[128...) while((s32[]{:T(128)}, f32[128,2048]{1,0:T(8,128)S(1)}, ...), condition=%wide.region_7.8_spmd, body=%wide.region_6.7_spmd.sunk | while | flops 50528260 | bytes 1976119 | solution.py:61
  95.2 1.7 fusion.89
  98.2 1.7 fusion.89
  101.2 1.7 fusion.89
  104.3 1.7 fusion.89
  107.3 1.7 fusion.89
  110.3 1.7 fusion.89
  113.3 1.7 fusion.89
  116.4 1.7 fusion.89
  118.2 1.2 fusion.47
  120.3 108.8 %all-reduce.6.cloned.1.call-done = (f32[128,512]{1,0:T(8,128)}, f32[128,128]{1,0:T(8,128)}) async-done(((f32[128,512]{1,0:T(8,128)}, f32[128,128]{1,0:T(8,128)}), (f32[128,512]{1,0:T(8,128)}, f32[128,128]{1,0:T(8,128)})) %all-reduce.6.cloned.1.call-update) | async-done | bytes 327696 | tf_op jit(solution)/shard_map/psum | solution.py:110
  229.1 1.9 gather_fusion.1
  231.1 19.1 %while.81 = (s32[]{:T(128)}, f32[128,512]{1,0:T(8,128)S(1)}, s32[8]{0:T(128)S(1)}, f32[128,512]{1,0:T(8,128)}, f32[128,128]{1,0:T(8,128)}, /*index=5*/f32[128]{0...) while((s32[]{:T(128)}, f32[128,512]{1,0:T(8,128)S(1)}, s32[8]{0:T(128)S(1)}, f32[128,512]{1,0:T(8,128)}, ...), condition=%wide.region_11.12_spmd, body=%wide.region_10.11_spmd.sunk | while | flops 12632070 | bytes 436007 | solution.py:81
  232.4 1.0 fusion.92
  234.8 1.0 fusion.92
  237.2 1.0 fusion.92
  239.5 1.0 fusion.92
  250.1 19.1 %while.82 = (s32[]{:T(128)}, f32[128,512]{1,0:T(8,128)S(1)}, s32[8]{0:T(128)S(1)}, f32[128,512]{1,0:T(8,128)}, f32[128,128]{1,0:T(8,128)}, /*index=5*/f32[128]{0...) while((s32[]{:T(128)}, f32[128,512]{1,0:T(8,128)S(1)}, s32[8]{0:T(128)S(1)}, f32[128,512]{1,0:T(8,128)}, ...), condition=%wide.region_13.14_spmd, body=%wide.region_12.13_spmd.sunk | while | flops 12632070 | bytes 436007 | solution.py:81
  269.2 19.1 %while.83 = (s32[]{:T(128)}, f32[128,512]{1,0:T(8,128)S(1)}, s32[8]{0:T(128)S(1)}, f32[128,512]{1,0:T(8,128)}, f32[128,128]{1,0:T(8,128)}, /*index=5*/f32[128]{0...) while((s32[]{:T(128)}, f32[128,512]{1,0:T(8,128)S(1)}, s32[8]{0:T(128)S(1)}, f32[128,512]{1,0:T(8,128)}, ...), condition=%wide.region_15.16_spmd, body=%wide.region_14.15_spmd.sunk | while | flops 12632070 | bytes 436007 | solution.py:81
  (192 shorter events, 56.0 us)
Async XLA Ops:
  7.2 10.9 %copy-start = (bf16[2048,512]{1,0:T(8,128)(2,1)S(1)}, bf16[2048,512]{1,0:T(8,128)(2,1)}, u32[]{:S(2)}) copy-start(bf16[2048,512]{1,0:T(8,128)(2,1)} %param.17) | copy-start | bytes 6291460
  7.2 36.2 %all-reduce.8.cloned.1.call-start = ((), (), s32[]{:S(2)}) async-start(), calls=%async_computation.1 | async-start | bytes 2228224 | tf_op jit(solution)/shard_map/psum | solution.py:101
  9.3 27.6 %collective-permute-start = (bf16[128,1,16,128]{3,2,0,1:T(8,128)(2,1)}, bf16[128,1,16,128]{3,2,0,1:T(8,128)(2,1)}, u32[]{:S(2)}, u32[]{:S(2)}) collective-permute-start(bf16[128,1,16,128]{3,2,0,1:T(8,128)(2,1)} %bitcast.12), channel_id=1, source_target_pairs={{0,2},{2,4},{4,6},{6,8},{8,10},{10,12},{12,14},{14,16},{16,18},{18... | collective-permute-start | bytes 1572872 | tf_op jit(solution)/shard_map/ppermute | solution.py:25
  15.0 23.8 %collective-permute-start.1 = (bf16[128,1,16,128]{3,2,0,1:T(8,128)(2,1)}, bf16[128,1,16,128]{3,2,0,1:T(8,128)(2,1)}, u32[]{:S(2)}, u32[]{:S(2)}) collective-permute-start(bf16[128,1,16,128]{3,2,0,1:T(8,128)(2,1)} %bitcast.12), channel_id=1, source_target_pairs={{2,0},{4,2},{6,4},{8,6},{10,8},{12,10},{14,12},{16,14},{18,16},{20... | collective-permute-start | bytes 1572872 | tf_op jit(solution)/shard_map/ppermute | solution.py:27
  18.1 2.8 copy-start.4
  20.8 208.3 %all-reduce.6.cloned.1.call-start = ((), (), s32[]{:S(2)}) async-start(), calls=%async_computation | async-start | bytes 655360 | tf_op jit(solution)/shard_map/psum | solution.py:110
  41.2 4.1 %copy-start.5 = (s32[8]{0:T(128)S(1)}, s32[8]{0:T(128)}, u32[]{:S(2)}) copy-start(s32[8]{0:T(128)} %param.21) | copy-start | bytes 100
  118.1 1.2 copy-start.2
  118.2 2.1 copy-start.3
  288.3 0.7 copy-start.1
Sparse Core Ops, SparseCore 0:
  20.9 22.1 all-reduce.7
  120.4 108.6 all-reduce.5
where the time goes:
time: 299 us; the launch traced here: 296 us
  waiting for transfers between devices  125 us (42%)
  matrix products  71 us (24%)
  local copies, waits for them, and re-layouts  41.9 us (14%)
  loops' own time  33 us (11%)
  between operations  14.2 us (5%)
  starting transfers between devices  7.03 us (2%)
  other arithmetic  3.91 us (1%)
    psum x1, waiting for transfers between devices, local(): projection, cross = lax.psum((projection, cross), 'vox')  109 us
    dot_general x24, matrix products, footprint_advance(): product = jnp.dot(gram_rows, current, precision=lax.Precision.HIGHEST)  39.8 us
    dot_general x24, matrix products, trace_advance(): product = jnp.dot(cross_rows, current, precision=lax.Precision.HIGHEST)  24.5 us
    another operation x3, loops' own time, footprint_sweep(): weights = lax.fori_loop(0, block_order.shape[0], footprint_advance, weights)  16.5 us
    another operation x3, loops' own time, trace_sweep(): values = lax.fori_loop(0, block_order.shape[0], trace_advance, values)  16.5 us
    dynamic_slice x24, local copies, waits for them, and re-layouts, footprint_advance(): start = block_order[position] * BLOCKC  14.1 us
    dynamic_slice x24, local copies, waits for them, and re-layouts, trace_advance(): start = block_order[position] * BLOCKC  14.1 us
    ppermute x1, waiting for transfers between devices, padded_2(): lax.ppermute(tail, axis, [(i, (i + 1) % count) for i in range(ends)])  14.1 us
  transfers between devices with their start and end apart: 4, of which 3 were waited for; matrix products, arithmetic and copies ran while one was open for 4% of the time, Pallas kernels for 0%

commit v1 on v0

v1 whole, which is shorter than its diff:
```python
import functools

import jax
import jax.numpy as jnp
from jax import lax
from jax.experimental import pallas as pl
from jax.experimental.pallas import tpu as pltpu
from jax.sharding import PartitionSpec as P

BLOCKC = 16
XC = 128
INNER = 3

smooth_weight = 256.0
ridge_weight = 2048.0

F32 = jnp.float32
BF16 = jnp.bfloat16
VMEM = pl.BlockSpec(memory_space=pltpu.VMEM)
SMEM = pl.BlockSpec(memory_space=pltpu.SMEM)


def split_rows(system, gs_ref):
    comps = system.shape[0]
    high = system.astype(BF16)
    low = (system - high.astype(F32)).astype(BF16)
    for start in range(0, comps, BLOCKC):
        rows = slice(start, start + BLOCKC)
        for side in range(2):
            lanes = slice(side * comps, (side + 1) * comps)
            gs_ref[2 * start : 2 * start + BLOCKC, lanes] = high[rows]
            gs_ref[2 * start + BLOCKC : 2 * start + 2 * BLOCKC, lanes] = low[rows]


def diagonal_of(gram):
    row = lax.broadcasted_iota(jnp.int32, gram.shape, 0)
    col = lax.broadcasted_iota(jnp.int32, gram.shape, 1)
    eye = row == col
    return eye, jnp.sum(jnp.where(eye, gram, 0.0), axis=1, keepdims=True)


def sweep_steps(order_ref, gs_ref, target_ref, stacked_ref, keep_ref=None, out_ref=None):
    comps = target_ref.shape[0]
    blocks = comps // BLOCKC
    for step in range(INNER * blocks):
        block = order_ref[step % blocks]
        rows = pl.ds(pl.multiple_of(block * BLOCKC, BLOCKC), BLOCKC)
        low_rows = pl.ds(pl.multiple_of(comps + block * BLOCKC, BLOCKC), BLOCKC)
        pair = pl.ds(pl.multiple_of(block * 2 * BLOCKC, 2 * BLOCKC), 2 * BLOCKC)
        product = jnp.dot(gs_ref[pair, :], stacked_ref[...], preferred_element_type=F32)
        updated = jnp.maximum(target_ref[rows, :] + (product[:BLOCKC] + product[BLOCKC:]), 0.0)
        if keep_ref is not None:
            updated = updated * keep_ref[rows, :]
        high = updated.astype(BF16)
        stacked_ref[rows, :] = high
        stacked_ref[low_rows, :] = (updated - high.astype(F32)).astype(BF16)
        if out_ref is not None:
            out_ref[rows, :] = updated


def prepare_kernel(corr_ref, gram_ref, fp_ref, support_ref, target_ref, keep_ref, gs_ref, scale_ref):
    comps, share = corr_ref.shape
    me = lax.axis_index("tm")
    count = fp_ref.shape[1] // share
    first = me * share
    gram = gram_ref[...]
    eye, diagonal = diagonal_of(gram)
    inverse = 1.0 / (diagonal + 6.0 * smooth_weight)
    split_rows(jnp.where(eye, 6.0 * smooth_weight * inverse, -gram * inverse), gs_ref)
    scale_ref[...] = jnp.broadcast_to(smooth_weight * inverse, scale_ref.shape)

    lane = lax.broadcasted_iota(jnp.int32, (comps, XC), 1)
    column = lax.broadcasted_iota(jnp.int32, support_ref.shape, 1)
    support = support_ref[...].astype(F32)

    def row_at(offset):
        at = pl.multiple_of(first + offset, XC)
        return fp_ref[:, pl.ds(at, XC)].astype(F32)

    below = pl.multiple_of(jnp.maximum(first - XC, 0), XC)
    above = pl.multiple_of(jnp.minimum(first + share, fp_ref.shape[1] - XC), XC)
    before = fp_ref[:, pl.ds(below, XC)].astype(F32) * jnp.where(me > 0, 1.0, 0.0)
    center = row_at(0)
    for offset in range(0, share, XC):
        if offset + XC < share:
            after = row_at(offset + XC)
        else:
            after = fp_ref[:, pl.ds(above, XC)].astype(F32) * jnp.where(me < count - 1, 1.0, 0.0)
        left = jnp.where(lane == 0, 0.0, pltpu.roll(center, 1, 1))
        right = jnp.where(lane == XC - 1, 0.0, pltpu.roll(center, XC - 1, 1))
        beside = before + after + left + right
        smoothing = smooth_weight * (6.0 * center - beside)
        lanes = slice(offset, offset + XC)
        target_ref[:, lanes] = (corr_ref[:, lanes] - smoothing) * inverse
        here = me * (share // XC) + offset // XC
        kept = jnp.sum(jnp.where(column == here, support, 0.0), axis=1, keepdims=True)
        keep_ref[:, lanes] = jnp.broadcast_to(kept, (comps, XC))
        before, center = center, after


def footprint_kernel(order_ref, target_ref, keep_ref, gs_ref, scale_ref, fp_ref, head_ref, tail_ref, out_ref, goal_ref, stacked_ref):
    comps, share = target_ref.shape
    me = lax.axis_index("tm")
    for offset in range(0, share, XC):
        lanes = slice(offset, offset + XC)
        sides = head_ref[:, lanes].astype(F32) + tail_ref[:, lanes].astype(F32)
        goal_ref[:, lanes] = target_ref[:, lanes] + sides * scale_ref[...]
        at = pl.multiple_of(me * share + offset, XC)
        center = fp_ref[:, pl.ds(at, XC)].astype(F32)
        stacked_ref[:comps, lanes] = (center * keep_ref[:, lanes]).astype(BF16)
    stacked_ref[comps:, :] = jnp.zeros((comps, share), BF16)
    sweep_steps(order_ref, gs_ref, goal_ref, stacked_ref, keep_ref)
    out_ref[...] = stacked_ref[:comps, :]


def product_kernel(pieces, frames, *refs):
    piece_refs, movie_ref, joined_ref, full_ref = refs[:pieces], refs[pieces], refs[pieces + 1], refs[pieces + 2]
    me = lax.axis_index("tm")
    projection = cross = None
    for index, ref in enumerate(piece_refs):
        width = ref.shape[1]
        place = pl.multiple_of((me if index == 0 else 1 - me) * width, width) if pieces > 1 else 0
        piece = ref[...]
        full_ref[:, pl.ds(place, width)] = piece
        part = jnp.dot(piece, movie_ref[pl.ds(place, width), :], preferred_element_type=F32)
        own = lax.dot_general(piece, piece, (((1,), (1,)), ((), ())), preferred_element_type=F32)
        projection = part if projection is None else projection + part
        cross = own if cross is None else cross + own
    joined_ref[:, :frames] = projection
    joined_ref[:, frames:] = cross


def trace_kernel(order_ref, joined_ref, traces_ref, out_ref, goal_ref, gs_ref, stacked_ref):
    comps, frames = traces_ref.shape
    cross = joined_ref[:, frames:]
    eye, diagonal = diagonal_of(cross)
    inverse = 1.0 / (diagonal + ridge_weight)
    split_rows(jnp.where(eye, 0.0, -cross * inverse), gs_ref)
    goal_ref[...] = joined_ref[:, :frames] * inverse
    stacked_ref[:comps, :] = traces_ref[...]
    stacked_ref[comps:, :] = jnp.zeros((comps, frames), BF16)
    sweep_steps(order_ref, gs_ref, goal_ref, stacked_ref, None, out_ref)


def shape_of(dims, dtype):
    return jax.ShapeDtypeStruct(dims, dtype)


def swap(array):
    return lax.ppermute(array, "tm", [(0, 1), (1, 0)])


def sum_over_vox(joined):
    count = lax.axis_size("vox")
    comps, width = joined.shape
    if comps % count:
        return lax.psum(joined, "vox")
    parts = lax.all_to_all(joined, "vox", 0, 0, tiled=True)
    mine = jnp.sum(parts.reshape(count, comps // count, width), axis=0)
    spread = jnp.broadcast_to(mine[None], (count, comps // count, width)).reshape(comps, width)
    return lax.all_to_all(spread, "vox", 0, 0, tiled=True)


def local(movie, footprints, traces, support, block_order):
    comps, vox_local = footprints.shape
    frames = traces.shape[1]
    cores = lax.axis_size("tm")
    planes = lax.axis_size("vox")
    share = vox_local // cores
    me = lax.axis_index("tm")

    own = lax.dynamic_slice_in_dim(footprints, me * share, share, 1)
    head = lax.ppermute(own, "vox", [(i, i + 1) for i in range(planes - 1)])
    tail = lax.ppermute(own, "vox", [(i + 1, i) for i in range(planes - 1)])

    correlation = lax.dot_general(traces, movie, (((1,), (1,)), ((), ())), preferred_element_type=F32)
    gram = lax.dot_general(traces, traces, (((1,), (1,)), ((), ())), preferred_element_type=F32)
    if cores == 2:
        theirs = lax.dynamic_slice_in_dim(correlation, (1 - me) * share, share, 1)
        ours = lax.dynamic_slice_in_dim(correlation, me * share, share, 1)
        correlation = ours + swap(theirs)
        gram = gram + swap(gram)
    else:
        correlation = lax.psum_scatter(correlation, "tm", scatter_dimension=1, tiled=True)
        gram = lax.psum(gram, "tm")

    target, keep, system, scale = pl.pallas_call(
        prepare_kernel,
        out_shape=[
            shape_of((comps, share), F32),
            shape_of((comps, share), F32),
            shape_of((2 * comps, 2 * comps), BF16),
            shape_of((comps, XC), F32),
        ],
        in_specs=[VMEM] * 4,
        out_specs=[VMEM] * 4,
        cost_estimate=pl.CostEstimate(flops=20 * comps * share, bytes_accessed=16 * comps * share, transcendentals=0),
    )(correlation, gram, footprints, support)

    half = pl.pallas_call(
        footprint_kernel,
        out_shape=shape_of((comps, share), BF16),
        in_specs=[SMEM] + [VMEM] * 7,
        out_specs=VMEM,
        scratch_shapes=[pltpu.VMEM((comps, share), F32), pltpu.VMEM((2 * comps, share), BF16)],
    )(block_order, target, keep, system, scale, footprints, head, tail)

    if cores == 2:
        pieces = [half, swap(half)]
    else:
        pieces = [lax.all_gather(half, "tm", axis=1, tiled=True)]
    joined, new_footprints = pl.pallas_call(
        functools.partial(product_kernel, len(pieces), frames),
        out_shape=[shape_of((comps, frames + comps), F32), shape_of((comps, vox_local), BF16)],
        in_specs=[VMEM] * (len(pieces) + 1),
        out_specs=[VMEM] * 2,
    )(*pieces, movie)

    joined = sum_over_vox(joined)
    new_traces = pl.pallas_call(
        trace_kernel,
        out_shape=shape_of((comps, frames), F32),
        in_specs=[SMEM] + [VMEM] * 2,
        out_specs=VMEM,
        scratch_shapes=[
            pltpu.VMEM((comps, frames), F32),
            pltpu.VMEM((2 * comps, 2 * comps), BF16),
            pltpu.VMEM((2 * comps, frames), BF16),
        ],
    )(block_order, joined, traces)
    return (new_footprints, new_traces)


def solution(mesh):
    placed = (P("vox", "tm"), P(None, "vox"), P(None, "tm"), P(None, "vox"), P())
    return jax.shard_map(
        local,
        mesh=mesh,
        in_specs=placed,
        out_specs=(P(None, "vox"), P(None, "tm")),
        check_vma=False,
    )
```

time: 299 us -> 73.9 us (0.25)
  waiting for transfers between devices: 125 us -> 8.71 us
  matrix products: 71 us -> 2.71 us
  local copies, waits for them, and re-layouts: 41.9 us -> 2.25 us
  loops' own time: 33 us -> 0 us
  blocking collectives: 0 us -> 31.8 us
  Pallas kernels: 0 us -> 19 us
  between operations: 14.2 us -> 0.73 us
    psum x2 -> x0, waiting for transfers between devices: 109 us -> none  [the longest x1 109 us: local(): projection, cross = lax.psum((projection, cross), 'vox')]
    dot_general x50 -> x0, matrix products: 66.5 us -> none  [the longest x24 39.8 us: footprint_advance(): product = jnp.dot(gram_rows, current, precision=lax.Precision.HIGHEST)]
    another operation x6 -> x0, loops' own time: 33 us -> none  [the longest x3 16.5 us: footprint_sweep(): weights = lax.fori_loop(0, block_order.shape[0], footprint_advance, weights)]
    dynamic_slice x96 -> x2, local copies, waits for them, and re-layouts: 31.9 us -> 0.07 us  [the longest x1 0.05 us: local(): theirs = lax.dynamic_slice_in_dim(correlation, (1 - me) * share, share, 1)]
    all_to_all x0 -> x2, blocking collectives: none -> 31.8 us  [the longest x1 17.5 us: sum_over_vox(): parts = lax.all_to_all(joined, 'vox', 0, 0, tiled=True)]
    pallas_call x0 -> x4, Pallas kernels: none -> 19 us  [the longest x1 7.45 us: local(): pl.pallas_call(footprint_kernel, out_shape=shape_of((comps, share), BF16)...]
    ppermute x2 -> x5, waiting for transfers between devices: 16 us -> 8.71 us  [the longest x1 5.04 us: local(): head = lax.ppermute(own, 'vox', [(i, i + 1) for i in range(planes - 1)])]
    gather x2 -> x0, local copies, waits for them, and re-layouts: 3.88 us -> none  [the longest x1 1.94 us: footprint_sweep(): diagonal_f = jnp.diagonal(trace_gram) + 6.0 * smooth_weight]
  transfers between devices with their start and end apart: 4 -> 5, of which waited for: 3 -> 3; matrix products, arithmetic and copies ran while one was open for 4% -> 3% of each run, Pallas kernels for 0% -> 4%
where the time goes in v1:
time: 73.9 us; the launch traced here: 73.5 us
  blocking collectives  31.8 us (43%)
  Pallas kernels  19 us (26%)
  waiting for transfers between devices  8.71 us (12%)
  starting transfers between devices  6.79 us (9%)
  matrix products  2.71 us (4%)
  local copies, waits for them, and re-layouts  2.25 us (3%)
  other arithmetic  1.52 us (2%)
    all_to_all x1, blocking collectives, sum_over_vox(): parts = lax.all_to_all(joined, 'vox', 0, 0, tiled=True)  17.5 us
    all_to_all x1, blocking collectives, sum_over_vox(): return lax.all_to_all(spread, 'vox', 0, 0, tiled=True)  14.2 us
    pallas_call x1, Pallas kernels, local(): pl.pallas_call(footprint_kernel, out_shape=shape_of((comps, share), BF16)...  7.45 us
    pallas_call x1, Pallas kernels, local(): pl.pallas_call(trace_kernel, out_shape=shape_of((comps, frames), F32), in...  5.71 us
    ppermute x1, waiting for transfers between devices, local(): head = lax.ppermute(own, 'vox', [(i, i + 1) for i in range(planes - 1)])  5.04 us
    ppermute x1, starting transfers between devices, local(): head = lax.ppermute(own, 'vox', [(i, i + 1) for i in range(planes - 1)])  4.85 us
    pallas_call x1, Pallas kernels, local(): pl.pallas_call(functools.partial(product_kernel, len(pieces), frames), ou...  3.08 us
    pallas_call x1, Pallas kernels, local(): pl.pallas_call(prepare_kernel, out_shape=[shape_of((comps, share), F32),...  2.79 us
  transfers between devices with their start and end apart: 5, of which 3 were waited for; matrix products, arithmetic and copies ran while one was open for 3% of the time, Pallas kernels for 4%

profile of v1, /device:TPU:0, one launch (start us, length us, event | category | flops | bytes accessed | tf_op | source)
XLA Modules:
  0.0 73.5 jit_solution(961712460868517633)
XLA Ops:
  0.6 0.0 copy-start.1
  0.6 0.0 copy-start
  0.7 0.0 copy-start.5
  0.7 2.5 %fusion = f32[128,2048]{1,0:T(8,128)S(1)} fusion(bf16[128,512]{1,0:T(8,128)(2,1)} %traces_ref.1, bf16[2048,512]{1,0:T(8,128)(2,1)} %refs_2_.1), kind=kOutput, calls=%fused_computation.3 | convolution fusion | flops 268435456 | bytes 3276800 | tf_op jit(solution)/shard_map/dot_general | solution.py:176
  3.3 0.5 collective-permute-start
  3.8 0.0 copy-done.1
  3.8 0.2 fusion.1
  4.0 0.1 collective-permute-start.1
  4.1 0.0 copy-done
  4.1 4.9 %collective-permute-start.2 = (bf16[128,1024]{1,0:T(8,128)(2,1)S(1)}, bf16[128,1024]{1,0:T(8,128)(2,1)S(1)}, u32[]{:S(2)}, u32[]{:S(2)}) collective-permute-start(bf16[128,1024]{1,0:T(8,128)(2,1)S(1)} %constant_dynamic-slice_fusion), channel_id=1, source_target_pairs={{0,2},{2,4},{4,6},{6,8},{8,10},{10,12},{12,14},{14,16},{16,18},{18... | collective-permute-start | bytes 786440 | tf_op jit(solution)/shard_map/ppermute | solution.py:173
  9.0 1.3 %collective-permute-start.3 = (bf16[128,1024]{1,0:T(8,128)(2,1)S(1)}, bf16[128,1024]{1,0:T(8,128)(2,1)S(1)}, u32[]{:S(2)}, u32[]{:S(2)}) collective-permute-start(bf16[128,1024]{1,0:T(8,128)(2,1)S(1)} %constant_dynamic-slice_fusion), channel_id=1, source_target_pairs={{2,0},{4,2},{6,4},{8,6},{10,8},{12,10},{14,12},{16,14},{18,16},{20... | collective-permute-start | bytes 786440 | tf_op jit(solution)/shard_map/ppermute | solution.py:174
  10.3 0.0 copy-done.5
  10.3 0.7 copy.7.support_ref
  11.0 0.0 collective-permute-done.1
  11.0 0.6 add.16.gram_ref
  11.7 0.0 collective-permute-done
  11.7 0.9 %dynamic-slice_add_fusion.corr_ref = f32[128,1024]{1,0:T(8,128)} fusion(f32[128,1024]{1,0:T(8,128)S(1)} %collective-permute-done, f32[128,2048]{1,0:T(8,128)S(1)} %fusion, s32[]{:T(128)S(6)} %select_n.7), kind=kLoop, calls=%fused_computation | loop fusion | flops 131072 | bytes 1572868 | tf_op jit(solution)/shard_map/add | solution.py:181
  12.5 2.8 %shard_map.68 = (f32[128,1024]{1,0:T(8,128)}, f32[128,1024]{1,0:T(8,128)}, bf16[256,256]{1,0:T(8,128)(2,1)}, f32[128,128]{1,0:T(8,128)}) custom-call(f32[128,1024]{1,0:T(8,128)} %dynamic-slice_add_fusion.corr_ref, f32[128,128]{1,0:T(8,128)} %add.16.gram_ref, bf16[128,2048]{1,0:T(8,128)(2,1)} %fp_ref.3, s32[128,16]{1,0:T(8,128)} %copy.7.support_ref), custom_call_target="tpu_custom_call" | custom-call | flops 2621440 | bytes 2097152 | tf_op jit(solution)/shard_map/pallas_call | solution.py:187
  15.3 5.0 %collective-permute-done.2.head_ref = bf16[128,1024]{1,0:T(8,128)(2,1)S(1)} collective-permute-done((bf16[128,1024]{1,0:T(8,128)(2,1)S(1)}, bf16[128,1024]{1,0:T(8,128)(2,1)S(1)}, u32[]{:S(2)}, u32[]{:S(2)}) %collective-permute-start.2) | collective-permute-done | bytes 262176 | tf_op jit(solution)/shard_map/ppermute | solution.py:173
  20.4 0.0 copy-start.3
  20.4 1.9 %collective-permute-done.3.tail_ref = bf16[128,1024]{1,0:T(8,128)(2,1)S(1)} collective-permute-done((bf16[128,1024]{1,0:T(8,128)(2,1)S(1)}, bf16[128,1024]{1,0:T(8,128)(2,1)S(1)}, u32[]{:S(2)}, u32[]{:S(2)}) %collective-permute-start.3) | collective-permute-done | bytes 262176 | tf_op jit(solution)/shard_map/ppermute | solution.py:174
  22.3 0.0 copy-start.4
  22.3 0.0 copy-done.3
  22.3 0.7 copy-done.4
  23.0 7.5 %shard_map.69.refs_0_ = bf16[128,1024]{1,0:T(8,128)(2,1)} custom-call(s32[8]{0:T(128)} %order_ref.3, f32[128,1024]{1,0:T(8,128)} %get-tuple-element.8.target_ref, f32[128,1024]{1,0:T(8,128)} %get-tuple-element.9.keep_ref, bf16[256,256]{1,0:T(8,128)(2,1)} %get-tuple-element.10.gs_ref, f32[128,128]{1,0:T(8,128)} %get-tuple-element.11.scale_ref, ...), custom_call_target="tpu_custom_call" | custom-call | tf_op jit(solution)/shard_map/pallas_call | solution.py:200
  30.4 0.0 collective-permute-start.4
  30.4 1.7 %collective-permute-done.4.refs_1_ = bf16[128,1024]{1,0:T(8,128)(2,1)S(1)} collective-permute-done((bf16[128,1024]{1,0:T(8,128)(2,1)}, bf16[128,1024]{1,0:T(8,128)(2,1)S(1)}, u32[]{:S(2)}, u32[]{:S(2)}) %collective-permute-start.4) | collective-permute-done | bytes 262176 | tf_op jit(solution)/shard_map/ppermute | solution.py:150
  32.2 0.0 copy-start.2
  32.2 0.7 copy-done.2
  32.9 3.1 %shard_map.70 = (f32[128,640]{1,0:T(8,128)}, bf16[128,2048]{1,0:T(8,128)(2,1)}) custom-call(bf16[128,1024]{1,0:T(8,128)(2,1)} %shard_map.69.refs_0_, bf16[128,1024]{1,0:T(8,128)(2,1)} %copy-done.2, bf16[2048,512]{1,0:T(8,128)(2,1)} %refs_2_.1), custom_call_target="tpu_custom_call" | custom-call | tf_op jit(solution)/shard_map/pallas_call | solution.py:212
  36.0 17.5 %all_to_all.17 = f32[16,8,640]{2,1,0:T(8,128)S(1)} all-to-all(f32[16,8,640]{2,1,0:T(8,128)} %bitcast.7), channel_id=1, replica_groups=mesh['vox'=16,'tm'=2] {'vox'}, dimensions={0} | all-to-all | bytes 655360 | tf_op jit(solution)/shard_map/all_to_all | solution.py:158
  53.6 14.2 %all_to_all.18 = f32[16,8,640]{2,1,0:T(8,128)} all-to-all(f32[16,8,640]{2,1,0:T(8,128)S(1)} %broadcast_in_dim.2), channel_id=1, replica_groups=mesh['vox'=16,'tm'=2] {'vox'}, dimensions={0} | all-to-all | bytes 655360 | tf_op jit(solution)/shard_map/all_to_all | solution.py:161
  67.8 5.7 %shard_map.71 = f32[128,512]{1,0:T(8,128)} custom-call(s32[8]{0:T(128)} %order_ref.3, f32[128,640]{1,0:T(8,128)} %bitcast.6, bf16[128,512]{1,0:T(8,128)(2,1)} %traces_ref.1), custom_call_target="tpu_custom_call" | custom-call | tf_op jit(solution)/shard_map/pallas_call | solution.py:220
  (4 shorter events, 0.1 us)
Async XLA Ops:
  0.6 3.1 %copy-start.1 = (bf16[128,512]{1,0:T(8,128)(2,1)S(1)}, bf16[128,512]{1,0:T(8,128)(2,1)}, u32[]{:S(2)}) copy-start(bf16[128,512]{1,0:T(8,128)(2,1)} %traces_ref.1) | copy-start | bytes 393220
  0.6 3.5 %copy-start = (bf16[128,2048]{1,0:T(8,128)(2,1)S(1)}, bf16[128,2048]{1,0:T(8,128)(2,1)}, u32[]{:S(2)}) copy-start(bf16[128,2048]{1,0:T(8,128)(2,1)} %fp_ref.3) | copy-start | bytes 1572868
  0.7 9.6 %copy-start.5 = (s32[128,16]{0,1:T(8,128)S(1)}, s32[128,16]{0,1:T(8,128)}, u32[]{:S(2)}) copy-start(s32[128,16]{0,1:T(8,128)} %param.8) | copy-start | bytes 24580
  3.3 8.4 %collective-permute-start = (f32[128,1024]{1,0:T(8,128)S(1)}, f32[128,1024]{1,0:T(8,128)S(1)}, u32[]{:S(2)}, u32[]{:S(2)}) collective-permute-start(f32[128,1024]{1,0:T(8,128)S(1)} %constant_dynamic-slice_fusion.1), channel_id=1, source_target_pairs={{0,1},{1,0},{2,3},{3,2},{4,5},{5,4},{6,7},{7,6},{8,9},{9,8},{10,11... | collective-permute-start | bytes 1572872 | tf_op jit(solution)/shard_map/ppermute | solution.py:150
  4.0 7.1 %collective-permute-start.1 = (f32[128,128]{1,0:T(8,128)S(1)}, f32[128,128]{1,0:T(8,128)S(1)}, u32[]{:S(2)}, u32[]{:S(2)}) collective-permute-start(f32[128,128]{1,0:T(8,128)S(1)} %fusion.1), channel_id=1, source_target_pairs={{0,1},{1,0},{2,3},{3,2},{4,5},{5,4},{6,7},{7,6},{8,9},{9,8},{10,11... | collective-permute-start | bytes 196616 | tf_op jit(solution)/shard_map/ppermute | solution.py:150
  4.1 16.2 %collective-permute-start.2 = (bf16[128,1024]{1,0:T(8,128)(2,1)S(1)}, bf16[128,1024]{1,0:T(8,128)(2,1)S(1)}, u32[]{:S(2)}, u32[]{:S(2)}) collective-permute-start(bf16[128,1024]{1,0:T(8,128)(2,1)S(1)} %constant_dynamic-slice_fusion), channel_id=1, source_target_pairs={{0,2},{2,4},{4,6},{6,8},{8,10},{10,12},{12,14},{14,16},{16,18},{18... | collective-permute-start | bytes 786440 | tf_op jit(solution)/shard_map/ppermute | solution.py:173
  9.0 13.3 %collective-permute-start.3 = (bf16[128,1024]{1,0:T(8,128)(2,1)S(1)}, bf16[128,1024]{1,0:T(8,128)(2,1)S(1)}, u32[]{:S(2)}, u32[]{:S(2)}) collective-permute-start(bf16[128,1024]{1,0:T(8,128)(2,1)S(1)} %constant_dynamic-slice_fusion), channel_id=1, source_target_pairs={{2,0},{4,2},{6,4},{8,6},{10,8},{12,10},{14,12},{16,14},{18,16},{20... | collective-permute-start | bytes 786440 | tf_op jit(solution)/shard_map/ppermute | solution.py:174
  20.4 1.9 %copy-start.3 = (bf16[128,1024]{1,0:T(8,128)(2,1)}, bf16[128,1024]{1,0:T(8,128)(2,1)S(1)}, u32[]{:S(2)}) copy-start(bf16[128,1024]{1,0:T(8,128)(2,1)S(1)} %collective-permute-done.2.head_ref) | copy-start | bytes 786436
  22.3 0.7 copy-start.4
  30.4 1.7 %collective-permute-start.4 = (bf16[128,1024]{1,0:T(8,128)(2,1)}, bf16[128,1024]{1,0:T(8,128)(2,1)S(1)}, u32[]{:S(2)}, u32[]{:S(2)}) collective-permute-start(bf16[128,1024]{1,0:T(8,128)(2,1)} %shard_map.69.refs_0_), channel_id=1, source_target_pairs={{0,1},{1,0},{2,3},{3,2},{4,5},{5,4},{6,7},{7,6},{8,9},{9,8},{10,11... | collective-permute-start | bytes 786440 | tf_op jit(solution)/shard_map/ppermute | solution.py:150
  32.2 0.7 copy-start.2

commit v2 on v1

v2 whole, which is shorter than its diff:
```python
import functools

import jax
import jax.numpy as jnp
from jax import lax
from jax.experimental import pallas as pl
from jax.experimental.pallas import tpu as pltpu
from jax.sharding import PartitionSpec as P

BLOCKC = 16
XC = 128
INNER = 3
GROUP = 4

smooth_weight = 256.0
ridge_weight = 2048.0

F32 = jnp.float32
BF16 = jnp.bfloat16
VMEM = pl.BlockSpec(memory_space=pltpu.VMEM)
SMEM = pl.BlockSpec(memory_space=pltpu.SMEM)
ANY = pl.BlockSpec(memory_space=pl.ANY)
SMALL = pltpu.CompilerParams(vmem_limit_bytes=12 * 1024 * 1024)
BY_LAST = (((1,), (1,)), ((), ()))


def shape_of(dims, dtype):
    return jax.ShapeDtypeStruct(dims, dtype)


def split_rows(system, gs_ref):
    comps = system.shape[0]
    high = system.astype(BF16)
    low = (system - high.astype(F32)).astype(BF16)
    for start in range(0, comps, BLOCKC):
        rows = slice(start, start + BLOCKC)
        for side in range(2):
            lanes = slice(side * comps, (side + 1) * comps)
            gs_ref[2 * start : 2 * start + BLOCKC, lanes] = high[rows]
            gs_ref[2 * start + BLOCKC : 2 * start + 2 * BLOCKC, lanes] = low[rows]


def diagonal_of(gram):
    row = lax.broadcasted_iota(jnp.int32, gram.shape, 0)
    col = lax.broadcasted_iota(jnp.int32, gram.shape, 1)
    eye = row == col
    return eye, jnp.sum(jnp.where(eye, gram, 0.0), axis=1, keepdims=True)


def sweep_steps(order_ref, gs_ref, target_ref, stacked_ref, keep_ref=None, out_ref=None):
    comps = target_ref.shape[0]
    blocks = comps // BLOCKC
    for step in range(INNER * blocks):
        block = order_ref[step % blocks]
        rows = pl.ds(pl.multiple_of(block * BLOCKC, BLOCKC), BLOCKC)
        low_rows = pl.ds(pl.multiple_of(comps + block * BLOCKC, BLOCKC), BLOCKC)
        pair = pl.ds(pl.multiple_of(block * 2 * BLOCKC, 2 * BLOCKC), 2 * BLOCKC)
        product = jnp.dot(gs_ref[pair, :], stacked_ref[...], preferred_element_type=F32)
        updated = jnp.maximum(target_ref[rows, :] + (product[:BLOCKC] + product[BLOCKC:]), 0.0)
        if keep_ref is not None:
            updated = updated * keep_ref[rows, :]
        high = updated.astype(BF16)
        stacked_ref[rows, :] = high
        stacked_ref[low_rows, :] = (updated - high.astype(F32)).astype(BF16)
        if out_ref is not None:
            out_ref[rows, :] = updated


def movie_copies(movie_refs, movie_bufs, sems):
    copies = []
    for index, (ref, buf) in enumerate(zip(movie_refs, movie_bufs)):
        share = buf.shape[0]
        place = lax.axis_index("tm") * share if ref.shape[0] > share else 0
        copies.append(pltpu.make_async_copy(ref.at[pl.ds(place, share), :], buf, sems.at[index]))
    return copies


def prepare_kernel(pieces, *refs):
    trace_refs, movie_refs, refs = refs[:pieces], refs[pieces : 2 * pieces], refs[2 * pieces :]
    fp_ref, support_ref, target_ref, keep_ref, gs_ref, scale_ref = refs[:6]
    movie_bufs, sems = refs[6:-1], refs[-1]
    comps, share = target_ref.shape
    copies = movie_copies(movie_refs, movie_bufs, sems)
    for copy in copies:
        copy.start()

    me = lax.axis_index("tm")
    count = fp_ref.shape[1] // share
    first = me * share
    gram = None
    for ref in trace_refs:
        part = lax.dot_general(ref[...], ref[...], BY_LAST, preferred_element_type=F32)
        gram = part if gram is None else gram + part
    eye, diagonal = diagonal_of(gram)
    inverse = 1.0 / (diagonal + 6.0 * smooth_weight)
    split_rows(jnp.where(eye, 6.0 * smooth_weight * inverse, -gram * inverse), gs_ref)
    scale_ref[...] = jnp.broadcast_to(smooth_weight * inverse, scale_ref.shape)

    lane = lax.broadcasted_iota(jnp.int32, (comps, XC), 1)
    column = lax.broadcasted_iota(jnp.int32, support_ref.shape, 1)
    support = support_ref[...].astype(F32)

    def row_at(offset):
        at = pl.multiple_of(first + offset, XC)
        return fp_ref[:, pl.ds(at, XC)].astype(F32)

    below = pl.multiple_of(jnp.maximum(first - XC, 0), XC)
    above = pl.multiple_of(jnp.minimum(first + share, fp_ref.shape[1] - XC), XC)
    before = fp_ref[:, pl.ds(below, XC)].astype(F32) * jnp.where(me > 0, 1.0, 0.0)
    center = row_at(0)
    for offset in range(0, share, XC):
        if offset + XC < share:
            after = row_at(offset + XC)
        else:
            after = fp_ref[:, pl.ds(above, XC)].astype(F32) * jnp.where(me < count - 1, 1.0, 0.0)
        left = jnp.where(lane == 0, 0.0, pltpu.roll(center, 1, 1))
        right = jnp.where(lane == XC - 1, 0.0, pltpu.roll(center, XC - 1, 1))
        beside = before + after + left + right
        lanes = slice(offset, offset + XC)
        target_ref[:, lanes] = smooth_weight * (6.0 * center - beside)
        here = me * (share // XC) + offset // XC
        kept = jnp.sum(jnp.where(column == here, support, 0.0), axis=1, keepdims=True)
        keep_ref[:, lanes] = jnp.broadcast_to(kept, (comps, XC))
        before, center = center, after

    for copy in copies:
        copy.wait()
    correlation = None
    for ref, buf in zip(trace_refs, movie_bufs):
        part = lax.dot_general(ref[...], buf[...], BY_LAST, preferred_element_type=F32)
        correlation = part if correlation is None else correlation + part
    target_ref[...] = (correlation - target_ref[...]) * inverse


def footprint_kernel(pieces, order_ref, target_ref, keep_ref, gs_ref, scale_ref, fp_ref, head_ref, tail_ref, *refs):
    movie_refs, half_ref, joined_refs, refs = refs[:pieces], refs[pieces], refs[pieces + 1 : 2 * pieces + 1], refs[2 * pieces + 1 :]
    goal_ref, stacked_ref, movie_bufs, sems = refs[0], refs[1], refs[2:-1], refs[-1]
    comps, share = target_ref.shape
    copies = movie_copies(movie_refs, movie_bufs, sems)
    for copy in copies:
        copy.start()
    me = lax.axis_index("tm")
    for offset in range(0, share, XC):
        lanes = slice(offset, offset + XC)
        sides = head_ref[:, lanes].astype(F32) + tail_ref[:, lanes].astype(F32)
        goal_ref[:, lanes] = target_ref[:, lanes] + sides * scale_ref[...]
        at = pl.multiple_of(me * share + offset, XC)
        center = fp_ref[:, pl.ds(at, XC)].astype(F32)
        stacked_ref[:comps, lanes] = (center * keep_ref[:, lanes]).astype(BF16)
    stacked_ref[comps:, :] = jnp.zeros((comps, share), BF16)
    sweep_steps(order_ref, gs_ref, goal_ref, stacked_ref, keep_ref)
    half = stacked_ref[:comps, :]
    half_ref[...] = half
    for copy in copies:
        copy.wait()
    cross = lax.dot_general(half, half, BY_LAST, preferred_element_type=F32)
    for buf, joined_ref in zip(movie_bufs, joined_refs):
        frames = buf.shape[1]
        joined_ref[:, :frames] = jnp.dot(half, buf[...], preferred_element_type=F32)
        joined_ref[:, frames:] = cross


def chunk_kernel(stride, ours_ref, theirs_ref, *out_refs):
    rows = out_refs[0].shape[0]
    digit = lax.axis_index("vox") // stride % GROUP
    for index, out_ref in enumerate(out_refs):
        at = pl.ds(pl.multiple_of((digit ^ index) * rows, rows), rows)
        out_ref[...] = ours_ref[at, :] + theirs_ref[at, :]


def trace_kernel(order_ref, traces_ref, *refs):
    joined_refs, (out_ref, joined, goal_ref, gs_ref, stacked_ref) = refs[:-5], refs[-5:]
    comps, frames = traces_ref.shape
    digit = lax.axis_index("vox") % GROUP
    for index, ref in enumerate(joined_refs):
        rows = ref.shape[0]
        place = pl.multiple_of((digit ^ index) * rows, rows) if rows < comps else 0
        joined[pl.ds(place, rows), :] = ref[...]
    cross = joined[:, frames:]
    eye, diagonal = diagonal_of(cross)
    inverse = 1.0 / (diagonal + ridge_weight)
    split_rows(jnp.where(eye, 0.0, -cross * inverse), gs_ref)
    goal_ref[...] = joined[:, :frames] * inverse
    stacked_ref[:comps, :] = traces_ref[...]
    stacked_ref[comps:, :] = jnp.zeros((comps, frames), BF16)
    sweep_steps(order_ref, gs_ref, goal_ref, stacked_ref, None, out_ref)


def swap(array):
    return lax.ppermute(array, "tm", [(0, 1), (1, 0)])


def from_group(arrays, stride):
    count = lax.axis_size("vox")
    return [lax.ppermute(array, "vox", [(i, i ^ (k * stride)) for i in range(count)]) for k, array in arrays]


def tree_sum(own, others):
    return (own + others[0]) + (others[1] + others[2])


def sum_over_vox(ours, theirs):
    comps, width = ours.shape
    rows = comps // GROUP
    top = lax.axis_size("vox") // GROUP
    chunks = pl.pallas_call(
        functools.partial(chunk_kernel, 1),
        out_shape=[shape_of((rows, width), F32)] * GROUP,
        in_specs=[VMEM] * 2,
        compiler_params=SMALL,
        out_specs=[VMEM] * GROUP,
    )(ours, theirs)
    mine = tree_sum(chunks[0], from_group([(k, chunks[k]) for k in range(1, GROUP)], 1))
    mine = tree_sum(mine, from_group([(k, mine) for k in range(1, GROUP)], top))
    return [mine] + from_group([(k, mine) for k in range(1, GROUP)], 1)


def local(movie, footprints, traces, support, block_order):
    comps, vox_local = footprints.shape
    frames = traces.shape[1]
    cores = lax.axis_size("tm")
    planes = lax.axis_size("vox")
    share = vox_local // cores
    me = lax.axis_index("tm")

    own = lax.dynamic_slice_in_dim(footprints, me * share, share, 1)
    head = lax.ppermute(own, "vox", [(i, i + 1) for i in range(planes - 1)])
    tail = lax.ppermute(own, "vox", [(i + 1, i) for i in range(planes - 1)])
    if cores == 2:
        movies = [movie, swap(movie)]
        all_traces = [traces, swap(traces)]
    else:
        movies = [lax.all_to_all(movie, "tm", 0, 1, tiled=True)]
        all_traces = [lax.all_gather(traces, "tm", axis=1, tiled=True)]
    pieces = len(movies)
    movie_scratch = [pltpu.VMEM((share, part.shape[1]), BF16) for part in movies] + [pltpu.SemaphoreType.DMA((pieces,))]

    target, keep, system, scale = pl.pallas_call(
        functools.partial(prepare_kernel, pieces),
        out_shape=[
            shape_of((comps, share), F32),
            shape_of((comps, share), F32),
            shape_of((2 * comps, 2 * comps), BF16),
            shape_of((comps, XC), F32),
        ],
        in_specs=[VMEM] * pieces + [ANY] * pieces + [VMEM] * 2,
        compiler_params=SMALL,
        out_specs=[VMEM] * 4,
        scratch_shapes=movie_scratch,
    )(*all_traces, *movies, footprints, support)

    half, *joined = pl.pallas_call(
        functools.partial(footprint_kernel, pieces),
        out_shape=[shape_of((comps, share), BF16)]
        + [shape_of((comps, part.shape[1] + comps), F32) for part in movies],
        in_specs=[SMEM] + [VMEM] * 7 + [ANY] * pieces,
        compiler_params=SMALL,
        out_specs=[VMEM] * (pieces + 1),
        scratch_shapes=[pltpu.VMEM((comps, share), F32), pltpu.VMEM((2 * comps, share), BF16)] + movie_scratch,
    )(block_order, target, keep, system, scale, footprints, head, tail, *movies)

    if cores == 2:
        ours, theirs = joined[0], swap(joined[1])
        other = swap(half)
        new_footprints = jnp.where(
            me == 0, jnp.concatenate([half, other], axis=1), jnp.concatenate([other, half], axis=1)
        )
    else:
        joined = joined[0]
        projection = lax.psum_scatter(joined[:, : frames * cores], "tm", scatter_dimension=1, tiled=True)
        ours = jnp.concatenate([projection, lax.psum(joined[:, frames * cores :], "tm")], axis=1)
        theirs = jnp.zeros_like(ours)
        new_footprints = lax.all_gather(half, "tm", axis=1, tiled=True)

    if planes == GROUP * GROUP:
        joined = sum_over_vox(ours, theirs)
    else:
        joined = [lax.psum(ours + theirs, "vox")]
    new_traces = pl.pallas_call(
        trace_kernel,
        out_shape=shape_of((comps, frames), F32),
        in_specs=[SMEM] + [VMEM] * (len(joined) + 1),
        compiler_params=SMALL,
        out_specs=VMEM,
        scratch_shapes=[
            pltpu.VMEM((comps, frames + comps), F32),
            pltpu.VMEM((comps, frames), F32),
            pltpu.VMEM((2 * comps, 2 * comps), BF16),
            pltpu.VMEM((2 * comps, frames), BF16),
        ],
    )(block_order, traces, *joined)
    return (new_footprints, new_traces)


def solution(mesh):
    placed = (P("vox", "tm"), P(None, "vox"), P(None, "tm"), P(None, "vox"), P())
    return jax.shard_map(
        local,
        mesh=mesh,
        in_specs=placed,
        out_specs=(P(None, "vox"), P(None, "tm")),
        check_vma=False,
    )
```

time: 73.9 us -> 58.8 us (0.80)
  blocking collectives: 31.8 us -> 0 us
  starting transfers between devices: 6.79 us -> 19.3 us
  waiting for transfers between devices: 8.71 us -> 18.7 us
  Pallas kernels: 19 us -> 13.5 us
  local copies, waits for them, and re-layouts: 2.25 us -> 5.33 us
  matrix products: 2.71 us -> 0 us
    all_to_all x2 -> x0, blocking collectives: 31.8 us -> none  [the longest x1 17.5 us: sum_over_vox(): parts = lax.all_to_all(joined, 'vox', 0, 0, tiled=True)]
    ppermute x0 -> x9, starting transfers between devices: none -> 12.1 us  [from_group(): lax.ppermute(array, 'vox', [(i, i ^ k * stride) for i in range(count)])]
    ppermute x0 -> x9, waiting for transfers between devices: none -> 11.6 us  [from_group(): lax.ppermute(array, 'vox', [(i, i ^ k * stride) for i in range(count)])]
    pallas_call x3, Pallas kernels: 13.3 us -> 8.17 us  [the longest x1 6.53 us: local(): pl.pallas_call(functools.partial(footprint_kernel, pieces), out_shape=[sh...]
    dot_general x2 -> x0, matrix products: 2.71 us -> none  [the longest x1 2.53 us: local(): lax.dot_general(traces, movie, (((1,), (1,)), ((), ())), preferred_elemen...]
    unnamed x13 -> x15, local copies, waits for them, and re-layouts: 2.16 us -> 4.36 us
    ppermute x1, waiting for transfers between devices: 1.91 us -> 0.01 us  [local(): tail = lax.ppermute(own, 'vox', [(i + 1, i) for i in range(planes - 1)])]
    add x2, other arithmetic: 1.49 us -> 0.04 us  [tree_sum(): return own + others[0] + (others[1] + others[2])]
  transfers between devices with their start and end apart: 5 -> 15, of which waited for: 3 -> 9; matrix products, arithmetic and copies ran while one was open for 3% -> 5% of each run, Pallas kernels for 4% -> 3%
where the time goes in v2:
time: 58.8 us; the launch traced here: 58.5 us
  starting transfers between devices  19.3 us (33%)
  waiting for transfers between devices  18.7 us (32%)
  Pallas kernels  13.5 us (23%)
  local copies, waits for them, and re-layouts  5.33 us (9%)
  other arithmetic  0.96 us (2%)
  between operations  0.71 us (1%)
    ppermute x9, starting transfers between devices, from_group(): lax.ppermute(array, 'vox', [(i, i ^ k * stride) for i in range(count)])  12.1 us
    ppermute x9, waiting for transfers between devices, from_group(): lax.ppermute(array, 'vox', [(i, i ^ k * stride) for i in range(count)])  11.6 us
    pallas_call x1, Pallas kernels, local(): pl.pallas_call(functools.partial(footprint_kernel, pieces), out_shape=[sh...  6.53 us
    pallas_call x1, Pallas kernels, local(): pl.pallas_call(trace_kernel, out_shape=shape_of((comps, frames), F32), in...  5.28 us
    ppermute x1, starting transfers between devices, local(): head = lax.ppermute(own, 'vox', [(i, i + 1) for i in range(planes - 1)])  5.06 us
    ppermute x1, waiting for transfers between devices, local(): head = lax.ppermute(own, 'vox', [(i, i + 1) for i in range(planes - 1)])  4.94 us
    unnamed x15, local copies, waits for them, and re-layouts  4.36 us
    ppermute x4, waiting for transfers between devices, swap(): return lax.ppermute(array, 'tm', [(0, 1), (1, 0)])  2.14 us
  transfers between devices with their start and end apart: 15, of which 9 were waited for; matrix products, arithmetic and copies ran while one was open for 5% of the time, Pallas kernels for 3%

profile of v2, /device:TPU:0, one launch (start us, length us, event | category | flops | bytes accessed | tf_op | source)
XLA Modules:
  0.0 58.5 jit_solution(6483141162996806290)
XLA Ops:
  0.6 0.5 collective-permute-start.1
  1.1 1.0 %constant_dynamic-slice_fusion = bf16[128,1024]{1,0:T(8,128)(2,1)S(1)} fusion(bf16[128,2048]{1,0:T(8,128)(2,1)} %fp_ref.1, s32[]{:T(128)S(6)} %select_n.12), kind=kLoop, calls=%fused_computation.3 | loop fusion | bytes 524292 | tf_op jit(solution)/shard_map/dynamic_slice | solution.py:226
  2.1 1.3 %collective-permute-start.3 = (bf16[128,1024]{1,0:T(8,128)(2,1)S(1)}, bf16[128,1024]{1,0:T(8,128)(2,1)S(1)}, u32[]{:S(2)}, u32[]{:S(2)}) collective-permute-start(bf16[128,1024]{1,0:T(8,128)(2,1)S(1)} %constant_dynamic-slice_fusion), channel_id=1, source_target_pairs={{2,0},{4,2},{6,4},{8,6},{10,8},{12,10},{14,12},{16,14},{18,16},{20... | collective-permute-start | bytes 786440 | tf_op jit(solution)/shard_map/ppermute | solution.py:228
  3.4 5.1 %collective-permute-start.2 = (bf16[128,1024]{1,0:T(8,128)(2,1)S(1)}, bf16[128,1024]{1,0:T(8,128)(2,1)S(1)}, u32[]{:S(2)}, u32[]{:S(2)}) collective-permute-start(bf16[128,1024]{1,0:T(8,128)(2,1)S(1)} %constant_dynamic-slice_fusion), channel_id=1, source_target_pairs={{0,2},{2,4},{4,6},{6,8},{8,10},{10,12},{12,14},{14,16},{16,18},{18... | collective-permute-start | bytes 786440 | tf_op jit(solution)/shard_map/ppermute | solution.py:227
  8.5 0.3 collective-permute-start
  8.8 0.0 copy-start.6
  8.8 0.8 %copy.7.refs_5_ = s32[128,16]{1,0:T(8,128)S(1)} copy(s32[128,16]{0,1:T(8,128)} %param.8) | data formatting | bytes 16384 | tf_op args[3]
  9.6 0.5 collective-permute-done.refs_1_
  10.1 0.0 collective-permute-done.1.refs_3_.refs_1_
  10.1 0.0 copy-start
  10.1 1.6 %copy-done = bf16[2048,512]{1,0:T(8,128)(2,1)S(1)} copy-done((bf16[2048,512]{1,0:T(8,128)(2,1)S(1)}, bf16[2048,512]{1,0:T(8,128)(2,1)}, u32[]{:S(2)}) %copy-start) | copy-done | bytes 2097176
  11.7 0.0 copy-start.2
  11.7 1.0 %copy-done.2 = bf16[128,2048]{1,0:T(8,128)(2,1)S(1)} copy-done((bf16[128,2048]{1,0:T(8,128)(2,1)S(1)}, bf16[128,2048]{1,0:T(8,128)(2,1)}, u32[]{:S(2)}) %copy-start.2) | copy-done | bytes 524312
  12.7 0.0 copy-start.4
  12.8 0.9 %copy-done.4 = bf16[128,512]{1,0:T(8,128)(2,1)S(1)} copy-done((bf16[128,512]{1,0:T(8,128)(2,1)S(1)}, bf16[128,512]{1,0:T(8,128)(2,1)}, u32[]{:S(2)}) %copy-start.4) | copy-done | bytes 131096
  13.7 1.6 %shard_map.68 = (f32[128,1024]{1,0:T(8,128)S(1)}, f32[128,1024]{1,0:T(8,128)S(1)}, bf16[256,256]{1,0:T(8,128)(2,1)S(1)}, f32[128,128]{1,0:T(8,128)S(1)}) custom-call(bf16[128,512]{1,0:T(8,128)(2,1)S(1)} %copy-done.4, bf16[128,512]{1,0:T(8,128)(2,1)S(1)} %collective-permute-done.refs_1_, bf16[2048,512]{1,0:T(8,128)(2,1)S(1)} %copy-done, ...), custom_call_target="tpu_custom_call" | custom-call | tf_op jit(solution)/shard_map/pallas_call | solution.py:238
  15.3 0.0 collective-permute-done.3.tail_ref
  15.3 4.9 %collective-permute-done.2.head_ref = bf16[128,1024]{1,0:T(8,128)(2,1)S(1)} collective-permute-done((bf16[128,1024]{1,0:T(8,128)(2,1)S(1)}, bf16[128,1024]{1,0:T(8,128)(2,1)S(1)}, u32[]{:S(2)}, u32[]{:S(2)}) %collective-permute-start.2) | collective-permute-done | bytes 262176 | tf_op jit(solution)/shard_map/ppermute | solution.py:227
  20.2 0.0 copy-done.6
  20.2 0.0 copy-done.1
  20.2 0.0 copy-done.3
  20.2 6.5 %shard_map.69 = (bf16[128,1024]{1,0:T(8,128)(2,1)S(1)}, f32[128,640]{1,0:T(8,128)S(1)}, f32[128,640]{1,0:T(8,128)S(1)}) custom-call(s32[8]{0:T(128)S(1)} %copy-done.6, f32[128,1024]{1,0:T(8,128)S(1)} %get-tuple-element.13.target_ref, f32[128,1024]{1,0:T(8,128)S(1)} %get-tuple-element.14.keep_ref, bf16[256,256]{1,0:T(8,128)(2,1)S(1)} %get-tuple-element.15.gs_ref, ...), custom_call_target="tpu_custom_call" | custom-call | tf_op jit(solution)/shard_map/pallas_call | solution.py:252
  26.8 0.0 copy-start.5
  26.8 0.1 collective-permute-start.5
  26.9 1.6 %collective-permute-done.5.theirs_ref = f32[128,640]{1,0:T(8,128)S(1)} collective-permute-done((f32[128,640]{1,0:T(8,128)S(1)}, f32[128,640]{1,0:T(8,128)S(1)}, u32[]{:S(2)}, u32[]{:S(2)}) %collective-permute-start.5) | collective-permute-done | bytes 327712 | tf_op jit(solution)/shard_map/ppermute | solution.py:190
  28.5 2.5 %collective-permute-start.6 = (f32[32,640]{1,0:T(8,128)S(1)}, f32[32,640]{1,0:T(8,128)S(1)}, u32[]{:S(2)}, u32[]{:S(2)}) collective-permute-start(f32[32,640]{1,0:T(8,128)S(1)} %get-tuple-element.21), channel_id=1, source_target_pairs={{0,2},{2,0},{4,6},{6,4},{8,10},{10,8},{12,14},{14,12},{16,18},{18,... | collective-permute-start | bytes 245768 | tf_op jit(solution)/shard_map/ppermute | solution.py:195
  31.0 0.0 collective-permute-start.7
  31.0 1.5 %collective-permute-start.8 = (f32[32,640]{1,0:T(8,128)S(1)}, f32[32,640]{1,0:T(8,128)S(1)}, u32[]{:S(2)}, u32[]{:S(2)}) collective-permute-start(f32[32,640]{1,0:T(8,128)S(1)} %get-tuple-element.23), channel_id=1, source_target_pairs={{0,6},{2,4},{4,2},{6,0},{8,14},{10,12},{12,10},{14,8},{16,22},{18,... | collective-permute-start | bytes 245768 | tf_op jit(solution)/shard_map/ppermute | solution.py:195
  32.6 1.2 %collective-permute-done.6 = f32[32,640]{1,0:T(8,128)S(1)} collective-permute-done((f32[32,640]{1,0:T(8,128)S(1)}, f32[32,640]{1,0:T(8,128)S(1)}, u32[]{:S(2)}, u32[]{:S(2)}) %collective-permute-start.6) | collective-permute-done | bytes 81952 | tf_op jit(solution)/shard_map/ppermute | solution.py:195
  33.8 3.2 %collective-permute-done.7 = f32[32,640]{1,0:T(8,128)S(1)} collective-permute-done((f32[32,640]{1,0:T(8,128)S(1)}, f32[32,640]{1,0:T(8,128)S(1)}, u32[]{:S(2)}, u32[]{:S(2)}) %collective-permute-start.7) | collective-permute-done | bytes 81952 | tf_op jit(solution)/shard_map/ppermute | solution.py:195
  37.0 0.0 collective-permute-done.8
  37.1 2.6 %collective-permute-start.11 = (f32[32,640]{1,0:T(8,128)S(1)}, f32[32,640]{1,0:T(8,128)S(1)}, u32[]{:S(2)}, u32[]{:S(2)}) collective-permute-start(f32[32,640]{1,0:T(8,128)S(1)} %add_add_fusion.1), channel_id=1, source_target_pairs={{0,24},{2,26},{4,28},{6,30},{8,16},{10,18},{12,20},{14,22},{16,8},... | collective-permute-start | bytes 245768 | tf_op jit(solution)/shard_map/ppermute | solution.py:195
  39.7 0.5 collective-permute-start.10
  40.2 1.3 %collective-permute-start.9 = (f32[32,640]{1,0:T(8,128)S(1)}, f32[32,640]{1,0:T(8,128)S(1)}, u32[]{:S(2)}, u32[]{:S(2)}) collective-permute-start(f32[32,640]{1,0:T(8,128)S(1)} %add_add_fusion.1), channel_id=1, source_target_pairs={{0,8},{2,10},{4,12},{6,14},{8,0},{10,2},{12,4},{14,6},{16,24},{18,... | collective-permute-start | bytes 245768 | tf_op jit(solution)/shard_map/ppermute | solution.py:195
  41.5 0.0 collective-permute-start.4
  41.5 2.7 %collective-permute-done.11 = f32[32,640]{1,0:T(8,128)S(1)} collective-permute-done((f32[32,640]{1,0:T(8,128)S(1)}, f32[32,640]{1,0:T(8,128)S(1)}, u32[]{:S(2)}, u32[]{:S(2)}) %collective-permute-start.11) | collective-permute-done | bytes 81952 | tf_op jit(solution)/shard_map/ppermute | solution.py:195
  44.2 2.1 %collective-permute-done.10 = f32[32,640]{1,0:T(8,128)S(1)} collective-permute-done((f32[32,640]{1,0:T(8,128)S(1)}, f32[32,640]{1,0:T(8,128)S(1)}, u32[]{:S(2)}, u32[]{:S(2)}) %collective-permute-start.10) | collective-permute-done | bytes 81952 | tf_op jit(solution)/shard_map/ppermute | solution.py:195
  46.3 0.0 collective-permute-done.9
  46.4 2.1 %collective-permute-start.14 = (f32[32,640]{1,0:T(8,128)S(1)}, f32[32,640]{1,0:T(8,128)S(1)}, u32[]{:S(2)}, u32[]{:S(2)}) collective-permute-start(f32[32,640]{1,0:T(8,128)S(1)} %add_add_fusion.refs_0_), channel_id=1, source_target_pairs={{0,6},{2,4},{4,2},{6,0},{8,14},{10,12},{12,10},{14,8},{16,22},{18,... | collective-permute-start | bytes 245768 | tf_op jit(solution)/shard_map/ppermute | solution.py:195
  48.5 0.0 collective-permute-start.13
  48.5 1.4 %collective-permute-start.12 = (f32[32,640]{1,0:T(8,128)S(1)}, f32[32,640]{1,0:T(8,128)S(1)}, u32[]{:S(2)}, u32[]{:S(2)}) collective-permute-start(f32[32,640]{1,0:T(8,128)S(1)} %add_add_fusion.refs_0_), channel_id=1, source_target_pairs={{0,2},{2,0},{4,6},{6,4},{8,10},{10,8},{12,14},{14,12},{16,18},{18,... | collective-permute-start | bytes 245768 | tf_op jit(solution)/shard_map/ppermute | solution.py:195
  49.9 0.0 collective-permute-done.4
  49.9 0.9 %maximum_select_fusion = bf16[128,2048]{1,0:T(8,128)(2,1)} fusion(bf16[128,1024]{1,0:T(8,128)(2,1)S(1)} %collective-permute-done.4, bf16[128,1024]{1,0:T(8,128)(2,1)S(1)} %get-tuple-element.17, pred[]{:T(512)S(6)} %eq.3), kind=kLoop, calls=%fused_computation | loop fusion | flops 2359296 | bytes 1048577 | tf_op jit(solution)/shard_map/jit(_where)/select_n | solution.py:265
  50.8 1.9 %collective-permute-done.14.refs_3_ = f32[32,640]{1,0:T(8,128)S(1)} collective-permute-done((f32[32,640]{1,0:T(8,128)S(1)}, f32[32,640]{1,0:T(8,128)S(1)}, u32[]{:S(2)}, u32[]{:S(2)}) %collective-permute-start.14) | collective-permute-done | bytes 81952 | tf_op jit(solution)/shard_map/ppermute | solution.py:195
  52.7 0.5 collective-permute-done.13.refs_2_
  53.2 0.0 collective-permute-done.12.refs_1_
  53.2 0.0 copy-done.5
  53.2 5.3 %shard_map.71 = f32[128,512]{1,0:T(8,128)} custom-call(s32[8]{0:T(128)S(1)} %copy-done.6, bf16[128,512]{1,0:T(8,128)(2,1)S(1)} %copy-done.5, f32[32,640]{1,0:T(8,128)S(1)} %add_add_fusion.refs_0_, f32[32,640]{1,0:T(8,128)S(1)} %collective-permute-done.12.refs_1_, f32[32,640]{1,0:T(8,128)S(1)} %collective-permute-done.13.refs_2_, ...), custom_call_target="tpu_custom_call" | custom-call | tf_op jit(solution)/shard_map/pallas_call | solution.py:279
  (5 shorter events, 0.1 us)
Async XLA Ops:
  0.6 9.5 %collective-permute-start.1 = (bf16[2048,512]{1,0:T(8,128)(2,1)}, bf16[2048,512]{1,0:T(8,128)(2,1)S(1)}, u32[]{:S(2)}, u32[]{:S(2)}) collective-permute-start(bf16[2048,512]{1,0:T(8,128)(2,1)} %refs_0_.3), channel_id=1, source_target_pairs={{0,1},{1,0},{2,3},{3,2},{4,5},{5,4},{6,7},{7,6},{8,9},{9,8},{10,11... | collective-permute-start | bytes 6291464 | tf_op jit(solution)/shard_map/ppermute | solution.py:190
  2.1 13.2 %collective-permute-start.3 = (bf16[128,1024]{1,0:T(8,128)(2,1)S(1)}, bf16[128,1024]{1,0:T(8,128)(2,1)S(1)}, u32[]{:S(2)}, u32[]{:S(2)}) collective-permute-start(bf16[128,1024]{1,0:T(8,128)(2,1)S(1)} %constant_dynamic-slice_fusion), channel_id=1, source_target_pairs={{2,0},{4,2},{6,4},{8,6},{10,8},{12,10},{14,12},{16,14},{18,16},{20... | collective-permute-start | bytes 786440 | tf_op jit(solution)/shard_map/ppermute | solution.py:228
  3.4 16.8 %collective-permute-start.2 = (bf16[128,1024]{1,0:T(8,128)(2,1)S(1)}, bf16[128,1024]{1,0:T(8,128)(2,1)S(1)}, u32[]{:S(2)}, u32[]{:S(2)}) collective-permute-start(bf16[128,1024]{1,0:T(8,128)(2,1)S(1)} %constant_dynamic-slice_fusion), channel_id=1, source_target_pairs={{0,2},{2,4},{4,6},{6,8},{8,10},{10,12},{12,14},{14,16},{16,18},{18... | collective-permute-start | bytes 786440 | tf_op jit(solution)/shard_map/ppermute | solution.py:227
  8.5 1.6 %collective-permute-start = (bf16[128,512]{1,0:T(8,128)(2,1)}, bf16[128,512]{1,0:T(8,128)(2,1)S(1)}, u32[]{:S(2)}, u32[]{:S(2)}) collective-permute-start(bf16[128,512]{1,0:T(8,128)(2,1)} %traces_ref.1), channel_id=1, source_target_pairs={{0,1},{1,0},{2,3},{3,2},{4,5},{5,4},{6,7},{7,6},{8,9},{9,8},{10,11... | collective-permute-start | bytes 393224 | tf_op jit(solution)/shard_map/ppermute | solution.py:190
  8.8 11.5 %copy-start.6 = (s32[8]{0:T(128)S(1)}, s32[8]{0:T(128)}, u32[]{:S(2)}) copy-start(s32[8]{0:T(128)} %order_ref.3) | copy-start | bytes 100
  10.1 1.6 %copy-start = (bf16[2048,512]{1,0:T(8,128)(2,1)S(1)}, bf16[2048,512]{1,0:T(8,128)(2,1)}, u32[]{:S(2)}) copy-start(bf16[2048,512]{1,0:T(8,128)(2,1)} %refs_0_.3) | copy-start | bytes 6291460
  11.7 1.0 %copy-start.2 = (bf16[128,2048]{1,0:T(8,128)(2,1)S(1)}, bf16[128,2048]{1,0:T(8,128)(2,1)}, u32[]{:S(2)}) copy-start(bf16[128,2048]{1,0:T(8,128)(2,1)} %fp_ref.1) | copy-start | bytes 1572868
  12.7 0.9 %copy-start.4 = (bf16[128,512]{1,0:T(8,128)(2,1)S(1)}, bf16[128,512]{1,0:T(8,128)(2,1)}, u32[]{:S(2)}) copy-start(bf16[128,512]{1,0:T(8,128)(2,1)} %traces_ref.1) | copy-start | bytes 393220
  13.7 6.6 %copy-start.1 = (bf16[2048,512]{1,0:T(8,128)(2,1)S(1)}, bf16[2048,512]{1,0:T(8,128)(2,1)}, u32[]{:S(2)}) copy-start(bf16[2048,512]{1,0:T(8,128)(2,1)} %refs_0_.3) | copy-start | bytes 6291460
  13.7 6.6 %copy-start.3 = (bf16[128,2048]{1,0:T(8,128)(2,1)S(1)}, bf16[128,2048]{1,0:T(8,128)(2,1)}, u32[]{:S(2)}) copy-start(bf16[128,2048]{1,0:T(8,128)(2,1)} %fp_ref.1) | copy-start | bytes 1572868
  26.8 26.4 %copy-start.5 = (bf16[128,512]{1,0:T(8,128)(2,1)S(1)}, bf16[128,512]{1,0:T(8,128)(2,1)}, u32[]{:S(2)}) copy-start(bf16[128,512]{1,0:T(8,128)(2,1)} %traces_ref.1) | copy-start | bytes 393220
  26.8 1.7 %collective-permute-start.5 = (f32[128,640]{1,0:T(8,128)S(1)}, f32[128,640]{1,0:T(8,128)S(1)}, u32[]{:S(2)}, u32[]{:S(2)}) collective-permute-start(f32[128,640]{1,0:T(8,128)S(1)} %get-tuple-element.19), channel_id=1, source_target_pairs={{0,1},{1,0},{2,3},{3,2},{4,5},{5,4},{6,7},{7,6},{8,9},{9,8},{10,11... | collective-permute-start | bytes 983048 | tf_op jit(solution)/shard_map/ppermute | solution.py:190
  28.5 5.3 %collective-permute-start.6 = (f32[32,640]{1,0:T(8,128)S(1)}, f32[32,640]{1,0:T(8,128)S(1)}, u32[]{:S(2)}, u32[]{:S(2)}) collective-permute-start(f32[32,640]{1,0:T(8,128)S(1)} %get-tuple-element.21), channel_id=1, source_target_pairs={{0,2},{2,0},{4,6},{6,4},{8,10},{10,8},{12,14},{14,12},{16,18},{18,... | collective-permute-start | bytes 245768 | tf_op jit(solution)/shard_map/ppermute | solution.py:195
  31.0 6.0 %collective-permute-start.7 = (f32[32,640]{1,0:T(8,128)S(1)}, f32[32,640]{1,0:T(8,128)S(1)}, u32[]{:S(2)}, u32[]{:S(2)}) collective-permute-start(f32[32,640]{1,0:T(8,128)S(1)} %get-tuple-element.22), channel_id=1, source_target_pairs={{0,4},{2,6},{4,0},{6,2},{8,12},{10,14},{12,8},{14,10},{16,20},{18,... | collective-permute-start | bytes 245768 | tf_op jit(solution)/shard_map/ppermute | solution.py:195
  31.0 6.0 %collective-permute-start.8 = (f32[32,640]{1,0:T(8,128)S(1)}, f32[32,640]{1,0:T(8,128)S(1)}, u32[]{:S(2)}, u32[]{:S(2)}) collective-permute-start(f32[32,640]{1,0:T(8,128)S(1)} %get-tuple-element.23), channel_id=1, source_target_pairs={{0,6},{2,4},{4,2},{6,0},{8,14},{10,12},{12,10},{14,8},{16,22},{18,... | collective-permute-start | bytes 245768 | tf_op jit(solution)/shard_map/ppermute | solution.py:195
  37.1 7.2 %collective-permute-start.11 = (f32[32,640]{1,0:T(8,128)S(1)}, f32[32,640]{1,0:T(8,128)S(1)}, u32[]{:S(2)}, u32[]{:S(2)}) collective-permute-start(f32[32,640]{1,0:T(8,128)S(1)} %add_add_fusion.1), channel_id=1, source_target_pairs={{0,24},{2,26},{4,28},{6,30},{8,16},{10,18},{12,20},{14,22},{16,8},... | collective-permute-start | bytes 245768 | tf_op jit(solution)/shard_map/ppermute | solution.py:195
  39.7 6.6 %collective-permute-start.10 = (f32[32,640]{1,0:T(8,128)S(1)}, f32[32,640]{1,0:T(8,128)S(1)}, u32[]{:S(2)}, u32[]{:S(2)}) collective-permute-start(f32[32,640]{1,0:T(8,128)S(1)} %add_add_fusion.1), channel_id=1, source_target_pairs={{0,16},{2,18},{4,20},{6,22},{8,24},{10,26},{12,28},{14,30},{16,0},... | collective-permute-start | bytes 245768 | tf_op jit(solution)/shard_map/ppermute | solution.py:195
  40.2 6.2 %collective-permute-start.9 = (f32[32,640]{1,0:T(8,128)S(1)}, f32[32,640]{1,0:T(8,128)S(1)}, u32[]{:S(2)}, u32[]{:S(2)}) collective-permute-start(f32[32,640]{1,0:T(8,128)S(1)} %add_add_fusion.1), channel_id=1, source_target_pairs={{0,8},{2,10},{4,12},{6,14},{8,0},{10,2},{12,4},{14,6},{16,24},{18,... | collective-permute-start | bytes 245768 | tf_op jit(solution)/shard_map/ppermute | solution.py:195
  41.5 8.4 %collective-permute-start.4 = (bf16[128,1024]{1,0:T(8,128)(2,1)S(1)}, bf16[128,1024]{1,0:T(8,128)(2,1)S(1)}, u32[]{:S(2)}, u32[]{:S(2)}) collective-permute-start(bf16[128,1024]{1,0:T(8,128)(2,1)S(1)} %get-tuple-element.17), channel_id=1, source_target_pairs={{0,1},{1,0},{2,3},{3,2},{4,5},{5,4},{6,7},{7,6},{8,9},{9,8},{10,11... | collective-permute-start | bytes 786440 | tf_op jit(solution)/shard_map/ppermute | solution.py:190
  46.4 6.3 %collective-permute-start.14 = (f32[32,640]{1,0:T(8,128)S(1)}, f32[32,640]{1,0:T(8,128)S(1)}, u32[]{:S(2)}, u32[]{:S(2)}) collective-permute-start(f32[32,640]{1,0:T(8,128)S(1)} %add_add_fusion.refs_0_), channel_id=1, source_target_pairs={{0,6},{2,4},{4,2},{6,0},{8,14},{10,12},{12,10},{14,8},{16,22},{18,... | collective-permute-start | bytes 245768 | tf_op jit(solution)/shard_map/ppermute | solution.py:195
  48.5 4.7 %collective-permute-start.13 = (f32[32,640]{1,0:T(8,128)S(1)}, f32[32,640]{1,0:T(8,128)S(1)}, u32[]{:S(2)}, u32[]{:S(2)}) collective-permute-start(f32[32,640]{1,0:T(8,128)S(1)} %add_add_fusion.refs_0_), channel_id=1, source_target_pairs={{0,4},{2,6},{4,0},{6,2},{8,12},{10,14},{12,8},{14,10},{16,20},{18,... | collective-permute-start | bytes 245768 | tf_op jit(solution)/shard_map/ppermute | solution.py:195
  48.5 4.7 %collective-permute-start.12 = (f32[32,640]{1,0:T(8,128)S(1)}, f32[32,640]{1,0:T(8,128)S(1)}, u32[]{:S(2)}, u32[]{:S(2)}) collective-permute-start(f32[32,640]{1,0:T(8,128)S(1)} %add_add_fusion.refs_0_), channel_id=1, source_target_pairs={{0,2},{2,0},{4,6},{6,4},{8,10},{10,8},{12,14},{14,12},{16,18},{18,... | collective-permute-start | bytes 245768 | tf_op jit(solution)/shard_map/ppermute | solution.py:195

commit v3 on v2

--- a/solution.py
+++ b/solution.py
@@ -28,16 +28,17 @@
     return jax.ShapeDtypeStruct(dims, dtype)
 
 
-def split_rows(system, gs_ref):
-    comps = system.shape[0]
-    high = system.astype(BF16)
-    low = (system - high.astype(F32)).astype(BF16)
-    for start in range(0, comps, BLOCKC):
-        rows = slice(start, start + BLOCKC)
-        for side in range(2):
-            lanes = slice(side * comps, (side + 1) * comps)
-            gs_ref[2 * start : 2 * start + BLOCKC, lanes] = high[rows]
-            gs_ref[2 * start + BLOCKC : 2 * start + 2 * BLOCKC, lanes] = low[rows]
+def split_terms(array):
+    high = array.astype(BF16)
+    return high, (array - high.astype(F32)).astype(BF16)
+
+
+def rows_of(place):
+    return slice(place * BLOCKC, (place + 1) * BLOCKC)
+
+
+def rows_from(order_ref, place):
+    return pl.ds(pl.multiple_of(order_ref[place] * BLOCKC, BLOCKC), BLOCKC)
 
 
 def diagonal_of(gram):
@@ -47,23 +48,57 @@
     return eye, jnp.sum(jnp.where(eye, gram, 0.0), axis=1, keepdims=True)
 
 
-def sweep_steps(order_ref, gs_ref, target_ref, stacked_ref, keep_ref=None, out_ref=None):
-    comps = target_ref.shape[0]
+def store_system(system, gs_ref, coef_ref):
+    comps = system.shape[0]
     blocks = comps // BLOCKC
-    for step in range(INNER * blocks):
-        block = order_ref[step % blocks]
-        rows = pl.ds(pl.multiple_of(block * BLOCKC, BLOCKC), BLOCKC)
-        low_rows = pl.ds(pl.multiple_of(comps + block * BLOCKC, BLOCKC), BLOCKC)
-        pair = pl.ds(pl.multiple_of(block * 2 * BLOCKC, 2 * BLOCKC), 2 * BLOCKC)
+    high, low = split_terms(system)
+    for place in range(blocks):
+        rows = rows_of(place)
+        before = (place - 1) % blocks * BLOCKC
+        for side in range(2):
+            lanes = slice(side * comps, (side + 1) * comps)
+            gs_ref[rows_of(2 * place), lanes] = high[rows]
+            gs_ref[rows_of(2 * place + 1), lanes] = low[rows]
+        for k in range(BLOCKC):
+            coef_ref[place, k] = jnp.broadcast_to(system[rows, before + k : before + k + 1], (BLOCKC, XC))
+
+
+def sweep_steps(gs_ref, coef_ref, goal_ref, stacked_ref, value_ref, keep_ref=None):
+    comps, width = goal_ref.shape
+    blocks = comps // BLOCKC
+
+    def product_of(place):
+        pair = slice(2 * BLOCKC * place, 2 * BLOCKC * (place + 1))
         product = jnp.dot(gs_ref[pair, :], stacked_ref[...], preferred_element_type=F32)
-        updated = jnp.maximum(target_ref[rows, :] + (product[:BLOCKC] + product[BLOCKC:]), 0.0)
+        return product[:BLOCKC] + product[BLOCKC:]
+
+    steps = INNER * blocks
+    ready, change = product_of(0), None
+    for step in range(steps):
+        place = step % blocks
+        rows = rows_of(place)
+        following = product_of((step + 1) % blocks) if step + 1 < steps else None
+        base = goal_ref[rows, :] + ready
+        columns = []
+        for lane in range(0, width, XC):
+            lanes = slice(lane, lane + XC)
+            total = base[:, lanes]
+            if change is not None:
+                parts = [None] * 4
+                for k in range(BLOCKC):
+                    term = coef_ref[place, k] * jnp.broadcast_to(change[k : k + 1, lanes], (BLOCKC, XC))
+                    parts[k % 4] = term if parts[k % 4] is None else parts[k % 4] + term
+                total = total + ((parts[0] + parts[1]) + (parts[2] + parts[3]))
+            columns.append(jnp.maximum(total, 0.0))
+        updated = jnp.concatenate(columns, axis=1)
         if keep_ref is not None:
             updated = updated * keep_ref[rows, :]
-        high = updated.astype(BF16)
+        change = updated - value_ref[rows, :]
+        value_ref[rows, :] = updated
+        high, low = split_terms(updated)
         stacked_ref[rows, :] = high
-        stacked_ref[low_rows, :] = (updated - high.astype(F32)).astype(BF16)
-        if out_ref is not None:
-            out_ref[rows, :] = updated
+        stacked_ref[comps + place * BLOCKC : comps + (place + 1) * BLOCKC, :] = low
+        ready = following
 
 
 def movie_copies(movie_refs, movie_bufs, sems):
@@ -75,44 +110,52 @@
     return copies
 
 
-def prepare_kernel(pieces, *refs):
+def prepare_kernel(pieces, order_ref, *refs):
     trace_refs, movie_refs, refs = refs[:pieces], refs[pieces : 2 * pieces], refs[2 * pieces :]
-    fp_ref, support_ref, target_ref, keep_ref, gs_ref, scale_ref = refs[:6]
-    movie_bufs, sems = refs[6:-1], refs[-1]
+    fp_ref, support_ref, target_ref, keep_ref, start_ref, gs_ref, coef_ref, scale_ref = refs[:8]
+    sorted_fp, sorted_support, refs = refs[8], refs[9], refs[10:]
+    sorted_traces, movie_bufs, sems = refs[:pieces], refs[pieces : 2 * pieces], refs[2 * pieces]
     comps, share = target_ref.shape
     copies = movie_copies(movie_refs, movie_bufs, sems)
     for copy in copies:
         copy.start()
 
+    for place in range(comps // BLOCKC):
+        rows, source = rows_of(place), rows_from(order_ref, place)
+        sorted_fp[rows, :] = fp_ref[source, :]
+        sorted_support[rows, :] = support_ref[source, :].astype(F32)
+        for ref, sorted_ref in zip(trace_refs, sorted_traces):
+            sorted_ref[rows, :] = ref[source, :]
+
     me = lax.axis_index("tm")
     count = fp_ref.shape[1] // share
     first = me * share
     gram = None
-    for ref in trace_refs:
+    for ref in sorted_traces:
         part = lax.dot_general(ref[...], ref[...], BY_LAST, preferred_element_type=F32)
         gram = part if gram is None else gram + part
     eye, diagonal = diagonal_of(gram)
     inverse = 1.0 / (diagonal + 6.0 * smooth_weight)
-    split_rows(jnp.where(eye, 6.0 * smooth_weight * inverse, -gram * inverse), gs_ref)
+    store_system(jnp.where(eye, 6.0 * smooth_weight * inverse, -gram * inverse), gs_ref, coef_ref)
     scale_ref[...] = jnp.broadcast_to(smooth_weight * inverse, scale_ref.shape)
 
     lane = lax.broadcasted_iota(jnp.int32, (comps, XC), 1)
     column = lax.broadcasted_iota(jnp.int32, support_ref.shape, 1)
-    support = support_ref[...].astype(F32)
+    support = sorted_support[...]
 
     def row_at(offset):
         at = pl.multiple_of(first + offset, XC)
-        return fp_ref[:, pl.ds(at, XC)].astype(F32)
+        return sorted_fp[:, pl.ds(at, XC)].astype(F32)
 
     below = pl.multiple_of(jnp.maximum(first - XC, 0), XC)
     above = pl.multiple_of(jnp.minimum(first + share, fp_ref.shape[1] - XC), XC)
-    before = fp_ref[:, pl.ds(below, XC)].astype(F32) * jnp.where(me > 0, 1.0, 0.0)
+    before = sorted_fp[:, pl.ds(below, XC)].astype(F32) * jnp.where(me > 0, 1.0, 0.0)
     center = row_at(0)
     for offset in range(0, share, XC):
         if offset + XC < share:
             after = row_at(offset + XC)
         else:
-            after = fp_ref[:, pl.ds(above, XC)].astype(F32) * jnp.where(me < count - 1, 1.0, 0.0)
+            after = sorted_fp[:, pl.ds(above, XC)].astype(F32) * jnp.where(me < count - 1, 1.0, 0.0)
         left = jnp.where(lane == 0, 0.0, pltpu.roll(center, 1, 1))
         right = jnp.where(lane == XC - 1, 0.0, pltpu.roll(center, XC - 1, 1))
         beside = before + after + left + right
@@ -120,37 +163,40 @@
         target_ref[:, lanes] = smooth_weight * (6.0 * center - beside)
         here = me * (share // XC) + offset // XC
         kept = jnp.sum(jnp.where(column == here, support, 0.0), axis=1, keepdims=True)
-        keep_ref[:, lanes] = jnp.broadcast_to(kept, (comps, XC))
+        kept = jnp.broadcast_to(kept, (comps, XC))
+        keep_ref[:, lanes] = kept
+        start_ref[:, lanes] = center * kept
         before, center = center, after
 
     for copy in copies:
         copy.wait()
     correlation = None
-    for ref, buf in zip(trace_refs, movie_bufs):
+    for ref, buf in zip(sorted_traces, movie_bufs):
         part = lax.dot_general(ref[...], buf[...], BY_LAST, preferred_element_type=F32)
         correlation = part if correlation is None else correlation + part
     target_ref[...] = (correlation - target_ref[...]) * inverse
 
 
-def footprint_kernel(pieces, order_ref, target_ref, keep_ref, gs_ref, scale_ref, fp_ref, head_ref, tail_ref, *refs):
+def footprint_kernel(pieces, order_ref, target_ref, keep_ref, start_ref, gs_ref, coef_ref, scale_ref, head_ref, tail_ref, *refs):
     movie_refs, half_ref, joined_refs, refs = refs[:pieces], refs[pieces], refs[pieces + 1 : 2 * pieces + 1], refs[2 * pieces + 1 :]
-    goal_ref, stacked_ref, movie_bufs, sems = refs[0], refs[1], refs[2:-1], refs[-1]
+    goal_ref, value_ref, stacked_ref, movie_bufs, sems = refs[0], refs[1], refs[2], refs[3:-1], refs[-1]
     comps, share = target_ref.shape
     copies = movie_copies(movie_refs, movie_bufs, sems)
     for copy in copies:
         copy.start()
-    me = lax.axis_index("tm")
-    for offset in range(0, share, XC):
-        lanes = slice(offset, offset + XC)
-        sides = head_ref[:, lanes].astype(F32) + tail_ref[:, lanes].astype(F32)
-        goal_ref[:, lanes] = target_ref[:, lanes] + sides * scale_ref[...]
-        at = pl.multiple_of(me * share + offset, XC)
-        center = fp_ref[:, pl.ds(at, XC)].astype(F32)
-        stacked_ref[:comps, lanes] = (center * keep_ref[:, lanes]).astype(BF16)
+    value_ref[...] = start_ref[...]
+    stacked_ref[:comps, :] = start_ref[...].astype(BF16)
     stacked_ref[comps:, :] = jnp.zeros((comps, share), BF16)
-    sweep_steps(order_ref, gs_ref, goal_ref, stacked_ref, keep_ref)
+    for place in range(comps // BLOCKC):
+        rows, source = rows_of(place), rows_from(order_ref, place)
+        for offset in range(0, share, XC):
+            lanes = slice(offset, offset + XC)
+            sides = head_ref[source, lanes].astype(F32) + tail_ref[source, lanes].astype(F32)
+            goal_ref[rows, lanes] = target_ref[rows, lanes] + sides * scale_ref[rows, :]
+    sweep_steps(gs_ref, coef_ref, goal_ref, stacked_ref, value_ref, keep_ref)
     half = stacked_ref[:comps, :]
-    half_ref[...] = half
+    for place in range(comps // BLOCKC):
+        half_ref[rows_from(order_ref, place), :] = stacked_ref[rows_of(place), :]
     for copy in copies:
         copy.wait()
     cross = lax.dot_general(half, half, BY_LAST, preferred_element_type=F32)
@@ -169,7 +215,7 @@
 
 
 def trace_kernel(order_ref, traces_ref, *refs):
-    joined_refs, (out_ref, joined, goal_ref, gs_ref, stacked_ref) = refs[:-5], refs[-5:]
+    joined_refs, (out_ref, joined, goal_ref, gs_ref, coef_ref, stacked_ref, value_ref) = refs[:-7], refs[-7:]
     comps, frames = traces_ref.shape
     digit = lax.axis_index("vox") % GROUP
     for index, ref in enumerate(joined_refs):
@@ -179,11 +225,16 @@
     cross = joined[:, frames:]
     eye, diagonal = diagonal_of(cross)
     inverse = 1.0 / (diagonal + ridge_weight)
-    split_rows(jnp.where(eye, 0.0, -cross * inverse), gs_ref)
+    store_system(jnp.where(eye, 0.0, -cross * inverse), gs_ref, coef_ref)
     goal_ref[...] = joined[:, :frames] * inverse
-    stacked_ref[:comps, :] = traces_ref[...]
+    for place in range(comps // BLOCKC):
+        begin = traces_ref[rows_from(order_ref, place), :]
+        stacked_ref[rows_of(place), :] = begin
+        value_ref[rows_of(place), :] = begin.astype(F32)
     stacked_ref[comps:, :] = jnp.zeros((comps, frames), BF16)
-    sweep_steps(order_ref, gs_ref, goal_ref, stacked_ref, None, out_ref)
+    sweep_steps(gs_ref, coef_ref, goal_ref, stacked_ref, value_ref)
+    for place in range(comps // BLOCKC):
+        out_ref[rows_from(order_ref, place), :] = value_ref[rows_of(place), :]
 
 
 def swap(array):
@@ -224,8 +275,8 @@
     me = lax.axis_index("tm")
 
     own = lax.dynamic_slice_in_dim(footprints, me * share, share, 1)
-    head = lax.ppermute(own, "vox", [(i, i + 1) for i in range(planes - 1)])
-    tail = lax.ppermute(own, "vox", [(i + 1, i) for i in range(planes - 1)])
+    up = [(i, i + 1) for i in range(planes - 1)]
+    sides = [lax.ppermute(own, "vox", up), lax.ppermute(own, "vox", [(j, i) for i, j in up])]
     if cores == 2:
         movies = [movie, swap(movie)]
         all_traces = [traces, swap(traces)]
@@ -235,29 +286,35 @@
     pieces = len(movies)
     movie_scratch = [pltpu.VMEM((share, part.shape[1]), BF16) for part in movies] + [pltpu.SemaphoreType.DMA((pieces,))]
 
-    target, keep, system, scale = pl.pallas_call(
+    blocks = comps // BLOCKC
+    table = (blocks, BLOCKC, BLOCKC, XC)
+    target, keep, start, system, coef, scale = pl.pallas_call(
         functools.partial(prepare_kernel, pieces),
         out_shape=[
             shape_of((comps, share), F32),
             shape_of((comps, share), F32),
+            shape_of((comps, share), F32),
             shape_of((2 * comps, 2 * comps), BF16),
+            shape_of(table, F32),
             shape_of((comps, XC), F32),
         ],
-        in_specs=[VMEM] * pieces + [ANY] * pieces + [VMEM] * 2,
+        in_specs=[SMEM] + [VMEM] * pieces + [ANY] * pieces + [VMEM] * 2,
         compiler_params=SMALL,
-        out_specs=[VMEM] * 4,
-        scratch_shapes=movie_scratch,
-    )(*all_traces, *movies, footprints, support)
+        out_specs=[VMEM] * 6,
+        scratch_shapes=[pltpu.VMEM(footprints.shape, BF16), pltpu.VMEM(support.shape, F32)]
+        + [pltpu.VMEM(part.shape, BF16) for part in all_traces]
+        + movie_scratch,
+    )(block_order, *all_traces, *movies, footprints, support)
 
     half, *joined = pl.pallas_call(
         functools.partial(footprint_kernel, pieces),
         out_shape=[shape_of((comps, share), BF16)]
         + [shape_of((comps, part.shape[1] + comps), F32) for part in movies],
-        in_specs=[SMEM] + [VMEM] * 7 + [ANY] * pieces,
+        in_specs=[SMEM] + [VMEM] * 8 + [ANY] * pieces,
         compiler_params=SMALL,
         out_specs=[VMEM] * (pieces + 1),
-        scratch_shapes=[pltpu.VMEM((comps, share), F32), pltpu.VMEM((2 * comps, share), BF16)] + movie_scratch,
-    )(block_order, target, keep, system, scale, footprints, head, tail, *movies)
+        scratch_shapes=[pltpu.VMEM((comps, share), F32)] * 2 + [pltpu.VMEM((2 * comps, share), BF16)] + movie_scratch,
+    )(block_order, target, keep, start, system, coef, scale, *sides, *movies)
 
     if cores == 2:
         ours, theirs = joined[0], swap(joined[1])
@@ -286,7 +343,9 @@
             pltpu.VMEM((comps, frames + comps), F32),
             pltpu.VMEM((comps, frames), F32),
             pltpu.VMEM((2 * comps, 2 * comps), BF16),
+            pltpu.VMEM(table, F32),
             pltpu.VMEM((2 * comps, frames), BF16),
+            pltpu.VMEM((comps, frames), F32),
         ],
     )(block_order, traces, *joined)
     return (new_footprints, new_traces)

time: 58.8 us -> 55.1 us (0.937)
  Pallas kernels: 13.5 us -> 11.1 us
  waiting for transfers between devices: 18.7 us -> 16.7 us
  local copies, waits for them, and re-layouts: 5.33 us -> 5.97 us
    ppermute x2, waiting for transfers between devices: 4.95 us -> 2.93 us  [the longest x1 2.92 us: local(): lax.ppermute(own, 'vox', up)]
    pallas_call x1, Pallas kernels: 6.53 us -> 4.61 us  [local(): pl.pallas_call(functools.partial(footprint_kernel, pieces), out_shape=[sh...]
    pallas_call x1, Pallas kernels: 5.28 us -> 3.46 us  [local(): pl.pallas_call(trace_kernel, out_shape=shape_of((comps, frames), F32), in...]
    pallas_call x1, Pallas kernels: 1.61 us -> 2.98 us  [local(): pl.pallas_call(functools.partial(prepare_kernel, pieces), out_shape=[shap...]
    unnamed x15, local copies, waits for them, and re-layouts: 4.36 us -> 5 us
  transfers between devices with their start and end apart: 15 -> 15, of which waited for: 9 -> 9; matrix products, arithmetic and copies ran while one was open for 5% -> 5% of each run, Pallas kernels for 3% -> 5%
where the time goes in v3:
time: 55.1 us; the launch traced here: 54.8 us
  starting transfers between devices  19.3 us (35%)
  waiting for transfers between devices  16.7 us (30%)
  Pallas kernels  11.1 us (20%)
  local copies, waits for them, and re-layouts  5.97 us (11%)
  other arithmetic  0.97 us (2%)
  between operations  0.72 us (1%)
    ppermute x9, starting transfers between devices, from_group(): lax.ppermute(array, 'vox', [(i, i ^ k * stride) for i in range(count)])  12.1 us
    ppermute x9, waiting for transfers between devices, from_group(): lax.ppermute(array, 'vox', [(i, i ^ k * stride) for i in range(count)])  11.6 us
    ppermute x1, starting transfers between devices, local(): lax.ppermute(own, 'vox', up)  5.06 us
    unnamed x15, local copies, waits for them, and re-layouts  5 us
    pallas_call x1, Pallas kernels, local(): pl.pallas_call(functools.partial(footprint_kernel, pieces), out_shape=[sh...  4.61 us
    pallas_call x1, Pallas kernels, local(): pl.pallas_call(trace_kernel, out_shape=shape_of((comps, frames), F32), in...  3.46 us
    pallas_call x1, Pallas kernels, local(): pl.pallas_call(functools.partial(prepare_kernel, pieces), out_shape=[shap...  2.98 us
    ppermute x1, waiting for transfers between devices, local(): lax.ppermute(own, 'vox', up)  2.92 us
  transfers between devices with their start and end apart: 15, of which 9 were waited for; matrix products, arithmetic and copies ran while one was open for 5% of the time, Pallas kernels for 5%

profile of v3, /device:TPU:0, one launch (start us, length us, event | category | flops | bytes accessed | tf_op | source)
XLA Modules:
  0.0 54.8 jit_solution(13053685824122338204)
XLA Ops:
  0.6 0.5 collective-permute-start.1
  1.1 1.0 %constant_dynamic-slice_fusion = bf16[128,1024]{1,0:T(8,128)(2,1)S(1)} fusion(bf16[128,2048]{1,0:T(8,128)(2,1)} %refs_4_.1, s32[]{:T(128)S(6)} %select_n.12), kind=kLoop, calls=%fused_computation.3 | loop fusion | bytes 524292 | tf_op jit(solution)/shard_map/dynamic_slice | solution.py:277
  2.1 1.3 %collective-permute-start.3 = (bf16[128,1024]{1,0:T(8,128)(2,1)S(1)}, bf16[128,1024]{1,0:T(8,128)(2,1)S(1)}, u32[]{:S(2)}, u32[]{:S(2)}) collective-permute-start(bf16[128,1024]{1,0:T(8,128)(2,1)S(1)} %constant_dynamic-slice_fusion), channel_id=1, source_target_pairs={{2,0},{4,2},{6,4},{8,6},{10,8},{12,10},{14,12},{16,14},{18,16},{20... | collective-permute-start | bytes 786440 | tf_op jit(solution)/shard_map/ppermute | solution.py:279
  3.4 5.1 %collective-permute-start.2 = (bf16[128,1024]{1,0:T(8,128)(2,1)S(1)}, bf16[128,1024]{1,0:T(8,128)(2,1)S(1)}, u32[]{:S(2)}, u32[]{:S(2)}) collective-permute-start(bf16[128,1024]{1,0:T(8,128)(2,1)S(1)} %constant_dynamic-slice_fusion), channel_id=1, source_target_pairs={{0,2},{2,4},{4,6},{6,8},{8,10},{10,12},{12,14},{14,16},{16,18},{18... | collective-permute-start | bytes 786440 | tf_op jit(solution)/shard_map/ppermute | solution.py:279
  8.5 0.3 collective-permute-start
  8.8 0.8 %copy.7.refs_5_ = s32[128,16]{1,0:T(8,128)S(1)} copy(s32[128,16]{0,1:T(8,128)} %param.8) | data formatting | bytes 16384 | tf_op args[3]
  9.6 0.6 %collective-permute-done.refs_1_ = bf16[128,512]{1,0:T(8,128)(2,1)S(1)} collective-permute-done((bf16[128,512]{1,0:T(8,128)(2,1)}, bf16[128,512]{1,0:T(8,128)(2,1)S(1)}, u32[]{:S(2)}, u32[]{:S(2)}) %collective-permute-start) | collective-permute-done | bytes 131104 | tf_op jit(solution)/shard_map/ppermute | solution.py:241
  10.1 0.0 collective-permute-done.1.refs_3_.refs_1_
  10.1 0.0 copy-start
  10.1 1.6 %copy-done = bf16[2048,512]{1,0:T(8,128)(2,1)S(1)} copy-done((bf16[2048,512]{1,0:T(8,128)(2,1)S(1)}, bf16[2048,512]{1,0:T(8,128)(2,1)}, u32[]{:S(2)}) %copy-start) | copy-done | bytes 2097176
  11.7 0.0 copy-start.2
  11.7 1.0 %copy-done.2 = bf16[128,2048]{1,0:T(8,128)(2,1)S(1)} copy-done((bf16[128,2048]{1,0:T(8,128)(2,1)S(1)}, bf16[128,2048]{1,0:T(8,128)(2,1)}, u32[]{:S(2)}) %copy-start.2) | copy-done | bytes 524312
  12.7 0.0 copy-start.3
  12.8 0.9 %copy-done.3 = bf16[128,512]{1,0:T(8,128)(2,1)S(1)} copy-done((bf16[128,512]{1,0:T(8,128)(2,1)S(1)}, bf16[128,512]{1,0:T(8,128)(2,1)}, u32[]{:S(2)}) %copy-start.3) | copy-done | bytes 131096
  13.7 0.7 %copy-done.5 = s32[8]{0:T(128)S(1)} copy-done((s32[8]{0:T(128)S(1)}, s32[8]{0:T(128)}, u32[]{:S(2)}) %copy-start.5) | copy-done | bytes 56
  14.3 3.0 %shard_map.68 = (f32[128,1024]{1,0:T(8,128)S(1)}, f32[128,1024]{1,0:T(8,128)S(1)}, f32[128,1024]{1,0:T(8,128)S(1)}, bf16[256,256]{1,0:T(8,128)(2,1)S(1)}, f32[8,...) custom-call(s32[8]{0:T(128)S(1)} %copy-done.5, bf16[128,512]{1,0:T(8,128)(2,1)S(1)} %copy-done.3, ...), custom_call_target="tpu_custom_call" | custom-call | tf_op jit(solution)/shard_map/pallas_call | solution.py:291
  17.3 0.0 collective-permute-done.3.tail_ref
  17.3 2.9 %collective-permute-done.2.head_ref = bf16[128,1024]{1,0:T(8,128)(2,1)S(1)} collective-permute-done((bf16[128,1024]{1,0:T(8,128)(2,1)S(1)}, bf16[128,1024]{1,0:T(8,128)(2,1)S(1)}, u32[]{:S(2)}, u32[]{:S(2)}) %collective-permute-start.2) | collective-permute-done | bytes 262176 | tf_op jit(solution)/shard_map/ppermute | solution.py:279
  20.2 0.0 copy-done.1
  20.2 4.6 %shard_map.69 = (bf16[128,1024]{1,0:T(8,128)(2,1)S(1)}, f32[128,640]{1,0:T(8,128)S(1)}, f32[128,640]{1,0:T(8,128)S(1)}) custom-call(s32[8]{0:T(128)S(1)} %copy-done.5, f32[128,1024]{1,0:T(8,128)S(1)} %get-tuple-element.15.target_ref, f32[128,1024]{1,0:T(8,128)S(1)} %get-tuple-element.16.keep_ref, f32[128,1024]{1,0:T(8,128)S(1)} %get-tuple-element.17.start_ref, ...), custom_call_target="tpu_custom_call" | custom-call | tf_op jit(solution)/shard_map/pallas_call | solution.py:309
  24.9 0.0 copy-start.4
  24.9 0.0 copy-start.6
  24.9 0.1 collective-permute-start.5
  25.0 1.6 %collective-permute-done.5.theirs_ref = f32[128,640]{1,0:T(8,128)S(1)} collective-permute-done((f32[128,640]{1,0:T(8,128)S(1)}, f32[128,640]{1,0:T(8,128)S(1)}, u32[]{:S(2)}, u32[]{:S(2)}) %collective-permute-start.5) | collective-permute-done | bytes 327712 | tf_op jit(solution)/shard_map/ppermute | solution.py:241
  26.6 2.5 %collective-permute-start.6 = (f32[32,640]{1,0:T(8,128)S(1)}, f32[32,640]{1,0:T(8,128)S(1)}, u32[]{:S(2)}, u32[]{:S(2)}) collective-permute-start(f32[32,640]{1,0:T(8,128)S(1)} %get-tuple-element.25), channel_id=1, source_target_pairs={{0,2},{2,0},{4,6},{6,4},{8,10},{10,8},{12,14},{14,12},{16,18},{18,... | collective-permute-start | bytes 245768 | tf_op jit(solution)/shard_map/ppermute | solution.py:246
  29.1 0.0 collective-permute-start.7
  29.1 1.5 %collective-permute-start.8 = (f32[32,640]{1,0:T(8,128)S(1)}, f32[32,640]{1,0:T(8,128)S(1)}, u32[]{:S(2)}, u32[]{:S(2)}) collective-permute-start(f32[32,640]{1,0:T(8,128)S(1)} %get-tuple-element.27), channel_id=1, source_target_pairs={{0,6},{2,4},{4,2},{6,0},{8,14},{10,12},{12,10},{14,8},{16,22},{18,... | collective-permute-start | bytes 245768 | tf_op jit(solution)/shard_map/ppermute | solution.py:246
  30.7 1.2 %collective-permute-done.6 = f32[32,640]{1,0:T(8,128)S(1)} collective-permute-done((f32[32,640]{1,0:T(8,128)S(1)}, f32[32,640]{1,0:T(8,128)S(1)}, u32[]{:S(2)}, u32[]{:S(2)}) %collective-permute-start.6) | collective-permute-done | bytes 81952 | tf_op jit(solution)/shard_map/ppermute | solution.py:246
  31.9 3.2 %collective-permute-done.7 = f32[32,640]{1,0:T(8,128)S(1)} collective-permute-done((f32[32,640]{1,0:T(8,128)S(1)}, f32[32,640]{1,0:T(8,128)S(1)}, u32[]{:S(2)}, u32[]{:S(2)}) %collective-permute-start.7) | collective-permute-done | bytes 81952 | tf_op jit(solution)/shard_map/ppermute | solution.py:246
  35.1 0.0 collective-permute-done.8
  35.1 2.6 %collective-permute-start.11 = (f32[32,640]{1,0:T(8,128)S(1)}, f32[32,640]{1,0:T(8,128)S(1)}, u32[]{:S(2)}, u32[]{:S(2)}) collective-permute-start(f32[32,640]{1,0:T(8,128)S(1)} %add_add_fusion.1), channel_id=1, source_target_pairs={{0,24},{2,26},{4,28},{6,30},{8,16},{10,18},{12,20},{14,22},{16,8},... | collective-permute-start | bytes 245768 | tf_op jit(solution)/shard_map/ppermute | solution.py:246
  37.8 0.5 collective-permute-start.10
  38.3 1.3 %collective-permute-start.9 = (f32[32,640]{1,0:T(8,128)S(1)}, f32[32,640]{1,0:T(8,128)S(1)}, u32[]{:S(2)}, u32[]{:S(2)}) collective-permute-start(f32[32,640]{1,0:T(8,128)S(1)} %add_add_fusion.1), channel_id=1, source_target_pairs={{0,8},{2,10},{4,12},{6,14},{8,0},{10,2},{12,4},{14,6},{16,24},{18,... | collective-permute-start | bytes 245768 | tf_op jit(solution)/shard_map/ppermute | solution.py:246
  39.6 0.0 collective-permute-start.4
  39.6 2.7 %collective-permute-done.11 = f32[32,640]{1,0:T(8,128)S(1)} collective-permute-done((f32[32,640]{1,0:T(8,128)S(1)}, f32[32,640]{1,0:T(8,128)S(1)}, u32[]{:S(2)}, u32[]{:S(2)}) %collective-permute-start.11) | collective-permute-done | bytes 81952 | tf_op jit(solution)/shard_map/ppermute | solution.py:246
  42.3 2.1 %collective-permute-done.10 = f32[32,640]{1,0:T(8,128)S(1)} collective-permute-done((f32[32,640]{1,0:T(8,128)S(1)}, f32[32,640]{1,0:T(8,128)S(1)}, u32[]{:S(2)}, u32[]{:S(2)}) %collective-permute-start.10) | collective-permute-done | bytes 81952 | tf_op jit(solution)/shard_map/ppermute | solution.py:246
  44.4 0.0 collective-permute-done.9
  44.4 2.1 %collective-permute-start.14 = (f32[32,640]{1,0:T(8,128)S(1)}, f32[32,640]{1,0:T(8,128)S(1)}, u32[]{:S(2)}, u32[]{:S(2)}) collective-permute-start(f32[32,640]{1,0:T(8,128)S(1)} %add_add_fusion.refs_0_), channel_id=1, source_target_pairs={{0,6},{2,4},{4,2},{6,0},{8,14},{10,12},{12,10},{14,8},{16,22},{18,... | collective-permute-start | bytes 245768 | tf_op jit(solution)/shard_map/ppermute | solution.py:246
  46.6 0.0 collective-permute-start.13
  46.6 1.4 %collective-permute-start.12 = (f32[32,640]{1,0:T(8,128)S(1)}, f32[32,640]{1,0:T(8,128)S(1)}, u32[]{:S(2)}, u32[]{:S(2)}) collective-permute-start(f32[32,640]{1,0:T(8,128)S(1)} %add_add_fusion.refs_0_), channel_id=1, source_target_pairs={{0,2},{2,0},{4,6},{6,4},{8,10},{10,8},{12,14},{14,12},{16,18},{18,... | collective-permute-start | bytes 245768 | tf_op jit(solution)/shard_map/ppermute | solution.py:246
  48.0 0.0 collective-permute-done.4
  48.0 0.9 %maximum_select_fusion = bf16[128,2048]{1,0:T(8,128)(2,1)} fusion(bf16[128,1024]{1,0:T(8,128)(2,1)S(1)} %collective-permute-done.4, bf16[128,1024]{1,0:T(8,128)(2,1)S(1)} %get-tuple-element.21, pred[]{:T(512)S(6)} %eq.3), kind=kLoop, calls=%fused_computation | loop fusion | flops 2359296 | bytes 1048577 | tf_op jit(solution)/shard_map/jit(_where)/select_n | solution.py:322
  48.9 1.9 %collective-permute-done.14.refs_3_ = f32[32,640]{1,0:T(8,128)S(1)} collective-permute-done((f32[32,640]{1,0:T(8,128)S(1)}, f32[32,640]{1,0:T(8,128)S(1)}, u32[]{:S(2)}, u32[]{:S(2)}) %collective-permute-start.14) | collective-permute-done | bytes 81952 | tf_op jit(solution)/shard_map/ppermute | solution.py:246
  50.8 0.5 collective-permute-done.13.refs_2_
  51.3 0.0 collective-permute-done.12.refs_1_
  51.3 0.0 copy-done.4
  51.3 0.0 copy-done.6
  51.3 3.5 %shard_map.71 = f32[128,512]{1,0:T(8,128)} custom-call(s32[8]{0:T(128)S(1)} %copy-done.6, bf16[128,512]{1,0:T(8,128)(2,1)S(1)} %copy-done.4, f32[32,640]{1,0:T(8,128)S(1)} %add_add_fusion.refs_0_, f32[32,640]{1,0:T(8,128)S(1)} %collective-permute-done.12.refs_1_, f32[32,640]{1,0:T(8,128)S(1)} %collective-permute-done.13.refs_2_, ...), custom_call_target="tpu_custom_call" | custom-call | tf_op jit(solution)/shard_map/pallas_call | solution.py:336
  (5 shorter events, 0.1 us)
Async XLA Ops:
  0.6 9.5 %collective-permute-start.1 = (bf16[2048,512]{1,0:T(8,128)(2,1)}, bf16[2048,512]{1,0:T(8,128)(2,1)S(1)}, u32[]{:S(2)}, u32[]{:S(2)}) collective-permute-start(bf16[2048,512]{1,0:T(8,128)(2,1)} %refs_0_.3), channel_id=1, source_target_pairs={{0,1},{1,0},{2,3},{3,2},{4,5},{5,4},{6,7},{7,6},{8,9},{9,8},{10,11... | collective-permute-start | bytes 6291464 | tf_op jit(solution)/shard_map/ppermute | solution.py:241
  2.1 15.2 %collective-permute-start.3 = (bf16[128,1024]{1,0:T(8,128)(2,1)S(1)}, bf16[128,1024]{1,0:T(8,128)(2,1)S(1)}, u32[]{:S(2)}, u32[]{:S(2)}) collective-permute-start(bf16[128,1024]{1,0:T(8,128)(2,1)S(1)} %constant_dynamic-slice_fusion), channel_id=1, source_target_pairs={{2,0},{4,2},{6,4},{8,6},{10,8},{12,10},{14,12},{16,14},{18,16},{20... | collective-permute-start | bytes 786440 | tf_op jit(solution)/shard_map/ppermute | solution.py:279
  3.4 16.8 %collective-permute-start.2 = (bf16[128,1024]{1,0:T(8,128)(2,1)S(1)}, bf16[128,1024]{1,0:T(8,128)(2,1)S(1)}, u32[]{:S(2)}, u32[]{:S(2)}) collective-permute-start(bf16[128,1024]{1,0:T(8,128)(2,1)S(1)} %constant_dynamic-slice_fusion), channel_id=1, source_target_pairs={{0,2},{2,4},{4,6},{6,8},{8,10},{10,12},{12,14},{14,16},{16,18},{18... | collective-permute-start | bytes 786440 | tf_op jit(solution)/shard_map/ppermute | solution.py:279
  8.5 1.6 %collective-permute-start = (bf16[128,512]{1,0:T(8,128)(2,1)}, bf16[128,512]{1,0:T(8,128)(2,1)S(1)}, u32[]{:S(2)}, u32[]{:S(2)}) collective-permute-start(bf16[128,512]{1,0:T(8,128)(2,1)} %traces_ref.1), channel_id=1, source_target_pairs={{0,1},{1,0},{2,3},{3,2},{4,5},{5,4},{6,7},{7,6},{8,9},{9,8},{10,11... | collective-permute-start | bytes 393224 | tf_op jit(solution)/shard_map/ppermute | solution.py:241
  10.1 1.6 %copy-start = (bf16[2048,512]{1,0:T(8,128)(2,1)S(1)}, bf16[2048,512]{1,0:T(8,128)(2,1)}, u32[]{:S(2)}) copy-start(bf16[2048,512]{1,0:T(8,128)(2,1)} %refs_0_.3) | copy-start | bytes 6291460
  11.7 1.0 %copy-start.2 = (bf16[128,2048]{1,0:T(8,128)(2,1)S(1)}, bf16[128,2048]{1,0:T(8,128)(2,1)}, u32[]{:S(2)}) copy-start(bf16[128,2048]{1,0:T(8,128)(2,1)} %refs_4_.1) | copy-start | bytes 1572868
  12.7 0.9 %copy-start.3 = (bf16[128,512]{1,0:T(8,128)(2,1)S(1)}, bf16[128,512]{1,0:T(8,128)(2,1)}, u32[]{:S(2)}) copy-start(bf16[128,512]{1,0:T(8,128)(2,1)} %traces_ref.1) | copy-start | bytes 393220
  13.7 0.7 %copy-start.5 = (s32[8]{0:T(128)S(1)}, s32[8]{0:T(128)}, u32[]{:S(2)}) copy-start(s32[8]{0:T(128)} %order_ref.5) | copy-start | bytes 100
  14.3 5.9 %copy-start.1 = (bf16[2048,512]{1,0:T(8,128)(2,1)S(1)}, bf16[2048,512]{1,0:T(8,128)(2,1)}, u32[]{:S(2)}) copy-start(bf16[2048,512]{1,0:T(8,128)(2,1)} %refs_0_.3) | copy-start | bytes 6291460
  24.9 26.5 %copy-start.4 = (bf16[128,512]{1,0:T(8,128)(2,1)S(1)}, bf16[128,512]{1,0:T(8,128)(2,1)}, u32[]{:S(2)}) copy-start(bf16[128,512]{1,0:T(8,128)(2,1)} %traces_ref.1) | copy-start | bytes 393220
  24.9 26.5 %copy-start.6 = (s32[8]{0:T(128)S(1)}, s32[8]{0:T(128)}, u32[]{:S(2)}) copy-start(s32[8]{0:T(128)} %order_ref.5) | copy-start | bytes 100
  24.9 1.7 %collective-permute-start.5 = (f32[128,640]{1,0:T(8,128)S(1)}, f32[128,640]{1,0:T(8,128)S(1)}, u32[]{:S(2)}, u32[]{:S(2)}) collective-permute-start(f32[128,640]{1,0:T(8,128)S(1)} %get-tuple-element.23), channel_id=1, source_target_pairs={{0,1},{1,0},{2,3},{3,2},{4,5},{5,4},{6,7},{7,6},{8,9},{9,8},{10,11... | collective-permute-start | bytes 983048 | tf_op jit(solution)/shard_map/ppermute | solution.py:241
  26.6 5.3 %collective-permute-start.6 = (f32[32,640]{1,0:T(8,128)S(1)}, f32[32,640]{1,0:T(8,128)S(1)}, u32[]{:S(2)}, u32[]{:S(2)}) collective-permute-start(f32[32,640]{1,0:T(8,128)S(1)} %get-tuple-element.25), channel_id=1, source_target_pairs={{0,2},{2,0},{4,6},{6,4},{8,10},{10,8},{12,14},{14,12},{16,18},{18,... | collective-permute-start | bytes 245768 | tf_op jit(solution)/shard_map/ppermute | solution.py:246
  29.1 6.0 %collective-permute-start.7 = (f32[32,640]{1,0:T(8,128)S(1)}, f32[32,640]{1,0:T(8,128)S(1)}, u32[]{:S(2)}, u32[]{:S(2)}) collective-permute-start(f32[32,640]{1,0:T(8,128)S(1)} %get-tuple-element.26), channel_id=1, source_target_pairs={{0,4},{2,6},{4,0},{6,2},{8,12},{10,14},{12,8},{14,10},{16,20},{18,... | collective-permute-start | bytes 245768 | tf_op jit(solution)/shard_map/ppermute | solution.py:246
  29.1 6.0 %collective-permute-start.8 = (f32[32,640]{1,0:T(8,128)S(1)}, f32[32,640]{1,0:T(8,128)S(1)}, u32[]{:S(2)}, u32[]{:S(2)}) collective-permute-start(f32[32,640]{1,0:T(8,128)S(1)} %get-tuple-element.27), channel_id=1, source_target_pairs={{0,6},{2,4},{4,2},{6,0},{8,14},{10,12},{12,10},{14,8},{16,22},{18,... | collective-permute-start | bytes 245768 | tf_op jit(solution)/shard_map/ppermute | solution.py:246
  35.1 7.2 %collective-permute-start.11 = (f32[32,640]{1,0:T(8,128)S(1)}, f32[32,640]{1,0:T(8,128)S(1)}, u32[]{:S(2)}, u32[]{:S(2)}) collective-permute-start(f32[32,640]{1,0:T(8,128)S(1)} %add_add_fusion.1), channel_id=1, source_target_pairs={{0,24},{2,26},{4,28},{6,30},{8,16},{10,18},{12,20},{14,22},{16,8},... | collective-permute-start | bytes 245768 | tf_op jit(solution)/shard_map/ppermute | solution.py:246
  37.8 6.6 %collective-permute-start.10 = (f32[32,640]{1,0:T(8,128)S(1)}, f32[32,640]{1,0:T(8,128)S(1)}, u32[]{:S(2)}, u32[]{:S(2)}) collective-permute-start(f32[32,640]{1,0:T(8,128)S(1)} %add_add_fusion.1), channel_id=1, source_target_pairs={{0,16},{2,18},{4,20},{6,22},{8,24},{10,26},{12,28},{14,30},{16,0},... | collective-permute-start | bytes 245768 | tf_op jit(solution)/shard_map/ppermute | solution.py:246
  38.3 6.2 %collective-permute-start.9 = (f32[32,640]{1,0:T(8,128)S(1)}, f32[32,640]{1,0:T(8,128)S(1)}, u32[]{:S(2)}, u32[]{:S(2)}) collective-permute-start(f32[32,640]{1,0:T(8,128)S(1)} %add_add_fusion.1), channel_id=1, source_target_pairs={{0,8},{2,10},{4,12},{6,14},{8,0},{10,2},{12,4},{14,6},{16,24},{18,... | collective-permute-start | bytes 245768 | tf_op jit(solution)/shard_map/ppermute | solution.py:246
  39.6 8.4 %collective-permute-start.4 = (bf16[128,1024]{1,0:T(8,128)(2,1)S(1)}, bf16[128,1024]{1,0:T(8,128)(2,1)S(1)}, u32[]{:S(2)}, u32[]{:S(2)}) collective-permute-start(bf16[128,1024]{1,0:T(8,128)(2,1)S(1)} %get-tuple-element.21), channel_id=1, source_target_pairs={{0,1},{1,0},{2,3},{3,2},{4,5},{5,4},{6,7},{7,6},{8,9},{9,8},{10,11... | collective-permute-start | bytes 786440 | tf_op jit(solution)/shard_map/ppermute | solution.py:241
  44.4 6.3 %collective-permute-start.14 = (f32[32,640]{1,0:T(8,128)S(1)}, f32[32,640]{1,0:T(8,128)S(1)}, u32[]{:S(2)}, u32[]{:S(2)}) collective-permute-start(f32[32,640]{1,0:T(8,128)S(1)} %add_add_fusion.refs_0_), channel_id=1, source_target_pairs={{0,6},{2,4},{4,2},{6,0},{8,14},{10,12},{12,10},{14,8},{16,22},{18,... | collective-permute-start | bytes 245768 | tf_op jit(solution)/shard_map/ppermute | solution.py:246
  46.6 4.7 %collective-permute-start.13 = (f32[32,640]{1,0:T(8,128)S(1)}, f32[32,640]{1,0:T(8,128)S(1)}, u32[]{:S(2)}, u32[]{:S(2)}) collective-permute-start(f32[32,640]{1,0:T(8,128)S(1)} %add_add_fusion.refs_0_), channel_id=1, source_target_pairs={{0,4},{2,6},{4,0},{6,2},{8,12},{10,14},{12,8},{14,10},{16,20},{18,... | collective-permute-start | bytes 245768 | tf_op jit(solution)/shard_map/ppermute | solution.py:246
  46.6 4.7 %collective-permute-start.12 = (f32[32,640]{1,0:T(8,128)S(1)}, f32[32,640]{1,0:T(8,128)S(1)}, u32[]{:S(2)}, u32[]{:S(2)}) collective-permute-start(f32[32,640]{1,0:T(8,128)S(1)} %add_add_fusion.refs_0_), channel_id=1, source_target_pairs={{0,2},{2,0},{4,6},{6,4},{8,10},{10,8},{12,14},{14,12},{16,18},{18,... | collective-permute-start | bytes 245768 | tf_op jit(solution)/shard_map/ppermute | solution.py:246

commit v4 on v3

v4 whole, which is shorter than its diff:
```python
import functools

import jax
import jax.numpy as jnp
from jax import lax
from jax.experimental import pallas as pl
from jax.experimental.pallas import tpu as pltpu
from jax.sharding import PartitionSpec as P

BLOCKC = 16
XC = 128
INNER = 3
GROUP = 4
RELAYED = 64

smooth_weight = 256.0
ridge_weight = 2048.0

F32 = jnp.float32
BF16 = jnp.bfloat16
VMEM = pl.BlockSpec(memory_space=pltpu.VMEM)
SMEM = pl.BlockSpec(memory_space=pltpu.SMEM)
ANY = pl.BlockSpec(memory_space=pl.ANY)
SMALL = pltpu.CompilerParams(vmem_limit_bytes=14 * 1024 * 1024)
BY_LAST = (((1,), (1,)), ((), ()))


def shape_of(dims, dtype):
    return jax.ShapeDtypeStruct(dims, dtype)


def split_terms(array):
    high = array.astype(BF16)
    return high, (array - high.astype(F32)).astype(BF16)


def rows_of(place):
    return slice(place * BLOCKC, (place + 1) * BLOCKC)


def rows_from(order_ref, place):
    return pl.ds(pl.multiple_of(order_ref[place] * BLOCKC, BLOCKC), BLOCKC)


def diagonal_of(gram):
    row = lax.broadcasted_iota(jnp.int32, gram.shape, 0)
    col = lax.broadcasted_iota(jnp.int32, gram.shape, 1)
    eye = row == col
    return eye, jnp.sum(jnp.where(eye, gram, 0.0), axis=1, keepdims=True)


def store_system(system, gs_ref, coef_ref):
    comps = system.shape[0]
    blocks = comps // BLOCKC
    high, low = split_terms(system)
    for place in range(blocks):
        rows = rows_of(place)
        before = (place - 1) % blocks * BLOCKC
        for side in range(2):
            lanes = slice(side * comps, (side + 1) * comps)
            gs_ref[rows_of(2 * place), lanes] = high[rows]
            gs_ref[rows_of(2 * place + 1), lanes] = low[rows]
        for k in range(BLOCKC):
            coef_ref[place, k] = jnp.broadcast_to(system[rows, before + k : before + k + 1], (BLOCKC, XC))


def sweep_steps(gs_ref, coef_ref, goal_ref, stacked_ref, value_ref, keep_ref=None, finished=None):
    comps, width = goal_ref.shape
    blocks = comps // BLOCKC

    def product_of(place):
        pair = slice(2 * BLOCKC * place, 2 * BLOCKC * (place + 1))
        product = jnp.dot(gs_ref[pair, :], stacked_ref[...], preferred_element_type=F32)
        return product[:BLOCKC] + product[BLOCKC:]

    steps = INNER * blocks
    ready, change = product_of(0), None
    for step in range(steps):
        place = step % blocks
        rows = rows_of(place)
        following = product_of((step + 1) % blocks) if step + 1 < steps else None
        base = goal_ref[rows, :] + ready
        columns = []
        for lane in range(0, width, XC):
            lanes = slice(lane, lane + XC)
            total = base[:, lanes]
            if change is not None:
                parts = [None] * 4
                for k in range(BLOCKC):
                    term = coef_ref[place, k] * jnp.broadcast_to(change[k : k + 1, lanes], (BLOCKC, XC))
                    parts[k % 4] = term if parts[k % 4] is None else parts[k % 4] + term
                total = total + ((parts[0] + parts[1]) + (parts[2] + parts[3]))
            columns.append(jnp.maximum(total, 0.0))
        updated = jnp.concatenate(columns, axis=1)
        if keep_ref is not None:
            updated = updated * keep_ref[rows, :]
        change = updated - value_ref[rows, :]
        value_ref[rows, :] = updated
        if finished is not None and step >= steps - blocks:
            finished(place)
        high, low = split_terms(updated)
        stacked_ref[rows, :] = high
        stacked_ref[comps + place * BLOCKC : comps + (place + 1) * BLOCKC, :] = low
        ready = following


def movie_rows(ref, share):
    if ref.shape[0] == share:
        return ref[...]
    return ref[pl.ds(pl.multiple_of(lax.axis_index("tm") * share, share), share), :]


def load_kernel(order_ref, fp_ref, support_ref, traces_ref, movie_ref, sorted_fp, support_out, sorted_traces, movie_own, sems):
    share = movie_own.shape[0]
    blocks = sorted_fp.shape[0] // BLOCKC
    mine = pl.ds(pl.multiple_of(lax.axis_index("tm") * share, share), share)
    pairs = [(movie_ref.at[mine, :], movie_own), (support_ref, support_out)]
    for place in range(blocks):
        rows, source = rows_of(place), rows_from(order_ref, place)
        pairs.append((fp_ref.at[source, :], sorted_fp.at[rows, :]))
        pairs.append((traces_ref.at[source, :], sorted_traces.at[rows, :]))
    copies = [pltpu.make_async_copy(source, target, sems.at[index]) for index, (source, target) in enumerate(pairs)]
    for copy in copies:
        copy.start()
    for copy in copies:
        copy.wait()


def smooth_kernel(order_ref, sorted_fp, support_buf, smooth_ref, keep_ref, start_ref, sorted_support):
    comps, share = smooth_ref.shape
    blocks = comps // BLOCKC
    spread = jnp.concatenate([support_buf[...].astype(F32)] * (XC // support_buf.shape[0]), axis=0).T
    sorted_support[comps:, :] = spread
    for place in range(blocks):
        source = pl.ds(pl.multiple_of(comps + order_ref[place] * BLOCKC, BLOCKC), BLOCKC)
        sorted_support[rows_of(place), :] = sorted_support[source, :]

    me = lax.axis_index("tm")
    count = sorted_fp.shape[1] // share
    first = me * share
    lane = lax.broadcasted_iota(jnp.int32, (comps, XC), 1)
    support = sorted_support[:comps, :]

    def row_at(offset):
        at = pl.multiple_of(first + offset, XC)
        return sorted_fp[:, pl.ds(at, XC)].astype(F32)

    below = pl.multiple_of(jnp.maximum(first - XC, 0), XC)
    above = pl.multiple_of(jnp.minimum(first + share, sorted_fp.shape[1] - XC), XC)
    before = sorted_fp[:, pl.ds(below, XC)].astype(F32) * jnp.where(me > 0, 1.0, 0.0)
    center = row_at(0)
    for offset in range(0, share, XC):
        if offset + XC < share:
            after = row_at(offset + XC)
        else:
            after = sorted_fp[:, pl.ds(above, XC)].astype(F32) * jnp.where(me < count - 1, 1.0, 0.0)
        left = jnp.where(lane == 0, 0.0, pltpu.roll(center, 1, 1))
        right = jnp.where(lane == XC - 1, 0.0, pltpu.roll(center, XC - 1, 1))
        beside = before + after + left + right
        lanes = slice(offset, offset + XC)
        smooth_ref[:, lanes] = smooth_weight * (6.0 * center - beside)
        here = me * (share // XC) + offset // XC
        kept = jnp.sum(jnp.where(lane == here, support, 0.0), axis=1, keepdims=True)
        kept = jnp.broadcast_to(kept, (comps, XC))
        keep_ref[:, lanes] = kept
        start_ref[:, lanes] = center * kept
        before, center = center, after


def target_kernel(pieces, smooth_ref, *refs):
    trace_refs, movie_refs, refs = refs[:pieces], refs[pieces : 2 * pieces], refs[2 * pieces :]
    target_ref, gs_ref, coef_ref, scale_ref = refs
    share = target_ref.shape[1]
    gram = None
    for ref in trace_refs:
        part = lax.dot_general(ref[...], ref[...], BY_LAST, preferred_element_type=F32)
        gram = part if gram is None else gram + part
    eye, diagonal = diagonal_of(gram)
    inverse = 1.0 / (diagonal + 6.0 * smooth_weight)
    store_system(jnp.where(eye, 6.0 * smooth_weight * inverse, -gram * inverse), gs_ref, coef_ref)
    scale_ref[...] = jnp.broadcast_to(smooth_weight * inverse, scale_ref.shape)
    correlation = None
    for ref, movie_ref in zip(trace_refs, movie_refs):
        part = lax.dot_general(ref[...], movie_rows(movie_ref, share), BY_LAST, preferred_element_type=F32)
        correlation = part if correlation is None else correlation + part
    target_ref[...] = (correlation - smooth_ref[...]) * inverse


def footprint_kernel(sides, order_ref, target_ref, keep_ref, start_ref, gs_ref, coef_ref, scale_ref, *refs):
    side_refs, refs = refs[:sides], refs[sides:]
    movie_ref, half_ref, sorted_ref, joined_ref, goal_ref, value_ref, stacked_ref, sides_ref = refs
    comps, share = target_ref.shape
    value_ref[...] = start_ref[...]
    stacked_ref[:comps, :] = start_ref[...].astype(BF16)
    stacked_ref[comps:, :] = jnp.zeros((comps, share), BF16)
    relayed = side_refs[0].shape[0]
    sides_ref[:relayed, :] = side_refs[0][...].astype(F32) + side_refs[1][...].astype(F32)
    sides_ref[relayed:, :] = side_refs[2][...].astype(F32) + side_refs[3][...].astype(F32)
    for place in range(comps // BLOCKC):
        rows, source = rows_of(place), rows_from(order_ref, place)
        for offset in range(0, share, XC):
            lanes = slice(offset, offset + XC)
            goal_ref[rows, lanes] = target_ref[rows, lanes] + sides_ref[source, lanes] * scale_ref[rows, :]
    sweep_steps(gs_ref, coef_ref, goal_ref, stacked_ref, value_ref, keep_ref)
    half = stacked_ref[:comps, :]
    sorted_ref[...] = half
    for place in range(comps // BLOCKC):
        half_ref[rows_from(order_ref, place), :] = stacked_ref[rows_of(place), :]
    store_products(half, movie_ref, joined_ref)


def store_products(half, movie_ref, joined_ref):
    frames = movie_ref.shape[1]
    joined_ref[:, :frames] = jnp.dot(half, movie_rows(movie_ref, half.shape[1]), preferred_element_type=F32)
    joined_ref[:, frames:] = lax.dot_general(half, half, BY_LAST, preferred_element_type=F32)


def product_kernel(half_ref, movie_ref, joined_ref):
    store_products(half_ref[...], movie_ref, joined_ref)


def chunk_kernel(stride, ours_ref, theirs_ref, *out_refs):
    rows = out_refs[0].shape[0]
    digit = lax.axis_index("vox") // stride % GROUP
    for index, out_ref in enumerate(out_refs):
        at = pl.ds(pl.multiple_of((digit ^ index) * rows, rows), rows)
        out_ref[...] = ours_ref[at, :] + theirs_ref[at, :]


def trace_kernel(order_ref, traces_ref, *refs):
    joined_refs, (out_ref, joined, goal_ref, gs_ref, coef_ref, stacked_ref, value_ref, sems) = refs[:-8], refs[-8:]
    comps, frames = traces_ref.shape
    digit = lax.axis_index("vox") % GROUP
    for index, ref in enumerate(joined_refs):
        rows = ref.shape[0]
        place = pl.multiple_of((digit ^ index) * rows, rows) if rows < comps else 0
        joined[pl.ds(place, rows), :] = ref[...]
    cross = joined[:, frames:]
    eye, diagonal = diagonal_of(cross)
    inverse = 1.0 / (diagonal + ridge_weight)
    store_system(jnp.where(eye, 0.0, -cross * inverse), gs_ref, coef_ref)
    goal_ref[...] = joined[:, :frames] * inverse
    stacked_ref[:comps, :] = traces_ref[...]
    value_ref[...] = traces_ref[...].astype(F32)
    stacked_ref[comps:, :] = jnp.zeros((comps, frames), BF16)
    copies = [
        pltpu.make_async_copy(value_ref.at[rows_of(place), :], out_ref.at[rows_from(order_ref, place), :], sems.at[place])
        for place in range(comps // BLOCKC)
    ]
    sweep_steps(gs_ref, coef_ref, goal_ref, stacked_ref, value_ref, None, lambda place: copies[place].start())
    for copy in copies:
        copy.wait()


def in_hbm(array):
    return pltpu.with_memory_space_constraint(array, pltpu.HBM)


def swap(array):
    return lax.ppermute(array, "tm", [(0, 1), (1, 0)])


def from_group(arrays, stride):
    count = lax.axis_size("vox")
    return [lax.ppermute(array, "vox", [(i, i ^ (k * stride)) for i in range(count)]) for k, array in arrays]


def tree_sum(own, others):
    return (own + others[0]) + (others[1] + others[2])


def sum_over_vox(ours, theirs):
    comps, width = ours.shape
    rows = comps // GROUP
    top = lax.axis_size("vox") // GROUP
    chunks = pl.pallas_call(
        functools.partial(chunk_kernel, 1),
        out_shape=[shape_of((rows, width), F32)] * GROUP,
        in_specs=[VMEM] * 2,
        compiler_params=SMALL,
        out_specs=[VMEM] * GROUP,
    )(ours, theirs)
    mine = tree_sum(chunks[0], from_group([(k, chunks[k]) for k in range(1, GROUP)], 1))
    mine = tree_sum(mine, from_group([(k, mine) for k in range(1, GROUP)], top))
    return [mine] + from_group([(k, mine) for k in range(1, GROUP)], 1)


def local(movie, footprints, traces, support, block_order):
    comps, vox_local = footprints.shape
    frames = traces.shape[1]
    cores = lax.axis_size("tm")
    planes = lax.axis_size("vox")
    share = vox_local // cores
    me = lax.axis_index("tm")

    own = lax.dynamic_slice_in_dim(footprints, me * share, share, 1)
    pairs = [(i, i ^ 1) for i in range(planes)]
    across = [(i, i + 1) for i in range(1, planes - 1, 2)] + [(i + 1, i) for i in range(1, planes - 1, 2)]
    onward = [(i, i + 2) for i in range(0, planes - 2, 2)] + [(i, i - 2) for i in range(3, planes, 2)]
    relayed, direct = lax.optimization_barrier((own[:RELAYED], own[RELAYED:]))
    beside_relayed = lax.ppermute(relayed, "vox", pairs)
    across_direct = lax.ppermute(direct, "vox", across)
    beside_direct = lax.ppermute(direct, "vox", pairs)
    blocks = comps // BLOCKC
    sorted_fp, support_rows, sorted_traces, movie_own = pl.pallas_call(
        load_kernel,
        out_shape=[
            shape_of(footprints.shape, BF16),
            shape_of(support.shape[::-1], jnp.int32),
            shape_of(traces.shape, BF16),
            shape_of((share, frames), BF16),
        ],
        in_specs=[SMEM] + [ANY] * 4,
        compiler_params=SMALL,
        out_specs=[VMEM] * 4,
        scratch_shapes=[pltpu.SemaphoreType.DMA((2 * blocks + 2,))],
    )(*[in_hbm(array) for array in (block_order, footprints, support.T, traces, movie)])
    sides = [beside_relayed, lax.ppermute(beside_relayed, "vox", onward), beside_direct, across_direct]

    smooth, keep, start = pl.pallas_call(
        smooth_kernel,
        out_shape=[shape_of((comps, share), F32)] * 3,
        in_specs=[SMEM] + [VMEM] * 2,
        compiler_params=SMALL,
        out_specs=[VMEM] * 3,
        scratch_shapes=[pltpu.VMEM((2 * comps, XC), F32)],
    )(in_hbm(block_order), sorted_fp, support_rows)

    if cores == 2:
        movies = [movie_own, swap(movie)]
        all_traces = [sorted_traces, swap(sorted_traces)]
    else:
        movies = [lax.all_to_all(movie, "tm", 0, 1, tiled=True)]
        all_traces = [lax.all_gather(sorted_traces, "tm", axis=1, tiled=True)]
    pieces = len(movies)
    table = (blocks, BLOCKC, BLOCKC, XC)
    target, system, coef, scale = pl.pallas_call(
        functools.partial(target_kernel, pieces),
        out_shape=[
            shape_of((comps, share), F32),
            shape_of((2 * comps, 2 * comps), BF16),
            shape_of(table, F32),
            shape_of((comps, XC), F32),
        ],
        in_specs=[VMEM] * (2 * pieces + 1),
        compiler_params=SMALL,
        out_specs=[VMEM] * 4,
    )(smooth, *all_traces, *movies)

    half, sorted_half, joined = pl.pallas_call(
        functools.partial(footprint_kernel, len(sides)),
        out_shape=[shape_of((comps, share), BF16)] * 2 + [shape_of((comps, movies[-1].shape[1] + comps), F32)],
        in_specs=[SMEM] + [VMEM] * (7 + len(sides)),
        compiler_params=SMALL,
        out_specs=[VMEM] * 3,
        scratch_shapes=[pltpu.VMEM((comps, share), F32)] * 2
        + [pltpu.VMEM((2 * comps, share), BF16), pltpu.VMEM((comps, share), F32)],
    )(block_order, target, keep, start, system, coef, scale, *sides, movies[-1])

    if cores == 2:
        theirs = swap(joined)
        ours = pl.pallas_call(
            product_kernel,
            out_shape=shape_of((comps, frames + comps), F32),
            in_specs=[VMEM] * 2,
            compiler_params=SMALL,
            out_specs=VMEM,
        )(sorted_half, movies[0])
        other = swap(half)
        new_footprints = jnp.where(
            me == 0, jnp.concatenate([half, other], axis=1), jnp.concatenate([other, half], axis=1)
        )
    else:
        projection = lax.psum_scatter(joined[:, : frames * cores], "tm", scatter_dimension=1, tiled=True)
        ours = jnp.concatenate([projection, lax.psum(joined[:, frames * cores :], "tm")], axis=1)
        theirs = jnp.zeros_like(ours)
        new_footprints = lax.all_gather(half, "tm", axis=1, tiled=True)

    if planes == GROUP * GROUP:
        joined = sum_over_vox(ours, theirs)
    else:
        joined = [lax.psum(ours + theirs, "vox")]
    new_traces = pl.pallas_call(
        trace_kernel,
        out_shape=shape_of((comps, frames), F32),
        in_specs=[SMEM] + [VMEM] * (len(joined) + 1),
        compiler_params=SMALL,
        out_specs=ANY,
        scratch_shapes=[
            pltpu.VMEM((comps, frames + comps), F32),
            pltpu.VMEM((comps, frames), F32),
            pltpu.VMEM((2 * comps, 2 * comps), BF16),
            pltpu.VMEM(table, F32),
            pltpu.VMEM((2 * comps, frames), BF16),
            pltpu.VMEM((comps, frames), F32),
            pltpu.SemaphoreType.DMA((blocks,)),
        ],
    )(block_order, sorted_traces, *joined)
    return (new_footprints, new_traces)


def solution(mesh):
    placed = (P("vox", "tm"), P(None, "vox"), P(None, "tm"), P(None, "vox"), P())
    return jax.shard_map(
        local,
        mesh=mesh,
        in_specs=placed,
        out_specs=(P(None, "vox"), P(None, "tm")),
        check_vma=False,
    )
```

time: 55.1 us -> 53.3 us (0.967)
  local copies, waits for them, and re-layouts: 5.97 us -> 0.99 us
  starting transfers between devices: 19.3 us -> 23.5 us
  waiting for transfers between devices: 16.7 us -> 14.6 us
  Pallas kernels: 11.1 us -> 12.3 us
    unnamed x15 -> x2, local copies, waits for them, and re-layouts: 5 us -> 0.01 us
    ppermute x2 -> x4, starting transfers between devices: 6.35 us -> 10.9 us  [the longest x1 4.29 us: local(): beside_direct = lax.ppermute(direct, 'vox', pairs)]
    ppermute x2 -> x4, waiting for transfers between devices: 2.93 us -> 0.7 us  [the longest x1 0.69 us: local(): beside_direct = lax.ppermute(direct, 'vox', pairs)]
    pallas_call x2 -> x5, Pallas kernels: 7.59 us -> 8.9 us  [the longest x1 4.09 us: local(): pl.pallas_call(functools.partial(footprint_kernel, len(sides)), out_shape...]
    slice x0 -> x1, local copies, waits for them, and re-layouts: none -> 0.98 us  [local(): relayed, direct = lax.optimization_barrier((own[:RELAYED], own[RELAYED:]))]
    ppermute x9, waiting for transfers between devices: 11.6 us -> 12.6 us  [from_group(): lax.ppermute(array, 'vox', [(i, i ^ k * stride) for i in range(count)])]
    dynamic_slice x1 -> x0, local copies, waits for them, and re-layouts: 0.97 us -> none  [local(): own = lax.dynamic_slice_in_dim(footprints, me * share, share, 1)]
    ppermute x4, waiting for transfers between devices: 2.15 us -> 1.24 us  [swap(): return lax.ppermute(array, 'tm', [(0, 1), (1, 0)])]
  transfers between devices with their start and end apart: 15 -> 17, of which waited for: 9 -> 10; matrix products, arithmetic and copies ran while one was open for 5% -> 4% of each run, Pallas kernels for 5% -> 9%
where the time goes in v4:
time: 53.3 us; the launch traced here: 53.1 us
  starting transfers between devices  23.5 us (44%)
  waiting for transfers between devices  14.6 us (27%)
  Pallas kernels  12.3 us (23%)
  local copies, waits for them, and re-layouts  0.99 us (2%)
  other arithmetic  0.96 us (2%)
  between operations  0.75 us (1%)
    ppermute x9, waiting for transfers between devices, from_group(): lax.ppermute(array, 'vox', [(i, i ^ k * stride) for i in range(count)])  12.6 us
    ppermute x9, starting transfers between devices, from_group(): lax.ppermute(array, 'vox', [(i, i ^ k * stride) for i in range(count)])  11.7 us
    ppermute x1, starting transfers between devices, local(): beside_direct = lax.ppermute(direct, 'vox', pairs)  4.29 us
    pallas_call x1, Pallas kernels, local(): pl.pallas_call(functools.partial(footprint_kernel, len(sides)), out_shape...  4.09 us
    ppermute x1, starting transfers between devices, local(): lax.ppermute(beside_relayed, 'vox', onward)  3.42 us
    pallas_call x1, Pallas kernels, local(): pl.pallas_call(trace_kernel, out_shape=shape_of((comps, frames), F32), in...  3.41 us
    ppermute x1, starting transfers between devices, local(): beside_relayed = lax.ppermute(relayed, 'vox', pairs)  2.58 us
    pallas_call x1, Pallas kernels, local(): pl.pallas_call(load_kernel, out_shape=[shape_of(footprints.shape, BF16),...  2.21 us
  transfers between devices with their start and end apart: 17, of which 10 were waited for; matrix products, arithmetic and copies ran while one was open for 4% of the time, Pallas kernels for 9%

profile of v4, /device:TPU:0, one launch (start us, length us, event | category | flops | bytes accessed | tf_op | source)
XLA Modules:
  0.0 53.1 jit_solution(17409869352929065049)
XLA Ops:
  0.6 0.5 collective-permute-start.1
  1.1 1.0 %fusion = (bf16[64,1024]{1,0:T(8,128)(2,1)S(1)}, bf16[64,1024]{1,0:T(8,128)(2,1)S(1)}) fusion(bf16[128,2048]{1,0:T(8,128)(2,1)} %fp_ref.1, s32[]{:T(128)S(6)} %add.28, s32[]{:T(128)S(6)} %select_n.12), kind=kLoop, calls=%fused_computation.4 | loop fusion | bytes 524296 | tf_op jit(solution)/shard_map/slice | solution.py:300
  2.1 2.6 %collective-permute-start.2 = (bf16[64,1024]{1,0:T(8,128)(2,1)S(1)}, bf16[64,1024]{1,0:T(8,128)(2,1)S(1)}, u32[]{:S(2)}, u32[]{:S(2)}) collective-permute-start(bf16[64,1024]{1,0:T(8,128)(2,1)S(1)} %get-tuple-element.33), channel_id=1, source_target_pairs={{0,2},{2,0},{4,6},{6,4},{8,10},{10,8},{12,14},{14,12},{16,18},{18,... | collective-permute-start | bytes 393224 | tf_op jit(solution)/shard_map/ppermute | solution.py:301
  4.7 2.2 %shard_map.68 = (bf16[128,2048]{1,0:T(8,128)(2,1)S(1)}, s32[16,128]{1,0:T(8,128)S(1)}, bf16[128,512]{1,0:T(8,128)(2,1)S(1)}, bf16[1024,512]{1,0:T(8,128)(2,1)S(1)}) custom-call(s32[8]{0:T(128)} %order_ref.7, bf16[128,2048]{1,0:T(8,128)(2,1)} %fp_ref.1, s32[16,128]{1,0:T(8,128)} %bitcast.1, bf16[128,512]{1,0:T(8,128)(2,1)} %traces_ref.1, ...), custom_call_target="tpu_custom_call" | custom-call | tf_op jit(solution)/shard_map/pallas_call | solution.py:305
  6.9 0.3 collective-permute-start
  7.2 0.7 %collective-permute-start.5 = (bf16[64,1024]{1,0:T(8,128)(2,1)S(1)}, bf16[64,1024]{1,0:T(8,128)(2,1)S(1)}, u32[]{:S(2)}, u32[]{:S(2)}) collective-permute-start(bf16[64,1024]{1,0:T(8,128)(2,1)S(1)} %get-tuple-element.34), channel_id=1, source_target_pairs={{2,4},{6,8},{10,12},{14,16},{18,20},{22,24},{26,28},{4,2},{8,6},{1... | collective-permute-start | bytes 393224 | tf_op jit(solution)/shard_map/ppermute | solution.py:302
  7.9 4.3 %collective-permute-start.4 = (bf16[64,1024]{1,0:T(8,128)(2,1)S(1)}, bf16[64,1024]{1,0:T(8,128)(2,1)S(1)}, u32[]{:S(2)}, u32[]{:S(2)}) collective-permute-start(bf16[64,1024]{1,0:T(8,128)(2,1)S(1)} %get-tuple-element.34), channel_id=1, source_target_pairs={{0,2},{2,0},{4,6},{6,4},{8,10},{10,8},{12,14},{14,12},{16,18},{18,... | collective-permute-start | bytes 393224 | tf_op jit(solution)/shard_map/ppermute | solution.py:303
  12.1 0.0 collective-permute-done.2.refs_0_
  12.2 3.4 %collective-permute-start.3 = (bf16[64,1024]{1,0:T(8,128)(2,1)S(1)}, bf16[64,1024]{1,0:T(8,128)(2,1)S(1)}, u32[]{:S(2)}, u32[]{:S(2)}) collective-permute-start(bf16[64,1024]{1,0:T(8,128)(2,1)S(1)} %collective-permute-done.2.refs_0_), channel_id=1, source_target_pairs={{0,4},{4,8},{8,12},{12,16},{16,20},{20,24},{24,28},{6,2},{10,6},{1... | collective-permute-start | bytes 393224 | tf_op jit(solution)/shard_map/ppermute | solution.py:318
  15.6 1.2 %shard_map.69 = (f32[128,1024]{1,0:T(8,128)S(1)}, f32[128,1024]{1,0:T(8,128)S(1)}, f32[128,1024]{1,0:T(8,128)S(1)}) custom-call(s32[8]{0:T(128)} %order_ref.7, bf16[128,2048]{1,0:T(8,128)(2,1)S(1)} %get-tuple-element.22.sorted_fp, s32[16,128]{1,0:T(8,128)S(1)} %get-tuple-element.23.support_buf), custom_call_target="tpu_custom_call" | custom-call | tf_op jit(solution)/shard_map/pallas_call | solution.py:320
  16.8 0.0 copy-start
  16.8 0.0 collective-permute-done.refs_1_
  16.8 0.0 collective-permute-done.1.refs_3_.refs_4_
  16.8 1.0 %shard_map.70 = (f32[128,1024]{1,0:T(8,128)S(1)}, bf16[256,256]{1,0:T(8,128)(2,1)S(1)}, f32[8,16,16,128]{3,2,1,0:T(8,128)S(1)}, f32[128,128]{1,0:T(8,128)S(1)}) custom-call(f32[128,1024]{1,0:T(8,128)S(1)} %get-tuple-element.24.smooth_ref, bf16[128,512]{1,0:T(8,128)(2,1)S(1)} %get-tuple-element.25.refs_0_.traces_ref, ...), custom_call_target="tpu_custom_call" | custom-call | tf_op jit(solution)/shard_map/pallas_call | solution.py:337
  17.8 0.0 collective-permute-done.5.refs_3_
  17.9 0.7 %collective-permute-done.4.refs_2_ = bf16[64,1024]{1,0:T(8,128)(2,1)S(1)} collective-permute-done((bf16[64,1024]{1,0:T(8,128)(2,1)S(1)}, bf16[64,1024]{1,0:T(8,128)(2,1)S(1)}, u32[]{:S(2)}, u32[]{:S(2)}) %collective-permute-start.4) | collective-permute-done | bytes 131104 | tf_op jit(solution)/shard_map/ppermute | solution.py:303
  18.6 0.0 collective-permute-done.3.refs_1_
  18.6 0.0 copy-done
  18.6 4.1 %shard_map.71 = (bf16[128,1024]{1,0:T(8,128)(2,1)S(1)}, bf16[128,1024]{1,0:T(8,128)(2,1)S(1)}, f32[128,640]{1,0:T(8,128)S(1)}) custom-call(s32[8]{0:T(128)S(1)} %copy-done, f32[128,1024]{1,0:T(8,128)S(1)} %get-tuple-element.27.target_ref, f32[128,1024]{1,0:T(8,128)S(1)} %get-tuple-element.28.keep_ref, f32[128,1024]{1,0:T(8,128)S(1)} %get-tuple-element.29.start_ref, ...), custom_call_target="tpu_custom_call" | custom-call | tf_op jit(solution)/shard_map/pallas_call | solution.py:350
  22.7 0.1 collective-permute-start.7
  22.7 0.4 shard_map.72.ours_ref
  23.1 1.2 %collective-permute-done.7.theirs_ref = f32[128,640]{1,0:T(8,128)S(1)} collective-permute-done((f32[128,640]{1,0:T(8,128)S(1)}, f32[128,640]{1,0:T(8,128)S(1)}, u32[]{:S(2)}, u32[]{:S(2)}) %collective-permute-start.7) | collective-permute-done | bytes 327712 | tf_op jit(solution)/shard_map/ppermute | solution.py:260
  24.4 1.5 %collective-permute-start.8 = (f32[32,640]{1,0:T(8,128)S(1)}, f32[32,640]{1,0:T(8,128)S(1)}, u32[]{:S(2)}, u32[]{:S(2)}) collective-permute-start(f32[32,640]{1,0:T(8,128)S(1)} %get-tuple-element.39), channel_id=1, source_target_pairs={{0,2},{2,0},{4,6},{6,4},{8,10},{10,8},{12,14},{14,12},{16,18},{18,... | collective-permute-start | bytes 245768 | tf_op jit(solution)/shard_map/ppermute | solution.py:265
  25.9 1.9 %collective-permute-start.9 = (f32[32,640]{1,0:T(8,128)S(1)}, f32[32,640]{1,0:T(8,128)S(1)}, u32[]{:S(2)}, u32[]{:S(2)}) collective-permute-start(f32[32,640]{1,0:T(8,128)S(1)} %get-tuple-element.40), channel_id=1, source_target_pairs={{0,4},{2,6},{4,0},{6,2},{8,12},{10,14},{12,8},{14,10},{16,20},{18,... | collective-permute-start | bytes 245768 | tf_op jit(solution)/shard_map/ppermute | solution.py:265
  27.8 0.3 collective-permute-start.10
  28.1 0.9 %collective-permute-done.8 = f32[32,640]{1,0:T(8,128)S(1)} collective-permute-done((f32[32,640]{1,0:T(8,128)S(1)}, f32[32,640]{1,0:T(8,128)S(1)}, u32[]{:S(2)}, u32[]{:S(2)}) %collective-permute-start.8) | collective-permute-done | bytes 81952 | tf_op jit(solution)/shard_map/ppermute | solution.py:265
  28.9 2.4 %collective-permute-done.9 = f32[32,640]{1,0:T(8,128)S(1)} collective-permute-done((f32[32,640]{1,0:T(8,128)S(1)}, f32[32,640]{1,0:T(8,128)S(1)}, u32[]{:S(2)}, u32[]{:S(2)}) %collective-permute-start.9) | collective-permute-done | bytes 81952 | tf_op jit(solution)/shard_map/ppermute | solution.py:265
  31.3 1.8 %collective-permute-done.10 = f32[32,640]{1,0:T(8,128)S(1)} collective-permute-done((f32[32,640]{1,0:T(8,128)S(1)}, f32[32,640]{1,0:T(8,128)S(1)}, u32[]{:S(2)}, u32[]{:S(2)}) %collective-permute-start.10) | collective-permute-done | bytes 81952 | tf_op jit(solution)/shard_map/ppermute | solution.py:265
  33.2 2.8 %collective-permute-start.13 = (f32[32,640]{1,0:T(8,128)S(1)}, f32[32,640]{1,0:T(8,128)S(1)}, u32[]{:S(2)}, u32[]{:S(2)}) collective-permute-start(f32[32,640]{1,0:T(8,128)S(1)} %add_add_fusion.1), channel_id=1, source_target_pairs={{0,24},{2,26},{4,28},{6,30},{8,16},{10,18},{12,20},{14,22},{16,8},... | collective-permute-start | bytes 245768 | tf_op jit(solution)/shard_map/ppermute | solution.py:265
  36.0 0.3 collective-permute-start.12
  36.3 1.3 %collective-permute-start.11 = (f32[32,640]{1,0:T(8,128)S(1)}, f32[32,640]{1,0:T(8,128)S(1)}, u32[]{:S(2)}, u32[]{:S(2)}) collective-permute-start(f32[32,640]{1,0:T(8,128)S(1)} %add_add_fusion.1), channel_id=1, source_target_pairs={{0,8},{2,10},{4,12},{6,14},{8,0},{10,2},{12,4},{14,6},{16,24},{18,... | collective-permute-start | bytes 245768 | tf_op jit(solution)/shard_map/ppermute | solution.py:265
  37.6 0.0 collective-permute-start.6
  37.6 2.6 %collective-permute-done.13 = f32[32,640]{1,0:T(8,128)S(1)} collective-permute-done((f32[32,640]{1,0:T(8,128)S(1)}, f32[32,640]{1,0:T(8,128)S(1)}, u32[]{:S(2)}, u32[]{:S(2)}) %collective-permute-start.13) | collective-permute-done | bytes 81952 | tf_op jit(solution)/shard_map/ppermute | solution.py:265
  40.2 2.5 %collective-permute-done.12 = f32[32,640]{1,0:T(8,128)S(1)} collective-permute-done((f32[32,640]{1,0:T(8,128)S(1)}, f32[32,640]{1,0:T(8,128)S(1)}, u32[]{:S(2)}, u32[]{:S(2)}) %collective-permute-start.12) | collective-permute-done | bytes 81952 | tf_op jit(solution)/shard_map/ppermute | solution.py:265
  42.7 0.0 collective-permute-done.11
  42.8 1.7 %collective-permute-start.16 = (f32[32,640]{1,0:T(8,128)S(1)}, f32[32,640]{1,0:T(8,128)S(1)}, u32[]{:S(2)}, u32[]{:S(2)}) collective-permute-start(f32[32,640]{1,0:T(8,128)S(1)} %add_add_fusion.refs_0_), channel_id=1, source_target_pairs={{0,6},{2,4},{4,2},{6,0},{8,14},{10,12},{12,10},{14,8},{16,22},{18,... | collective-permute-start | bytes 245768 | tf_op jit(solution)/shard_map/ppermute | solution.py:265
  44.5 0.7 %collective-permute-start.15 = (f32[32,640]{1,0:T(8,128)S(1)}, f32[32,640]{1,0:T(8,128)S(1)}, u32[]{:S(2)}, u32[]{:S(2)}) collective-permute-start(f32[32,640]{1,0:T(8,128)S(1)} %add_add_fusion.refs_0_), channel_id=1, source_target_pairs={{0,4},{2,6},{4,0},{6,2},{8,12},{10,14},{12,8},{14,10},{16,20},{18,... | collective-permute-start | bytes 245768 | tf_op jit(solution)/shard_map/ppermute | solution.py:265
  45.2 1.1 %collective-permute-start.14 = (f32[32,640]{1,0:T(8,128)S(1)}, f32[32,640]{1,0:T(8,128)S(1)}, u32[]{:S(2)}, u32[]{:S(2)}) collective-permute-start(f32[32,640]{1,0:T(8,128)S(1)} %add_add_fusion.refs_0_), channel_id=1, source_target_pairs={{0,2},{2,0},{4,6},{6,4},{8,10},{10,8},{12,14},{14,12},{16,18},{18,... | collective-permute-start | bytes 245768 | tf_op jit(solution)/shard_map/ppermute | solution.py:265
  46.3 0.0 collective-permute-done.6
  46.3 0.9 %maximum_select_fusion = bf16[128,2048]{1,0:T(8,128)(2,1)} fusion(bf16[128,1024]{1,0:T(8,128)(2,1)S(1)} %collective-permute-done.6, bf16[128,1024]{1,0:T(8,128)(2,1)S(1)} %get-tuple-element.35, pred[]{:T(512)S(6)} %eq.3), kind=kLoop, calls=%fused_computation | loop fusion | flops 2359296 | bytes 1048577 | tf_op jit(solution)/shard_map/jit(_where)/select_n | solution.py:370
  47.2 1.8 %collective-permute-done.16.refs_3_ = f32[32,640]{1,0:T(8,128)S(1)} collective-permute-done((f32[32,640]{1,0:T(8,128)S(1)}, f32[32,640]{1,0:T(8,128)S(1)}, u32[]{:S(2)}, u32[]{:S(2)}) %collective-permute-start.16) | collective-permute-done | bytes 81952 | tf_op jit(solution)/shard_map/ppermute | solution.py:265
  49.0 0.4 collective-permute-done.15.refs_2_
  49.4 0.2 collective-permute-done.14.refs_1_
  49.7 3.4 %shard_map.74 = f32[128,512]{1,0:T(8,128)} custom-call(s32[8]{0:T(128)S(1)} %copy-done, bf16[128,512]{1,0:T(8,128)(2,1)S(1)} %get-tuple-element.25.refs_0_.traces_ref, f32[32,640]{1,0:T(8,128)S(1)} %add_add_fusion.refs_0_, f32[32,640]{1,0:T(8,128)S(1)} %collective-permute-done.14.refs_1_, f32[32,640]{1,0:T(8,128)S(1)} %collective-permute-done.15.refs_2_, ...), custom_call_target="tpu_custom_call" | custom-call | tf_op jit(solution)/shard_map/pallas_call | solution.py:383
  (3 shorter events, 0.1 us)
Async XLA Ops:
  0.6 16.2 %collective-permute-start.1 = (bf16[2048,512]{1,0:T(8,128)(2,1)}, bf16[2048,512]{1,0:T(8,128)(2,1)S(1)}, u32[]{:S(2)}, u32[]{:S(2)}) collective-permute-start(bf16[2048,512]{1,0:T(8,128)(2,1)} %movie_ref.1), channel_id=1, source_target_pairs={{0,1},{1,0},{2,3},{3,2},{4,5},{5,4},{6,7},{7,6},{8,9},{9,8},{10,11... | collective-permute-start | bytes 6291464 | tf_op jit(solution)/shard_map/ppermute | solution.py:260
  2.1 10.0 %collective-permute-start.2 = (bf16[64,1024]{1,0:T(8,128)(2,1)S(1)}, bf16[64,1024]{1,0:T(8,128)(2,1)S(1)}, u32[]{:S(2)}, u32[]{:S(2)}) collective-permute-start(bf16[64,1024]{1,0:T(8,128)(2,1)S(1)} %get-tuple-element.33), channel_id=1, source_target_pairs={{0,2},{2,0},{4,6},{6,4},{8,10},{10,8},{12,14},{14,12},{16,18},{18,... | collective-permute-start | bytes 393224 | tf_op jit(solution)/shard_map/ppermute | solution.py:301
  6.9 9.9 %collective-permute-start = (bf16[128,512]{1,0:T(8,128)(2,1)S(1)}, bf16[128,512]{1,0:T(8,128)(2,1)S(1)}, u32[]{:S(2)}, u32[]{:S(2)}) collective-permute-start(bf16[128,512]{1,0:T(8,128)(2,1)S(1)} %get-tuple-element.25.refs_0_.traces_ref), channel_id=1, source_target_pairs={{0,1},{1,0},{2,3},{3,2},{4,5},{5,4},{6,7},{7,6},{8,9},{9,8},{10,11... | collective-permute-start | bytes 393224 | tf_op jit(solution)/shard_map/ppermute | solution.py:260
  7.2 10.7 %collective-permute-start.5 = (bf16[64,1024]{1,0:T(8,128)(2,1)S(1)}, bf16[64,1024]{1,0:T(8,128)(2,1)S(1)}, u32[]{:S(2)}, u32[]{:S(2)}) collective-permute-start(bf16[64,1024]{1,0:T(8,128)(2,1)S(1)} %get-tuple-element.34), channel_id=1, source_target_pairs={{2,4},{6,8},{10,12},{14,16},{18,20},{22,24},{26,28},{4,2},{8,6},{1... | collective-permute-start | bytes 393224 | tf_op jit(solution)/shard_map/ppermute | solution.py:302
  7.9 10.7 %collective-permute-start.4 = (bf16[64,1024]{1,0:T(8,128)(2,1)S(1)}, bf16[64,1024]{1,0:T(8,128)(2,1)S(1)}, u32[]{:S(2)}, u32[]{:S(2)}) collective-permute-start(bf16[64,1024]{1,0:T(8,128)(2,1)S(1)} %get-tuple-element.34), channel_id=1, source_target_pairs={{0,2},{2,0},{4,6},{6,4},{8,10},{10,8},{12,14},{14,12},{16,18},{18,... | collective-permute-start | bytes 393224 | tf_op jit(solution)/shard_map/ppermute | solution.py:303
  12.2 6.4 %collective-permute-start.3 = (bf16[64,1024]{1,0:T(8,128)(2,1)S(1)}, bf16[64,1024]{1,0:T(8,128)(2,1)S(1)}, u32[]{:S(2)}, u32[]{:S(2)}) collective-permute-start(bf16[64,1024]{1,0:T(8,128)(2,1)S(1)} %collective-permute-done.2.refs_0_), channel_id=1, source_target_pairs={{0,4},{4,8},{8,12},{12,16},{16,20},{20,24},{24,28},{6,2},{10,6},{1... | collective-permute-start | bytes 393224 | tf_op jit(solution)/shard_map/ppermute | solution.py:318
  16.8 1.7 %copy-start = (s32[8]{0:T(128)S(1)}, s32[8]{0:T(128)}, u32[]{:S(2)}) copy-start(s32[8]{0:T(128)} %order_ref.7) | copy-start | bytes 100
  22.7 1.7 %collective-permute-start.7 = (f32[128,640]{1,0:T(8,128)S(1)}, f32[128,640]{1,0:T(8,128)S(1)}, u32[]{:S(2)}, u32[]{:S(2)}) collective-permute-start(f32[128,640]{1,0:T(8,128)S(1)} %get-tuple-element.37), channel_id=1, source_target_pairs={{0,1},{1,0},{2,3},{3,2},{4,5},{5,4},{6,7},{7,6},{8,9},{9,8},{10,11... | collective-permute-start | bytes 983048 | tf_op jit(solution)/shard_map/ppermute | solution.py:260
  24.4 4.6 %collective-permute-start.8 = (f32[32,640]{1,0:T(8,128)S(1)}, f32[32,640]{1,0:T(8,128)S(1)}, u32[]{:S(2)}, u32[]{:S(2)}) collective-permute-start(f32[32,640]{1,0:T(8,128)S(1)} %get-tuple-element.39), channel_id=1, source_target_pairs={{0,2},{2,0},{4,6},{6,4},{8,10},{10,8},{12,14},{14,12},{16,18},{18,... | collective-permute-start | bytes 245768 | tf_op jit(solution)/shard_map/ppermute | solution.py:265
  25.9 5.5 %collective-permute-start.9 = (f32[32,640]{1,0:T(8,128)S(1)}, f32[32,640]{1,0:T(8,128)S(1)}, u32[]{:S(2)}, u32[]{:S(2)}) collective-permute-start(f32[32,640]{1,0:T(8,128)S(1)} %get-tuple-element.40), channel_id=1, source_target_pairs={{0,4},{2,6},{4,0},{6,2},{8,12},{10,14},{12,8},{14,10},{16,20},{18,... | collective-permute-start | bytes 245768 | tf_op jit(solution)/shard_map/ppermute | solution.py:265
  27.8 5.3 %collective-permute-start.10 = (f32[32,640]{1,0:T(8,128)S(1)}, f32[32,640]{1,0:T(8,128)S(1)}, u32[]{:S(2)}, u32[]{:S(2)}) collective-permute-start(f32[32,640]{1,0:T(8,128)S(1)} %get-tuple-element.41), channel_id=1, source_target_pairs={{0,6},{2,4},{4,2},{6,0},{8,14},{10,12},{12,10},{14,8},{16,22},{18,... | collective-permute-start | bytes 245768 | tf_op jit(solution)/shard_map/ppermute | solution.py:265
  33.2 7.0 %collective-permute-start.13 = (f32[32,640]{1,0:T(8,128)S(1)}, f32[32,640]{1,0:T(8,128)S(1)}, u32[]{:S(2)}, u32[]{:S(2)}) collective-permute-start(f32[32,640]{1,0:T(8,128)S(1)} %add_add_fusion.1), channel_id=1, source_target_pairs={{0,24},{2,26},{4,28},{6,30},{8,16},{10,18},{12,20},{14,22},{16,8},... | collective-permute-start | bytes 245768 | tf_op jit(solution)/shard_map/ppermute | solution.py:265
  36.0 6.8 %collective-permute-start.12 = (f32[32,640]{1,0:T(8,128)S(1)}, f32[32,640]{1,0:T(8,128)S(1)}, u32[]{:S(2)}, u32[]{:S(2)}) collective-permute-start(f32[32,640]{1,0:T(8,128)S(1)} %add_add_fusion.1), channel_id=1, source_target_pairs={{0,16},{2,18},{4,20},{6,22},{8,24},{10,26},{12,28},{14,30},{16,0},... | collective-permute-start | bytes 245768 | tf_op jit(solution)/shard_map/ppermute | solution.py:265
  36.3 6.5 %collective-permute-start.11 = (f32[32,640]{1,0:T(8,128)S(1)}, f32[32,640]{1,0:T(8,128)S(1)}, u32[]{:S(2)}, u32[]{:S(2)}) collective-permute-start(f32[32,640]{1,0:T(8,128)S(1)} %add_add_fusion.1), channel_id=1, source_target_pairs={{0,8},{2,10},{4,12},{6,14},{8,0},{10,2},{12,4},{14,6},{16,24},{18,... | collective-permute-start | bytes 245768 | tf_op jit(solution)/shard_map/ppermute | solution.py:265
  37.6 8.7 %collective-permute-start.6 = (bf16[128,1024]{1,0:T(8,128)(2,1)S(1)}, bf16[128,1024]{1,0:T(8,128)(2,1)S(1)}, u32[]{:S(2)}, u32[]{:S(2)}) collective-permute-start(bf16[128,1024]{1,0:T(8,128)(2,1)S(1)} %get-tuple-element.35), channel_id=1, source_target_pairs={{0,1},{1,0},{2,3},{3,2},{4,5},{5,4},{6,7},{7,6},{8,9},{9,8},{10,11... | collective-permute-start | bytes 786440 | tf_op jit(solution)/shard_map/ppermute | solution.py:260
  42.8 6.3 %collective-permute-start.16 = (f32[32,640]{1,0:T(8,128)S(1)}, f32[32,640]{1,0:T(8,128)S(1)}, u32[]{:S(2)}, u32[]{:S(2)}) collective-permute-start(f32[32,640]{1,0:T(8,128)S(1)} %add_add_fusion.refs_0_), channel_id=1, source_target_pairs={{0,6},{2,4},{4,2},{6,0},{8,14},{10,12},{12,10},{14,8},{16,22},{18,... | collective-permute-start | bytes 245768 | tf_op jit(solution)/shard_map/ppermute | solution.py:265
  44.5 4.9 %collective-permute-start.15 = (f32[32,640]{1,0:T(8,128)S(1)}, f32[32,640]{1,0:T(8,128)S(1)}, u32[]{:S(2)}, u32[]{:S(2)}) collective-permute-start(f32[32,640]{1,0:T(8,128)S(1)} %add_add_fusion.refs_0_), channel_id=1, source_target_pairs={{0,4},{2,6},{4,0},{6,2},{8,12},{10,14},{12,8},{14,10},{16,20},{18,... | collective-permute-start | bytes 245768 | tf_op jit(solution)/shard_map/ppermute | solution.py:265
  45.2 4.4 %collective-permute-start.14 = (f32[32,640]{1,0:T(8,128)S(1)}, f32[32,640]{1,0:T(8,128)S(1)}, u32[]{:S(2)}, u32[]{:S(2)}) collective-permute-start(f32[32,640]{1,0:T(8,128)S(1)} %add_add_fusion.refs_0_), channel_id=1, source_target_pairs={{0,2},{2,0},{4,6},{6,4},{8,10},{10,8},{12,14},{14,12},{16,18},{18,... | collective-permute-start | bytes 245768 | tf_op jit(solution)/shard_map/ppermute | solution.py:265

commit v5 on v4

--- a/solution.py
+++ b/solution.py
@@ -110,19 +110,32 @@
     return ref[pl.ds(pl.multiple_of(lax.axis_index("tm") * share, share), share), :]
 
 
-def load_kernel(order_ref, fp_ref, support_ref, traces_ref, movie_ref, sorted_fp, support_out, sorted_traces, movie_own, sems):
+def load_kernel(order_hbm, fp_ref, support_ref, traces_ref, movie_ref, relayed, direct, sorted_fp, support_out, sorted_traces, movie_own, order_ref, sems):
     share = movie_own.shape[0]
+    cut = relayed.shape[0]
     blocks = sorted_fp.shape[0] // BLOCKC
     mine = pl.ds(pl.multiple_of(lax.axis_index("tm") * share, share), share)
-    pairs = [(movie_ref.at[mine, :], movie_own), (support_ref, support_out)]
+    order_copy = pltpu.make_async_copy(order_hbm, order_ref, sems.at[0])
+    order_copy.start()
+    pairs = [
+        (fp_ref.at[:cut, mine], relayed),
+        (fp_ref.at[cut:, mine], direct),
+        (support_ref, support_out),
+        (movie_ref.at[mine, :], movie_own),
+    ]
+    copies = [pltpu.make_async_copy(source, target, sems.at[1 + index]) for index, (source, target) in enumerate(pairs)]
+    for copy in copies:
+        copy.start()
+    order_copy.wait()
+    pairs = []
     for place in range(blocks):
         rows, source = rows_of(place), rows_from(order_ref, place)
         pairs.append((fp_ref.at[source, :], sorted_fp.at[rows, :]))
         pairs.append((traces_ref.at[source, :], sorted_traces.at[rows, :]))
-    copies = [pltpu.make_async_copy(source, target, sems.at[index]) for index, (source, target) in enumerate(pairs)]
-    for copy in copies:
+    later = [pltpu.make_async_copy(source, target, sems.at[5 + index]) for index, (source, target) in enumerate(pairs)]
+    for copy in later:
         copy.start()
-    for copy in copies:
+    for copy in copies + later:
         copy.wait()
 
 
@@ -233,7 +246,8 @@
     digit = lax.axis_index("vox") % GROUP
     for index, ref in enumerate(joined_refs):
         rows = ref.shape[0]
-        place = pl.multiple_of((digit ^ index) * rows, rows) if rows < comps else 0
+        step = (GROUP - index) % GROUP
+        place = pl.multiple_of((digit ^ step) * rows, rows) if rows < comps else 0
         joined[pl.ds(place, rows), :] = ref[...]
     cross = joined[:, frames:]
     eye, diagonal = diagonal_of(cross)
@@ -266,7 +280,7 @@
 
 
 def tree_sum(own, others):
-    return (own + others[0]) + (others[1] + others[2])
+    return (others[1] + others[2]) + (own + others[0])
 
 
 def sum_over_vox(ours, theirs):
@@ -282,7 +296,7 @@
     )(ours, theirs)
     mine = tree_sum(chunks[0], from_group([(k, chunks[k]) for k in range(1, GROUP)], 1))
     mine = tree_sum(mine, from_group([(k, mine) for k in range(1, GROUP)], top))
-    return [mine] + from_group([(k, mine) for k in range(1, GROUP)], 1)
+    return [mine] + from_group([(k, mine) for k in range(1, GROUP)], 1)[::-1]
 
 
 def local(movie, footprints, traces, support, block_order):
@@ -293,28 +307,28 @@
     share = vox_local // cores
     me = lax.axis_index("tm")
 
-    own = lax.dynamic_slice_in_dim(footprints, me * share, share, 1)
     pairs = [(i, i ^ 1) for i in range(planes)]
     across = [(i, i + 1) for i in range(1, planes - 1, 2)] + [(i + 1, i) for i in range(1, planes - 1, 2)]
     onward = [(i, i + 2) for i in range(0, planes - 2, 2)] + [(i, i - 2) for i in range(3, planes, 2)]
-    relayed, direct = lax.optimization_barrier((own[:RELAYED], own[RELAYED:]))
-    beside_relayed = lax.ppermute(relayed, "vox", pairs)
-    across_direct = lax.ppermute(direct, "vox", across)
-    beside_direct = lax.ppermute(direct, "vox", pairs)
     blocks = comps // BLOCKC
-    sorted_fp, support_rows, sorted_traces, movie_own = pl.pallas_call(
+    relayed, direct, sorted_fp, support_rows, sorted_traces, movie_own = pl.pallas_call(
         load_kernel,
         out_shape=[
+            shape_of((RELAYED, share), BF16),
+            shape_of((comps - RELAYED, share), BF16),
             shape_of(footprints.shape, BF16),
             shape_of(support.shape[::-1], jnp.int32),
             shape_of(traces.shape, BF16),
             shape_of((share, frames), BF16),
         ],
-        in_specs=[SMEM] + [ANY] * 4,
-        compiler_params=SMALL,
-        out_specs=[VMEM] * 4,
-        scratch_shapes=[pltpu.SemaphoreType.DMA((2 * blocks + 2,))],
+        in_specs=[ANY] * 5,
+        compiler_params=SMALL,
+        out_specs=[VMEM] * 6,
+        scratch_shapes=[pltpu.SMEM(block_order.shape, jnp.int32), pltpu.SemaphoreType.DMA((2 * blocks + 5,))],
     )(*[in_hbm(array) for array in (block_order, footprints, support.T, traces, movie)])
+    beside_relayed = lax.ppermute(relayed, "vox", pairs)
+    across_direct = lax.ppermute(direct, "vox", across)
+    beside_direct = lax.ppermute(direct, "vox", pairs)
     sides = [beside_relayed, lax.ppermute(beside_relayed, "vox", onward), beside_direct, across_direct]
 
     smooth, keep, start = pl.pallas_call(

time: 53.3 us -> 52.5 us (0.985)
  waiting for transfers between devices: 14.6 us -> 17.2 us
  starting transfers between devices: 23.5 us -> 21.2 us
  local copies, waits for them, and re-layouts: 0.99 us -> 0.01 us
    ppermute x1, starting transfers between devices: 4.29 us -> 0.36 us  [local(): beside_direct = lax.ppermute(direct, 'vox', pairs)]
    ppermute x1, waiting for transfers between devices: 0.01 us -> 3.12 us  [local(): beside_relayed = lax.ppermute(relayed, 'vox', pairs)]
    ppermute x9, starting transfers between devices: 11.7 us -> 12.9 us  [from_group(): lax.ppermute(array, 'vox', [(i, i ^ k * stride) for i in range(count)])]
    ppermute x1, waiting for transfers between devices: 0.01 us -> 1.04 us  [local(): lax.ppermute(beside_relayed, 'vox', onward)]
    slice x1 -> x0, local copies, waits for them, and re-layouts: 0.98 us -> none  [local(): relayed, direct = lax.optimization_barrier((own[:RELAYED], own[RELAYED:]))]
    ppermute x9, waiting for transfers between devices: 12.6 us -> 11.8 us  [from_group(): lax.ppermute(array, 'vox', [(i, i ^ k * stride) for i in range(count)])]
    ppermute x1, waiting for transfers between devices: 0.69 us -> 0.01 us  [local(): beside_direct = lax.ppermute(direct, 'vox', pairs)]
  transfers between devices with their start and end apart: 17 -> 17, of which waited for: 10 -> 11; matrix products, arithmetic and copies ran while one was open for 4% -> 2% of each run, Pallas kernels for 9% -> 9%
where the time goes in v5:
time: 52.5 us; the launch traced here: 52.3 us
  starting transfers between devices  21.2 us (40%)
  waiting for transfers between devices  17.2 us (33%)
  Pallas kernels  12.2 us (23%)
  other arithmetic  0.97 us (2%)
  between operations  0.75 us (1%)
    ppermute x9, starting transfers between devices, from_group(): lax.ppermute(array, 'vox', [(i, i ^ k * stride) for i in range(count)])  12.9 us
    ppermute x9, waiting for transfers between devices, from_group(): lax.ppermute(array, 'vox', [(i, i ^ k * stride) for i in range(count)])  11.8 us
    pallas_call x1, Pallas kernels, local(): pl.pallas_call(functools.partial(footprint_kernel, len(sides)), out_shape...  4.12 us
    ppermute x1, starting transfers between devices, local(): lax.ppermute(beside_relayed, 'vox', onward)  3.87 us
    pallas_call x1, Pallas kernels, local(): pl.pallas_call(trace_kernel, out_shape=shape_of((comps, frames), F32), in...  3.41 us
    ppermute x1, waiting for transfers between devices, local(): beside_relayed = lax.ppermute(relayed, 'vox', pairs)  3.12 us
    ppermute x1, starting transfers between devices, local(): beside_relayed = lax.ppermute(relayed, 'vox', pairs)  2.57 us
    pallas_call x1, Pallas kernels, local(): pl.pallas_call(load_kernel, out_shape=[shape_of((RELAYED, share), BF16),...  2.02 us
  transfers between devices with their start and end apart: 17, of which 11 were waited for; matrix products, arithmetic and copies ran while one was open for 2% of the time, Pallas kernels for 9%

profile of v5, /device:TPU:0, one launch (start us, length us, event | category | flops | bytes accessed | tf_op | source)
XLA Modules:
  0.0 52.3 jit_solution(11662720038573300060)
XLA Ops:
  0.6 0.5 collective-permute-start.1
  1.1 2.0 %shard_map.68 = (bf16[64,1024]{1,0:T(8,128)(2,1)S(1)}, bf16[64,1024]{1,0:T(8,128)(2,1)S(1)}, bf16[128,2048]{1,0:T(8,128)(2,1)S(1)}, s32[16,128]{1,0:T(8,128)S(1)...) custom-call(s32[8]{0:T(128)} %order_ref.5, bf16[128,2048]{1,0:T(8,128)(2,1)} %fp_ref.1, s32[16,128]{1,0:T(8,128)} %bitcast.1, ...), custom_call_target="tpu_custom_call" | custom-call | tf_op jit(solution)/shard_map/pallas_call | solution.py:314
  3.2 2.6 %collective-permute-start.2 = (bf16[64,1024]{1,0:T(8,128)(2,1)S(1)}, bf16[64,1024]{1,0:T(8,128)(2,1)S(1)}, u32[]{:S(2)}, u32[]{:S(2)}) collective-permute-start(bf16[64,1024]{1,0:T(8,128)(2,1)S(1)} %get-tuple-element.33), channel_id=1, source_target_pairs={{0,2},{2,0},{4,6},{6,4},{8,10},{10,8},{12,14},{14,12},{16,18},{18,... | collective-permute-start | bytes 393224 | tf_op jit(solution)/shard_map/ppermute | solution.py:329
  5.7 0.2 collective-permute-start
  6.0 0.4 collective-permute-start.4
  6.3 0.7 %collective-permute-start.5 = (bf16[64,1024]{1,0:T(8,128)(2,1)S(1)}, bf16[64,1024]{1,0:T(8,128)(2,1)S(1)}, u32[]{:S(2)}, u32[]{:S(2)}) collective-permute-start(bf16[64,1024]{1,0:T(8,128)(2,1)S(1)} %get-tuple-element.34), channel_id=1, source_target_pairs={{2,4},{6,8},{10,12},{14,16},{18,20},{22,24},{26,28},{4,2},{8,6},{1... | collective-permute-start | bytes 393224 | tf_op jit(solution)/shard_map/ppermute | solution.py:330
  7.0 3.1 %collective-permute-done.2.refs_0_ = bf16[64,1024]{1,0:T(8,128)(2,1)S(1)} collective-permute-done((bf16[64,1024]{1,0:T(8,128)(2,1)S(1)}, bf16[64,1024]{1,0:T(8,128)(2,1)S(1)}, u32[]{:S(2)}, u32[]{:S(2)}) %collective-permute-start.2) | collective-permute-done | bytes 131104 | tf_op jit(solution)/shard_map/ppermute | solution.py:329
  10.1 3.9 %collective-permute-start.3 = (bf16[64,1024]{1,0:T(8,128)(2,1)S(1)}, bf16[64,1024]{1,0:T(8,128)(2,1)S(1)}, u32[]{:S(2)}, u32[]{:S(2)}) collective-permute-start(bf16[64,1024]{1,0:T(8,128)(2,1)S(1)} %collective-permute-done.2.refs_0_), channel_id=1, source_target_pairs={{0,4},{4,8},{8,12},{12,16},{16,20},{20,24},{24,28},{6,2},{10,6},{1... | collective-permute-start | bytes 393224 | tf_op jit(solution)/shard_map/ppermute | solution.py:332
  14.0 1.2 %shard_map.69 = (f32[128,1024]{1,0:T(8,128)S(1)}, f32[128,1024]{1,0:T(8,128)S(1)}, f32[128,1024]{1,0:T(8,128)S(1)}) custom-call(s32[8]{0:T(128)} %order_ref.5, bf16[128,2048]{1,0:T(8,128)(2,1)S(1)} %get-tuple-element.22.sorted_fp, s32[16,128]{1,0:T(8,128)S(1)} %get-tuple-element.23.support_buf), custom_call_target="tpu_custom_call" | custom-call | tf_op jit(solution)/shard_map/pallas_call | solution.py:334
  15.2 0.0 copy-start
  15.2 0.0 collective-permute-done.refs_1_
  15.2 0.0 collective-permute-done.1.refs_3_.refs_4_
  15.2 1.0 %shard_map.70 = (f32[128,1024]{1,0:T(8,128)S(1)}, bf16[256,256]{1,0:T(8,128)(2,1)S(1)}, f32[8,16,16,128]{3,2,1,0:T(8,128)S(1)}, f32[128,128]{1,0:T(8,128)S(1)}) custom-call(f32[128,1024]{1,0:T(8,128)S(1)} %get-tuple-element.24.smooth_ref, bf16[128,512]{1,0:T(8,128)(2,1)S(1)} %get-tuple-element.25.refs_0_.traces_ref, ...), custom_call_target="tpu_custom_call" | custom-call | tf_op jit(solution)/shard_map/pallas_call | solution.py:351
  16.2 0.0 collective-permute-done.4.refs_2_
  16.3 0.0 collective-permute-done.5.refs_3_
  16.3 1.0 %collective-permute-done.3.refs_1_ = bf16[64,1024]{1,0:T(8,128)(2,1)S(1)} collective-permute-done((bf16[64,1024]{1,0:T(8,128)(2,1)S(1)}, bf16[64,1024]{1,0:T(8,128)(2,1)S(1)}, u32[]{:S(2)}, u32[]{:S(2)}) %collective-permute-start.3) | collective-permute-done | bytes 131104 | tf_op jit(solution)/shard_map/ppermute | solution.py:332
  17.3 0.0 copy-done
  17.3 4.1 %shard_map.71 = (bf16[128,1024]{1,0:T(8,128)(2,1)S(1)}, bf16[128,1024]{1,0:T(8,128)(2,1)S(1)}, f32[128,640]{1,0:T(8,128)S(1)}) custom-call(s32[8]{0:T(128)S(1)} %copy-done, f32[128,1024]{1,0:T(8,128)S(1)} %get-tuple-element.27.target_ref, f32[128,1024]{1,0:T(8,128)S(1)} %get-tuple-element.28.keep_ref, f32[128,1024]{1,0:T(8,128)S(1)} %get-tuple-element.29.start_ref, ...), custom_call_target="tpu_custom_call" | custom-call | tf_op jit(solution)/shard_map/pallas_call | solution.py:364
  21.4 0.1 collective-permute-start.7
  21.5 0.4 shard_map.72.ours_ref
  21.9 1.2 %collective-permute-done.7.theirs_ref = f32[128,640]{1,0:T(8,128)S(1)} collective-permute-done((f32[128,640]{1,0:T(8,128)S(1)}, f32[128,640]{1,0:T(8,128)S(1)}, u32[]{:S(2)}, u32[]{:S(2)}) %collective-permute-start.7) | collective-permute-done | bytes 327712 | tf_op jit(solution)/shard_map/ppermute | solution.py:274
  23.2 3.8 %collective-permute-start.10 = (f32[32,640]{1,0:T(8,128)S(1)}, f32[32,640]{1,0:T(8,128)S(1)}, u32[]{:S(2)}, u32[]{:S(2)}) collective-permute-start(f32[32,640]{1,0:T(8,128)S(1)} %get-tuple-element.41), channel_id=1, source_target_pairs={{0,2},{2,0},{4,6},{6,4},{8,10},{10,8},{12,14},{14,12},{16,18},{18,... | collective-permute-start | bytes 245768 | tf_op jit(solution)/shard_map/ppermute | solution.py:279
  27.0 0.5 collective-permute-start.8
  27.4 1.1 %collective-permute-start.9 = (f32[32,640]{1,0:T(8,128)S(1)}, f32[32,640]{1,0:T(8,128)S(1)}, u32[]{:S(2)}, u32[]{:S(2)}) collective-permute-start(f32[32,640]{1,0:T(8,128)S(1)} %get-tuple-element.39), channel_id=1, source_target_pairs={{0,6},{2,4},{4,2},{6,0},{8,14},{10,12},{12,10},{14,8},{16,22},{18,... | collective-permute-start | bytes 245768 | tf_op jit(solution)/shard_map/ppermute | solution.py:279
  28.5 1.2 %collective-permute-done.10 = f32[32,640]{1,0:T(8,128)S(1)} collective-permute-done((f32[32,640]{1,0:T(8,128)S(1)}, f32[32,640]{1,0:T(8,128)S(1)}, u32[]{:S(2)}, u32[]{:S(2)}) %collective-permute-start.10) | collective-permute-done | bytes 81952 | tf_op jit(solution)/shard_map/ppermute | solution.py:279
  29.7 3.4 %collective-permute-done.8 = f32[32,640]{1,0:T(8,128)S(1)} collective-permute-done((f32[32,640]{1,0:T(8,128)S(1)}, f32[32,640]{1,0:T(8,128)S(1)}, u32[]{:S(2)}, u32[]{:S(2)}) %collective-permute-start.8) | collective-permute-done | bytes 81952 | tf_op jit(solution)/shard_map/ppermute | solution.py:279
  33.1 0.0 collective-permute-done.9
  33.2 2.7 %collective-permute-start.11 = (f32[32,640]{1,0:T(8,128)S(1)}, f32[32,640]{1,0:T(8,128)S(1)}, u32[]{:S(2)}, u32[]{:S(2)}) collective-permute-start(f32[32,640]{1,0:T(8,128)S(1)} %add_add_fusion.1), channel_id=1, source_target_pairs={{0,16},{2,18},{4,20},{6,22},{8,24},{10,26},{12,28},{14,30},{16,0},... | collective-permute-start | bytes 245768 | tf_op jit(solution)/shard_map/ppermute | solution.py:279
  35.8 1.3 %collective-permute-start.12 = (f32[32,640]{1,0:T(8,128)S(1)}, f32[32,640]{1,0:T(8,128)S(1)}, u32[]{:S(2)}, u32[]{:S(2)}) collective-permute-start(f32[32,640]{1,0:T(8,128)S(1)} %add_add_fusion.1), channel_id=1, source_target_pairs={{0,24},{2,26},{4,28},{6,30},{8,16},{10,18},{12,20},{14,22},{16,8},... | collective-permute-start | bytes 245768 | tf_op jit(solution)/shard_map/ppermute | solution.py:279
  37.2 0.0 collective-permute-start.13
  37.2 0.0 collective-permute-start.6
  37.2 3.4 %collective-permute-done.11 = f32[32,640]{1,0:T(8,128)S(1)} collective-permute-done((f32[32,640]{1,0:T(8,128)S(1)}, f32[32,640]{1,0:T(8,128)S(1)}, u32[]{:S(2)}, u32[]{:S(2)}) %collective-permute-start.11) | collective-permute-done | bytes 81952 | tf_op jit(solution)/shard_map/ppermute | solution.py:279
  40.6 1.6 %collective-permute-done.12 = f32[32,640]{1,0:T(8,128)S(1)} collective-permute-done((f32[32,640]{1,0:T(8,128)S(1)}, f32[32,640]{1,0:T(8,128)S(1)}, u32[]{:S(2)}, u32[]{:S(2)}) %collective-permute-start.12) | collective-permute-done | bytes 81952 | tf_op jit(solution)/shard_map/ppermute | solution.py:279
  42.2 0.3 collective-permute-done.13
  42.5 1.2 %collective-permute-start.14 = (f32[32,640]{1,0:T(8,128)S(1)}, f32[32,640]{1,0:T(8,128)S(1)}, u32[]{:S(2)}, u32[]{:S(2)}) collective-permute-start(f32[32,640]{1,0:T(8,128)S(1)} %add_add_fusion.refs_0_), channel_id=1, source_target_pairs={{0,6},{2,4},{4,2},{6,0},{8,14},{10,12},{12,10},{14,8},{16,22},{18,... | collective-permute-start | bytes 245768 | tf_op jit(solution)/shard_map/ppermute | solution.py:279
  43.7 0.7 %collective-permute-start.15 = (f32[32,640]{1,0:T(8,128)S(1)}, f32[32,640]{1,0:T(8,128)S(1)}, u32[]{:S(2)}, u32[]{:S(2)}) collective-permute-start(f32[32,640]{1,0:T(8,128)S(1)} %add_add_fusion.refs_0_), channel_id=1, source_target_pairs={{0,4},{2,6},{4,0},{6,2},{8,12},{10,14},{12,8},{14,10},{16,20},{18,... | collective-permute-start | bytes 245768 | tf_op jit(solution)/shard_map/ppermute | solution.py:279
  44.4 1.7 %collective-permute-start.16 = (f32[32,640]{1,0:T(8,128)S(1)}, f32[32,640]{1,0:T(8,128)S(1)}, u32[]{:S(2)}, u32[]{:S(2)}) collective-permute-start(f32[32,640]{1,0:T(8,128)S(1)} %add_add_fusion.refs_0_), channel_id=1, source_target_pairs={{0,2},{2,0},{4,6},{6,4},{8,10},{10,8},{12,14},{14,12},{16,18},{18,... | collective-permute-start | bytes 245768 | tf_op jit(solution)/shard_map/ppermute | solution.py:279
  46.1 0.0 collective-permute-done.6
  46.1 0.9 %maximum_select_fusion = bf16[128,2048]{1,0:T(8,128)(2,1)} fusion(bf16[128,1024]{1,0:T(8,128)(2,1)S(1)} %collective-permute-done.6, bf16[128,1024]{1,0:T(8,128)(2,1)S(1)} %get-tuple-element.35, pred[]{:T(512)S(6)} %eq.3), kind=kLoop, calls=%fused_computation | loop fusion | flops 2359296 | bytes 1048577 | tf_op jit(solution)/shard_map/jit(_where)/select_n | solution.py:384
  47.0 1.0 %collective-permute-done.14.refs_1_ = f32[32,640]{1,0:T(8,128)S(1)} collective-permute-done((f32[32,640]{1,0:T(8,128)S(1)}, f32[32,640]{1,0:T(8,128)S(1)}, u32[]{:S(2)}, u32[]{:S(2)}) %collective-permute-start.14) | collective-permute-done | bytes 81952 | tf_op jit(solution)/shard_map/ppermute | solution.py:279
  48.0 0.8 %collective-permute-done.15.refs_2_ = f32[32,640]{1,0:T(8,128)S(1)} collective-permute-done((f32[32,640]{1,0:T(8,128)S(1)}, f32[32,640]{1,0:T(8,128)S(1)}, u32[]{:S(2)}, u32[]{:S(2)}) %collective-permute-start.15) | collective-permute-done | bytes 81952 | tf_op jit(solution)/shard_map/ppermute | solution.py:279
  48.8 0.1 collective-permute-done.16.refs_3_
  48.9 3.4 %shard_map.74 = f32[128,512]{1,0:T(8,128)} custom-call(s32[8]{0:T(128)S(1)} %copy-done, bf16[128,512]{1,0:T(8,128)(2,1)S(1)} %get-tuple-element.25.refs_0_.traces_ref, f32[32,640]{1,0:T(8,128)S(1)} %add_add_fusion.refs_0_, f32[32,640]{1,0:T(8,128)S(1)} %collective-permute-done.14.refs_1_, f32[32,640]{1,0:T(8,128)S(1)} %collective-permute-done.15.refs_2_, ...), custom_call_target="tpu_custom_call" | custom-call | tf_op jit(solution)/shard_map/pallas_call | solution.py:397
  (3 shorter events, 0.1 us)
Async XLA Ops:
  0.6 14.6 %collective-permute-start.1 = (bf16[2048,512]{1,0:T(8,128)(2,1)}, bf16[2048,512]{1,0:T(8,128)(2,1)S(1)}, u32[]{:S(2)}, u32[]{:S(2)}) collective-permute-start(bf16[2048,512]{1,0:T(8,128)(2,1)} %movie_ref.1), channel_id=1, source_target_pairs={{0,1},{1,0},{2,3},{3,2},{4,5},{5,4},{6,7},{7,6},{8,9},{9,8},{10,11... | collective-permute-start | bytes 6291464 | tf_op jit(solution)/shard_map/ppermute | solution.py:274
  3.2 6.9 %collective-permute-start.2 = (bf16[64,1024]{1,0:T(8,128)(2,1)S(1)}, bf16[64,1024]{1,0:T(8,128)(2,1)S(1)}, u32[]{:S(2)}, u32[]{:S(2)}) collective-permute-start(bf16[64,1024]{1,0:T(8,128)(2,1)S(1)} %get-tuple-element.33), channel_id=1, source_target_pairs={{0,2},{2,0},{4,6},{6,4},{8,10},{10,8},{12,14},{14,12},{16,18},{18,... | collective-permute-start | bytes 393224 | tf_op jit(solution)/shard_map/ppermute | solution.py:329
  5.7 9.5 %collective-permute-start = (bf16[128,512]{1,0:T(8,128)(2,1)S(1)}, bf16[128,512]{1,0:T(8,128)(2,1)S(1)}, u32[]{:S(2)}, u32[]{:S(2)}) collective-permute-start(bf16[128,512]{1,0:T(8,128)(2,1)S(1)} %get-tuple-element.25.refs_0_.traces_ref), channel_id=1, source_target_pairs={{0,1},{1,0},{2,3},{3,2},{4,5},{5,4},{6,7},{7,6},{8,9},{9,8},{10,11... | collective-permute-start | bytes 393224 | tf_op jit(solution)/shard_map/ppermute | solution.py:274
  6.0 10.3 %collective-permute-start.4 = (bf16[64,1024]{1,0:T(8,128)(2,1)S(1)}, bf16[64,1024]{1,0:T(8,128)(2,1)S(1)}, u32[]{:S(2)}, u32[]{:S(2)}) collective-permute-start(bf16[64,1024]{1,0:T(8,128)(2,1)S(1)} %get-tuple-element.34), channel_id=1, source_target_pairs={{0,2},{2,0},{4,6},{6,4},{8,10},{10,8},{12,14},{14,12},{16,18},{18,... | collective-permute-start | bytes 393224 | tf_op jit(solution)/shard_map/ppermute | solution.py:331
  6.3 9.9 %collective-permute-start.5 = (bf16[64,1024]{1,0:T(8,128)(2,1)S(1)}, bf16[64,1024]{1,0:T(8,128)(2,1)S(1)}, u32[]{:S(2)}, u32[]{:S(2)}) collective-permute-start(bf16[64,1024]{1,0:T(8,128)(2,1)S(1)} %get-tuple-element.34), channel_id=1, source_target_pairs={{2,4},{6,8},{10,12},{14,16},{18,20},{22,24},{26,28},{4,2},{8,6},{1... | collective-permute-start | bytes 393224 | tf_op jit(solution)/shard_map/ppermute | solution.py:330
  10.1 7.2 %collective-permute-start.3 = (bf16[64,1024]{1,0:T(8,128)(2,1)S(1)}, bf16[64,1024]{1,0:T(8,128)(2,1)S(1)}, u32[]{:S(2)}, u32[]{:S(2)}) collective-permute-start(bf16[64,1024]{1,0:T(8,128)(2,1)S(1)} %collective-permute-done.2.refs_0_), channel_id=1, source_target_pairs={{0,4},{4,8},{8,12},{12,16},{16,20},{20,24},{24,28},{6,2},{10,6},{1... | collective-permute-start | bytes 393224 | tf_op jit(solution)/shard_map/ppermute | solution.py:332
  15.2 2.1 %copy-start = (s32[8]{0:T(128)S(1)}, s32[8]{0:T(128)}, u32[]{:S(2)}) copy-start(s32[8]{0:T(128)} %order_ref.5) | copy-start | bytes 100
  21.4 1.7 %collective-permute-start.7 = (f32[128,640]{1,0:T(8,128)S(1)}, f32[128,640]{1,0:T(8,128)S(1)}, u32[]{:S(2)}, u32[]{:S(2)}) collective-permute-start(f32[128,640]{1,0:T(8,128)S(1)} %get-tuple-element.37), channel_id=1, source_target_pairs={{0,1},{1,0},{2,3},{3,2},{4,5},{5,4},{6,7},{7,6},{8,9},{9,8},{10,11... | collective-permute-start | bytes 983048 | tf_op jit(solution)/shard_map/ppermute | solution.py:274
  23.2 6.5 %collective-permute-start.10 = (f32[32,640]{1,0:T(8,128)S(1)}, f32[32,640]{1,0:T(8,128)S(1)}, u32[]{:S(2)}, u32[]{:S(2)}) collective-permute-start(f32[32,640]{1,0:T(8,128)S(1)} %get-tuple-element.41), channel_id=1, source_target_pairs={{0,2},{2,0},{4,6},{6,4},{8,10},{10,8},{12,14},{14,12},{16,18},{18,... | collective-permute-start | bytes 245768 | tf_op jit(solution)/shard_map/ppermute | solution.py:279
  27.0 6.2 %collective-permute-start.8 = (f32[32,640]{1,0:T(8,128)S(1)}, f32[32,640]{1,0:T(8,128)S(1)}, u32[]{:S(2)}, u32[]{:S(2)}) collective-permute-start(f32[32,640]{1,0:T(8,128)S(1)} %get-tuple-element.38), channel_id=1, source_target_pairs={{0,4},{2,6},{4,0},{6,2},{8,12},{10,14},{12,8},{14,10},{16,20},{18,... | collective-permute-start | bytes 245768 | tf_op jit(solution)/shard_map/ppermute | solution.py:279
  27.4 5.7 %collective-permute-start.9 = (f32[32,640]{1,0:T(8,128)S(1)}, f32[32,640]{1,0:T(8,128)S(1)}, u32[]{:S(2)}, u32[]{:S(2)}) collective-permute-start(f32[32,640]{1,0:T(8,128)S(1)} %get-tuple-element.39), channel_id=1, source_target_pairs={{0,6},{2,4},{4,2},{6,0},{8,14},{10,12},{12,10},{14,8},{16,22},{18,... | collective-permute-start | bytes 245768 | tf_op jit(solution)/shard_map/ppermute | solution.py:279
  33.2 7.4 %collective-permute-start.11 = (f32[32,640]{1,0:T(8,128)S(1)}, f32[32,640]{1,0:T(8,128)S(1)}, u32[]{:S(2)}, u32[]{:S(2)}) collective-permute-start(f32[32,640]{1,0:T(8,128)S(1)} %add_add_fusion.1), channel_id=1, source_target_pairs={{0,16},{2,18},{4,20},{6,22},{8,24},{10,26},{12,28},{14,30},{16,0},... | collective-permute-start | bytes 245768 | tf_op jit(solution)/shard_map/ppermute | solution.py:279
  35.8 6.4 %collective-permute-start.12 = (f32[32,640]{1,0:T(8,128)S(1)}, f32[32,640]{1,0:T(8,128)S(1)}, u32[]{:S(2)}, u32[]{:S(2)}) collective-permute-start(f32[32,640]{1,0:T(8,128)S(1)} %add_add_fusion.1), channel_id=1, source_target_pairs={{0,24},{2,26},{4,28},{6,30},{8,16},{10,18},{12,20},{14,22},{16,8},... | collective-permute-start | bytes 245768 | tf_op jit(solution)/shard_map/ppermute | solution.py:279
  37.2 5.3 %collective-permute-start.13 = (f32[32,640]{1,0:T(8,128)S(1)}, f32[32,640]{1,0:T(8,128)S(1)}, u32[]{:S(2)}, u32[]{:S(2)}) collective-permute-start(f32[32,640]{1,0:T(8,128)S(1)} %add_add_fusion.1), channel_id=1, source_target_pairs={{0,8},{2,10},{4,12},{6,14},{8,0},{10,2},{12,4},{14,6},{16,24},{18,... | collective-permute-start | bytes 245768 | tf_op jit(solution)/shard_map/ppermute | solution.py:279
  37.2 8.9 %collective-permute-start.6 = (bf16[128,1024]{1,0:T(8,128)(2,1)S(1)}, bf16[128,1024]{1,0:T(8,128)(2,1)S(1)}, u32[]{:S(2)}, u32[]{:S(2)}) collective-permute-start(bf16[128,1024]{1,0:T(8,128)(2,1)S(1)} %get-tuple-element.35), channel_id=1, source_target_pairs={{0,1},{1,0},{2,3},{3,2},{4,5},{5,4},{6,7},{7,6},{8,9},{9,8},{10,11... | collective-permute-start | bytes 786440 | tf_op jit(solution)/shard_map/ppermute | solution.py:274
  42.5 5.5 %collective-permute-start.14 = (f32[32,640]{1,0:T(8,128)S(1)}, f32[32,640]{1,0:T(8,128)S(1)}, u32[]{:S(2)}, u32[]{:S(2)}) collective-permute-start(f32[32,640]{1,0:T(8,128)S(1)} %add_add_fusion.refs_0_), channel_id=1, source_target_pairs={{0,6},{2,4},{4,2},{6,0},{8,14},{10,12},{12,10},{14,8},{16,22},{18,... | collective-permute-start | bytes 245768 | tf_op jit(solution)/shard_map/ppermute | solution.py:279
  43.7 5.1 %collective-permute-start.15 = (f32[32,640]{1,0:T(8,128)S(1)}, f32[32,640]{1,0:T(8,128)S(1)}, u32[]{:S(2)}, u32[]{:S(2)}) collective-permute-start(f32[32,640]{1,0:T(8,128)S(1)} %add_add_fusion.refs_0_), channel_id=1, source_target_pairs={{0,4},{2,6},{4,0},{6,2},{8,12},{10,14},{12,8},{14,10},{16,20},{18,... | collective-permute-start | bytes 245768 | tf_op jit(solution)/shard_map/ppermute | solution.py:279
  44.4 4.4 %collective-permute-start.16 = (f32[32,640]{1,0:T(8,128)S(1)}, f32[32,640]{1,0:T(8,128)S(1)}, u32[]{:S(2)}, u32[]{:S(2)}) collective-permute-start(f32[32,640]{1,0:T(8,128)S(1)} %add_add_fusion.refs_0_), channel_id=1, source_target_pairs={{0,2},{2,0},{4,6},{6,4},{8,10},{10,8},{12,14},{14,12},{16,18},{18,... | collective-permute-start | bytes 245768 | tf_op jit(solution)/shard_map/ppermute | solution.py:279

commit v6 on v5

--- a/solution.py
+++ b/solution.py
@@ -295,7 +295,8 @@
         out_specs=[VMEM] * GROUP,
     )(ours, theirs)
     mine = tree_sum(chunks[0], from_group([(k, chunks[k]) for k in range(1, GROUP)], 1))
-    mine = tree_sum(mine, from_group([(k, mine) for k in range(1, GROUP)], top))
+    first, second, third = from_group([(k, mine) for k in range(1, GROUP)], top)
+    mine = (mine + first) + (second + third)
     return [mine] + from_group([(k, mine) for k in range(1, GROUP)], 1)[::-1]
 
 

time: 52.5 us -> 53.5 us (1.019)
  waiting for transfers between devices: 17.2 us -> 17.8 us
    ppermute x9, waiting for transfers between devices: 11.8 us -> 12.4 us  [from_group(): lax.ppermute(array, 'vox', [(i, i ^ k * stride) for i in range(count)])]
where the time goes in v6:
time: 53.5 us; the launch traced here: 53.3 us
  starting transfers between devices  21.6 us (40%)
  waiting for transfers between devices  17.8 us (33%)
  Pallas kernels  12.2 us (23%)
  other arithmetic  0.97 us (2%)
  between operations  0.75 us (1%)
    ppermute x9, starting transfers between devices, from_group(): lax.ppermute(array, 'vox', [(i, i ^ k * stride) for i in range(count)])  13.3 us
    ppermute x9, waiting for transfers between devices, from_group(): lax.ppermute(array, 'vox', [(i, i ^ k * stride) for i in range(count)])  12.4 us
    pallas_call x1, Pallas kernels, local(): pl.pallas_call(functools.partial(footprint_kernel, len(sides)), out_shape...  4.12 us
    ppermute x1, starting transfers between devices, local(): lax.ppermute(beside_relayed, 'vox', onward)  3.87 us
    pallas_call x1, Pallas kernels, local(): pl.pallas_call(trace_kernel, out_shape=shape_of((comps, frames), F32), in...  3.4 us
    ppermute x1, waiting for transfers between devices, local(): beside_relayed = lax.ppermute(relayed, 'vox', pairs)  3.12 us
    ppermute x1, starting transfers between devices, local(): beside_relayed = lax.ppermute(relayed, 'vox', pairs)  2.57 us
    pallas_call x1, Pallas kernels, local(): pl.pallas_call(load_kernel, out_shape=[shape_of((RELAYED, share), BF16),...  2.02 us
  transfers between devices with their start and end apart: 17, of which 11 were waited for; matrix products, arithmetic and copies ran while one was open for 2% of the time, Pallas kernels for 9%

profile of v6, /device:TPU:0, one launch (start us, length us, event | category | flops | bytes accessed | tf_op | source)
XLA Modules:
  0.0 53.3 jit_solution(2963188466200831468)
XLA Ops:
  0.6 0.5 collective-permute-start.1
  1.1 2.0 %shard_map.68 = (bf16[64,1024]{1,0:T(8,128)(2,1)S(1)}, bf16[64,1024]{1,0:T(8,128)(2,1)S(1)}, bf16[128,2048]{1,0:T(8,128)(2,1)S(1)}, s32[16,128]{1,0:T(8,128)S(1)...) custom-call(s32[8]{0:T(128)} %order_ref.5, bf16[128,2048]{1,0:T(8,128)(2,1)} %fp_ref.1, s32[16,128]{1,0:T(8,128)} %bitcast.1, ...), custom_call_target="tpu_custom_call" | custom-call | tf_op jit(solution)/shard_map/pallas_call | solution.py:315
  3.2 2.6 %collective-permute-start.2 = (bf16[64,1024]{1,0:T(8,128)(2,1)S(1)}, bf16[64,1024]{1,0:T(8,128)(2,1)S(1)}, u32[]{:S(2)}, u32[]{:S(2)}) collective-permute-start(bf16[64,1024]{1,0:T(8,128)(2,1)S(1)} %get-tuple-element.33), channel_id=1, source_target_pairs={{0,2},{2,0},{4,6},{6,4},{8,10},{10,8},{12,14},{14,12},{16,18},{18,... | collective-permute-start | bytes 393224 | tf_op jit(solution)/shard_map/ppermute | solution.py:330
  5.7 0.2 collective-permute-start
  6.0 0.4 collective-permute-start.4
  6.3 0.7 %collective-permute-start.5 = (bf16[64,1024]{1,0:T(8,128)(2,1)S(1)}, bf16[64,1024]{1,0:T(8,128)(2,1)S(1)}, u32[]{:S(2)}, u32[]{:S(2)}) collective-permute-start(bf16[64,1024]{1,0:T(8,128)(2,1)S(1)} %get-tuple-element.34), channel_id=1, source_target_pairs={{2,4},{6,8},{10,12},{14,16},{18,20},{22,24},{26,28},{4,2},{8,6},{1... | collective-permute-start | bytes 393224 | tf_op jit(solution)/shard_map/ppermute | solution.py:331
  7.0 3.1 %collective-permute-done.2.refs_0_ = bf16[64,1024]{1,0:T(8,128)(2,1)S(1)} collective-permute-done((bf16[64,1024]{1,0:T(8,128)(2,1)S(1)}, bf16[64,1024]{1,0:T(8,128)(2,1)S(1)}, u32[]{:S(2)}, u32[]{:S(2)}) %collective-permute-start.2) | collective-permute-done | bytes 131104 | tf_op jit(solution)/shard_map/ppermute | solution.py:330
  10.1 3.9 %collective-permute-start.3 = (bf16[64,1024]{1,0:T(8,128)(2,1)S(1)}, bf16[64,1024]{1,0:T(8,128)(2,1)S(1)}, u32[]{:S(2)}, u32[]{:S(2)}) collective-permute-start(bf16[64,1024]{1,0:T(8,128)(2,1)S(1)} %collective-permute-done.2.refs_0_), channel_id=1, source_target_pairs={{0,4},{4,8},{8,12},{12,16},{16,20},{20,24},{24,28},{6,2},{10,6},{1... | collective-permute-start | bytes 393224 | tf_op jit(solution)/shard_map/ppermute | solution.py:333
  14.0 1.2 %shard_map.69 = (f32[128,1024]{1,0:T(8,128)S(1)}, f32[128,1024]{1,0:T(8,128)S(1)}, f32[128,1024]{1,0:T(8,128)S(1)}) custom-call(s32[8]{0:T(128)} %order_ref.5, bf16[128,2048]{1,0:T(8,128)(2,1)S(1)} %get-tuple-element.22.sorted_fp, s32[16,128]{1,0:T(8,128)S(1)} %get-tuple-element.23.support_buf), custom_call_target="tpu_custom_call" | custom-call | tf_op jit(solution)/shard_map/pallas_call | solution.py:335
  15.2 0.0 copy-start
  15.2 0.0 collective-permute-done.refs_1_
  15.2 0.0 collective-permute-done.1.refs_3_.refs_4_
  15.2 1.0 %shard_map.70 = (f32[128,1024]{1,0:T(8,128)S(1)}, bf16[256,256]{1,0:T(8,128)(2,1)S(1)}, f32[8,16,16,128]{3,2,1,0:T(8,128)S(1)}, f32[128,128]{1,0:T(8,128)S(1)}) custom-call(f32[128,1024]{1,0:T(8,128)S(1)} %get-tuple-element.24.smooth_ref, bf16[128,512]{1,0:T(8,128)(2,1)S(1)} %get-tuple-element.25.refs_0_.traces_ref, ...), custom_call_target="tpu_custom_call" | custom-call | tf_op jit(solution)/shard_map/pallas_call | solution.py:352
  16.2 0.0 collective-permute-done.4.refs_2_
  16.3 0.0 collective-permute-done.5.refs_3_
  16.3 1.0 %collective-permute-done.3.refs_1_ = bf16[64,1024]{1,0:T(8,128)(2,1)S(1)} collective-permute-done((bf16[64,1024]{1,0:T(8,128)(2,1)S(1)}, bf16[64,1024]{1,0:T(8,128)(2,1)S(1)}, u32[]{:S(2)}, u32[]{:S(2)}) %collective-permute-start.3) | collective-permute-done | bytes 131104 | tf_op jit(solution)/shard_map/ppermute | solution.py:333
  17.3 0.0 copy-done
  17.3 4.1 %shard_map.71 = (bf16[128,1024]{1,0:T(8,128)(2,1)S(1)}, bf16[128,1024]{1,0:T(8,128)(2,1)S(1)}, f32[128,640]{1,0:T(8,128)S(1)}) custom-call(s32[8]{0:T(128)S(1)} %copy-done, f32[128,1024]{1,0:T(8,128)S(1)} %get-tuple-element.27.target_ref, f32[128,1024]{1,0:T(8,128)S(1)} %get-tuple-element.28.keep_ref, f32[128,1024]{1,0:T(8,128)S(1)} %get-tuple-element.29.start_ref, ...), custom_call_target="tpu_custom_call" | custom-call | tf_op jit(solution)/shard_map/pallas_call | solution.py:365
  21.4 0.1 collective-permute-start.7
  21.5 0.4 shard_map.72.ours_ref
  21.9 1.2 %collective-permute-done.7.theirs_ref = f32[128,640]{1,0:T(8,128)S(1)} collective-permute-done((f32[128,640]{1,0:T(8,128)S(1)}, f32[128,640]{1,0:T(8,128)S(1)}, u32[]{:S(2)}, u32[]{:S(2)}) %collective-permute-start.7) | collective-permute-done | bytes 327712 | tf_op jit(solution)/shard_map/ppermute | solution.py:274
  23.2 3.8 %collective-permute-start.10 = (f32[32,640]{1,0:T(8,128)S(1)}, f32[32,640]{1,0:T(8,128)S(1)}, u32[]{:S(2)}, u32[]{:S(2)}) collective-permute-start(f32[32,640]{1,0:T(8,128)S(1)} %get-tuple-element.41), channel_id=1, source_target_pairs={{0,2},{2,0},{4,6},{6,4},{8,10},{10,8},{12,14},{14,12},{16,18},{18,... | collective-permute-start | bytes 245768 | tf_op jit(solution)/shard_map/ppermute | solution.py:279
  27.0 0.5 collective-permute-start.8
  27.4 1.1 %collective-permute-start.9 = (f32[32,640]{1,0:T(8,128)S(1)}, f32[32,640]{1,0:T(8,128)S(1)}, u32[]{:S(2)}, u32[]{:S(2)}) collective-permute-start(f32[32,640]{1,0:T(8,128)S(1)} %get-tuple-element.39), channel_id=1, source_target_pairs={{0,6},{2,4},{4,2},{6,0},{8,14},{10,12},{12,10},{14,8},{16,22},{18,... | collective-permute-start | bytes 245768 | tf_op jit(solution)/shard_map/ppermute | solution.py:279
  28.5 1.2 %collective-permute-done.10 = f32[32,640]{1,0:T(8,128)S(1)} collective-permute-done((f32[32,640]{1,0:T(8,128)S(1)}, f32[32,640]{1,0:T(8,128)S(1)}, u32[]{:S(2)}, u32[]{:S(2)}) %collective-permute-start.10) | collective-permute-done | bytes 81952 | tf_op jit(solution)/shard_map/ppermute | solution.py:279
  29.7 3.4 %collective-permute-done.8 = f32[32,640]{1,0:T(8,128)S(1)} collective-permute-done((f32[32,640]{1,0:T(8,128)S(1)}, f32[32,640]{1,0:T(8,128)S(1)}, u32[]{:S(2)}, u32[]{:S(2)}) %collective-permute-start.8) | collective-permute-done | bytes 81952 | tf_op jit(solution)/shard_map/ppermute | solution.py:279
  33.1 0.0 collective-permute-done.9
  33.2 1.6 %collective-permute-start.11 = (f32[32,640]{1,0:T(8,128)S(1)}, f32[32,640]{1,0:T(8,128)S(1)}, u32[]{:S(2)}, u32[]{:S(2)}) collective-permute-start(f32[32,640]{1,0:T(8,128)S(1)} %add_add_fusion.1), channel_id=1, source_target_pairs={{0,8},{2,10},{4,12},{6,14},{8,0},{10,2},{12,4},{14,6},{16,24},{18,... | collective-permute-start | bytes 245768 | tf_op jit(solution)/shard_map/ppermute | solution.py:279
  34.8 2.4 %collective-permute-start.12 = (f32[32,640]{1,0:T(8,128)S(1)}, f32[32,640]{1,0:T(8,128)S(1)}, u32[]{:S(2)}, u32[]{:S(2)}) collective-permute-start(f32[32,640]{1,0:T(8,128)S(1)} %add_add_fusion.1), channel_id=1, source_target_pairs={{0,16},{2,18},{4,20},{6,22},{8,24},{10,26},{12,28},{14,30},{16,0},... | collective-permute-start | bytes 245768 | tf_op jit(solution)/shard_map/ppermute | solution.py:279
  37.2 0.4 collective-permute-start.13
  37.6 0.0 collective-permute-start.6
  37.6 0.2 collective-permute-done.11
  37.9 4.0 %collective-permute-done.12 = f32[32,640]{1,0:T(8,128)S(1)} collective-permute-done((f32[32,640]{1,0:T(8,128)S(1)}, f32[32,640]{1,0:T(8,128)S(1)}, u32[]{:S(2)}, u32[]{:S(2)}) %collective-permute-start.12) | collective-permute-done | bytes 81952 | tf_op jit(solution)/shard_map/ppermute | solution.py:279
  41.9 1.7 %collective-permute-done.13 = f32[32,640]{1,0:T(8,128)S(1)} collective-permute-done((f32[32,640]{1,0:T(8,128)S(1)}, f32[32,640]{1,0:T(8,128)S(1)}, u32[]{:S(2)}, u32[]{:S(2)}) %collective-permute-start.13) | collective-permute-done | bytes 81952 | tf_op jit(solution)/shard_map/ppermute | solution.py:279
  43.6 1.2 %collective-permute-start.14 = (f32[32,640]{1,0:T(8,128)S(1)}, f32[32,640]{1,0:T(8,128)S(1)}, u32[]{:S(2)}, u32[]{:S(2)}) collective-permute-start(f32[32,640]{1,0:T(8,128)S(1)} %add_add_fusion.refs_0_), channel_id=1, source_target_pairs={{0,6},{2,4},{4,2},{6,0},{8,14},{10,12},{12,10},{14,8},{16,22},{18,... | collective-permute-start | bytes 245768 | tf_op jit(solution)/shard_map/ppermute | solution.py:279
  44.8 0.7 %collective-permute-start.15 = (f32[32,640]{1,0:T(8,128)S(1)}, f32[32,640]{1,0:T(8,128)S(1)}, u32[]{:S(2)}, u32[]{:S(2)}) collective-permute-start(f32[32,640]{1,0:T(8,128)S(1)} %add_add_fusion.refs_0_), channel_id=1, source_target_pairs={{0,4},{2,6},{4,0},{6,2},{8,12},{10,14},{12,8},{14,10},{16,20},{18,... | collective-permute-start | bytes 245768 | tf_op jit(solution)/shard_map/ppermute | solution.py:279
  45.5 1.6 %collective-permute-start.16 = (f32[32,640]{1,0:T(8,128)S(1)}, f32[32,640]{1,0:T(8,128)S(1)}, u32[]{:S(2)}, u32[]{:S(2)}) collective-permute-start(f32[32,640]{1,0:T(8,128)S(1)} %add_add_fusion.refs_0_), channel_id=1, source_target_pairs={{0,2},{2,0},{4,6},{6,4},{8,10},{10,8},{12,14},{14,12},{16,18},{18,... | collective-permute-start | bytes 245768 | tf_op jit(solution)/shard_map/ppermute | solution.py:279
  47.1 0.0 collective-permute-done.6
  47.1 0.9 %maximum_select_fusion = bf16[128,2048]{1,0:T(8,128)(2,1)} fusion(bf16[128,1024]{1,0:T(8,128)(2,1)S(1)} %collective-permute-done.6, bf16[128,1024]{1,0:T(8,128)(2,1)S(1)} %get-tuple-element.35, pred[]{:T(512)S(6)} %eq.3), kind=kLoop, calls=%fused_computation | loop fusion | flops 2359296 | bytes 1048577 | tf_op jit(solution)/shard_map/jit(_where)/select_n | solution.py:385
  48.1 1.0 %collective-permute-done.14.refs_1_ = f32[32,640]{1,0:T(8,128)S(1)} collective-permute-done((f32[32,640]{1,0:T(8,128)S(1)}, f32[32,640]{1,0:T(8,128)S(1)}, u32[]{:S(2)}, u32[]{:S(2)}) %collective-permute-start.14) | collective-permute-done | bytes 81952 | tf_op jit(solution)/shard_map/ppermute | solution.py:279
  49.0 0.8 %collective-permute-done.15.refs_2_ = f32[32,640]{1,0:T(8,128)S(1)} collective-permute-done((f32[32,640]{1,0:T(8,128)S(1)}, f32[32,640]{1,0:T(8,128)S(1)}, u32[]{:S(2)}, u32[]{:S(2)}) %collective-permute-start.15) | collective-permute-done | bytes 81952 | tf_op jit(solution)/shard_map/ppermute | solution.py:279
  49.9 0.1 collective-permute-done.16.refs_3_
  49.9 3.4 %shard_map.74 = f32[128,512]{1,0:T(8,128)} custom-call(s32[8]{0:T(128)S(1)} %copy-done, bf16[128,512]{1,0:T(8,128)(2,1)S(1)} %get-tuple-element.25.refs_0_.traces_ref, f32[32,640]{1,0:T(8,128)S(1)} %add_add_fusion.refs_0_, f32[32,640]{1,0:T(8,128)S(1)} %collective-permute-done.14.refs_1_, f32[32,640]{1,0:T(8,128)S(1)} %collective-permute-done.15.refs_2_, ...), custom_call_target="tpu_custom_call" | custom-call | tf_op jit(solution)/shard_map/pallas_call | solution.py:398
  (3 shorter events, 0.1 us)
Async XLA Ops:
  0.6 14.6 %collective-permute-start.1 = (bf16[2048,512]{1,0:T(8,128)(2,1)}, bf16[2048,512]{1,0:T(8,128)(2,1)S(1)}, u32[]{:S(2)}, u32[]{:S(2)}) collective-permute-start(bf16[2048,512]{1,0:T(8,128)(2,1)} %movie_ref.1), channel_id=1, source_target_pairs={{0,1},{1,0},{2,3},{3,2},{4,5},{5,4},{6,7},{7,6},{8,9},{9,8},{10,11... | collective-permute-start | bytes 6291464 | tf_op jit(solution)/shard_map/ppermute | solution.py:274
  3.2 6.9 %collective-permute-start.2 = (bf16[64,1024]{1,0:T(8,128)(2,1)S(1)}, bf16[64,1024]{1,0:T(8,128)(2,1)S(1)}, u32[]{:S(2)}, u32[]{:S(2)}) collective-permute-start(bf16[64,1024]{1,0:T(8,128)(2,1)S(1)} %get-tuple-element.33), channel_id=1, source_target_pairs={{0,2},{2,0},{4,6},{6,4},{8,10},{10,8},{12,14},{14,12},{16,18},{18,... | collective-permute-start | bytes 393224 | tf_op jit(solution)/shard_map/ppermute | solution.py:330
  5.7 9.5 %collective-permute-start = (bf16[128,512]{1,0:T(8,128)(2,1)S(1)}, bf16[128,512]{1,0:T(8,128)(2,1)S(1)}, u32[]{:S(2)}, u32[]{:S(2)}) collective-permute-start(bf16[128,512]{1,0:T(8,128)(2,1)S(1)} %get-tuple-element.25.refs_0_.traces_ref), channel_id=1, source_target_pairs={{0,1},{1,0},{2,3},{3,2},{4,5},{5,4},{6,7},{7,6},{8,9},{9,8},{10,11... | collective-permute-start | bytes 393224 | tf_op jit(solution)/shard_map/ppermute | solution.py:274
  6.0 10.3 %collective-permute-start.4 = (bf16[64,1024]{1,0:T(8,128)(2,1)S(1)}, bf16[64,1024]{1,0:T(8,128)(2,1)S(1)}, u32[]{:S(2)}, u32[]{:S(2)}) collective-permute-start(bf16[64,1024]{1,0:T(8,128)(2,1)S(1)} %get-tuple-element.34), channel_id=1, source_target_pairs={{0,2},{2,0},{4,6},{6,4},{8,10},{10,8},{12,14},{14,12},{16,18},{18,... | collective-permute-start | bytes 393224 | tf_op jit(solution)/shard_map/ppermute | solution.py:332
  6.3 9.9 %collective-permute-start.5 = (bf16[64,1024]{1,0:T(8,128)(2,1)S(1)}, bf16[64,1024]{1,0:T(8,128)(2,1)S(1)}, u32[]{:S(2)}, u32[]{:S(2)}) collective-permute-start(bf16[64,1024]{1,0:T(8,128)(2,1)S(1)} %get-tuple-element.34), channel_id=1, source_target_pairs={{2,4},{6,8},{10,12},{14,16},{18,20},{22,24},{26,28},{4,2},{8,6},{1... | collective-permute-start | bytes 393224 | tf_op jit(solution)/shard_map/ppermute | solution.py:331
  10.1 7.2 %collective-permute-start.3 = (bf16[64,1024]{1,0:T(8,128)(2,1)S(1)}, bf16[64,1024]{1,0:T(8,128)(2,1)S(1)}, u32[]{:S(2)}, u32[]{:S(2)}) collective-permute-start(bf16[64,1024]{1,0:T(8,128)(2,1)S(1)} %collective-permute-done.2.refs_0_), channel_id=1, source_target_pairs={{0,4},{4,8},{8,12},{12,16},{16,20},{20,24},{24,28},{6,2},{10,6},{1... | collective-permute-start | bytes 393224 | tf_op jit(solution)/shard_map/ppermute | solution.py:333
  15.2 2.1 %copy-start = (s32[8]{0:T(128)S(1)}, s32[8]{0:T(128)}, u32[]{:S(2)}) copy-start(s32[8]{0:T(128)} %order_ref.5) | copy-start | bytes 100
  21.4 1.7 %collective-permute-start.7 = (f32[128,640]{1,0:T(8,128)S(1)}, f32[128,640]{1,0:T(8,128)S(1)}, u32[]{:S(2)}, u32[]{:S(2)}) collective-permute-start(f32[128,640]{1,0:T(8,128)S(1)} %get-tuple-element.37), channel_id=1, source_target_pairs={{0,1},{1,0},{2,3},{3,2},{4,5},{5,4},{6,7},{7,6},{8,9},{9,8},{10,11... | collective-permute-start | bytes 983048 | tf_op jit(solution)/shard_map/ppermute | solution.py:274
  23.2 6.5 %collective-permute-start.10 = (f32[32,640]{1,0:T(8,128)S(1)}, f32[32,640]{1,0:T(8,128)S(1)}, u32[]{:S(2)}, u32[]{:S(2)}) collective-permute-start(f32[32,640]{1,0:T(8,128)S(1)} %get-tuple-element.41), channel_id=1, source_target_pairs={{0,2},{2,0},{4,6},{6,4},{8,10},{10,8},{12,14},{14,12},{16,18},{18,... | collective-permute-start | bytes 245768 | tf_op jit(solution)/shard_map/ppermute | solution.py:279
  27.0 6.2 %collective-permute-start.8 = (f32[32,640]{1,0:T(8,128)S(1)}, f32[32,640]{1,0:T(8,128)S(1)}, u32[]{:S(2)}, u32[]{:S(2)}) collective-permute-start(f32[32,640]{1,0:T(8,128)S(1)} %get-tuple-element.38), channel_id=1, source_target_pairs={{0,4},{2,6},{4,0},{6,2},{8,12},{10,14},{12,8},{14,10},{16,20},{18,... | collective-permute-start | bytes 245768 | tf_op jit(solution)/shard_map/ppermute | solution.py:279
  27.4 5.7 %collective-permute-start.9 = (f32[32,640]{1,0:T(8,128)S(1)}, f32[32,640]{1,0:T(8,128)S(1)}, u32[]{:S(2)}, u32[]{:S(2)}) collective-permute-start(f32[32,640]{1,0:T(8,128)S(1)} %get-tuple-element.39), channel_id=1, source_target_pairs={{0,6},{2,4},{4,2},{6,0},{8,14},{10,12},{12,10},{14,8},{16,22},{18,... | collective-permute-start | bytes 245768 | tf_op jit(solution)/shard_map/ppermute | solution.py:279
  33.2 4.7 %collective-permute-start.11 = (f32[32,640]{1,0:T(8,128)S(1)}, f32[32,640]{1,0:T(8,128)S(1)}, u32[]{:S(2)}, u32[]{:S(2)}) collective-permute-start(f32[32,640]{1,0:T(8,128)S(1)} %add_add_fusion.1), channel_id=1, source_target_pairs={{0,8},{2,10},{4,12},{6,14},{8,0},{10,2},{12,4},{14,6},{16,24},{18,... | collective-permute-start | bytes 245768 | tf_op jit(solution)/shard_map/ppermute | solution.py:279
  34.8 7.0 %collective-permute-start.12 = (f32[32,640]{1,0:T(8,128)S(1)}, f32[32,640]{1,0:T(8,128)S(1)}, u32[]{:S(2)}, u32[]{:S(2)}) collective-permute-start(f32[32,640]{1,0:T(8,128)S(1)} %add_add_fusion.1), channel_id=1, source_target_pairs={{0,16},{2,18},{4,20},{6,22},{8,24},{10,26},{12,28},{14,30},{16,0},... | collective-permute-start | bytes 245768 | tf_op jit(solution)/shard_map/ppermute | solution.py:279
  37.2 6.3 %collective-permute-start.13 = (f32[32,640]{1,0:T(8,128)S(1)}, f32[32,640]{1,0:T(8,128)S(1)}, u32[]{:S(2)}, u32[]{:S(2)}) collective-permute-start(f32[32,640]{1,0:T(8,128)S(1)} %add_add_fusion.1), channel_id=1, source_target_pairs={{0,24},{2,26},{4,28},{6,30},{8,16},{10,18},{12,20},{14,22},{16,8},... | collective-permute-start | bytes 245768 | tf_op jit(solution)/shard_map/ppermute | solution.py:279
  37.6 9.5 %collective-permute-start.6 = (bf16[128,1024]{1,0:T(8,128)(2,1)S(1)}, bf16[128,1024]{1,0:T(8,128)(2,1)S(1)}, u32[]{:S(2)}, u32[]{:S(2)}) collective-permute-start(bf16[128,1024]{1,0:T(8,128)(2,1)S(1)} %get-tuple-element.35), channel_id=1, source_target_pairs={{0,1},{1,0},{2,3},{3,2},{4,5},{5,4},{6,7},{7,6},{8,9},{9,8},{10,11... | collective-permute-start | bytes 786440 | tf_op jit(solution)/shard_map/ppermute | solution.py:274
  43.6 5.5 %collective-permute-start.14 = (f32[32,640]{1,0:T(8,128)S(1)}, f32[32,640]{1,0:T(8,128)S(1)}, u32[]{:S(2)}, u32[]{:S(2)}) collective-permute-start(f32[32,640]{1,0:T(8,128)S(1)} %add_add_fusion.refs_0_), channel_id=1, source_target_pairs={{0,6},{2,4},{4,2},{6,0},{8,14},{10,12},{12,10},{14,8},{16,22},{18,... | collective-permute-start | bytes 245768 | tf_op jit(solution)/shard_map/ppermute | solution.py:279
  44.8 5.1 %collective-permute-start.15 = (f32[32,640]{1,0:T(8,128)S(1)}, f32[32,640]{1,0:T(8,128)S(1)}, u32[]{:S(2)}, u32[]{:S(2)}) collective-permute-start(f32[32,640]{1,0:T(8,128)S(1)} %add_add_fusion.refs_0_), channel_id=1, source_target_pairs={{0,4},{2,6},{4,0},{6,2},{8,12},{10,14},{12,8},{14,10},{16,20},{18,... | collective-permute-start | bytes 245768 | tf_op jit(solution)/shard_map/ppermute | solution.py:279
  45.5 4.4 %collective-permute-start.16 = (f32[32,640]{1,0:T(8,128)S(1)}, f32[32,640]{1,0:T(8,128)S(1)}, u32[]{:S(2)}, u32[]{:S(2)}) collective-permute-start(f32[32,640]{1,0:T(8,128)S(1)} %add_add_fusion.refs_0_), channel_id=1, source_target_pairs={{0,2},{2,0},{4,6},{6,4},{8,10},{10,8},{12,14},{14,12},{16,18},{18,... | collective-permute-start | bytes 245768 | tf_op jit(solution)/shard_map/ppermute | solution.py:279
